TPU v7x, 128 devices: a whole 4x4x4 slice. The times are simulated.
128 devices in a mesh: group: 8 (over z, core), sub: 16 (over y, x).
Axes of the slice: x: 4, y: 4, z: 4, core: 2. Of those that a mesh axis runs over, the one named last changes fastest.
Arguments:
- adjoint: float32 [4, 256, 262144], P(None, None, ('group', 'sub')), may hold values from -6 to 6
- velocity: bfloat16 [3, 256, 262144], P(None, None, ('group', 'sub')), may hold values from -6 to 6
- face_speed: bfloat16 [216, 262144], P(None, ('group', 'sub')), may hold values from -6 to 6
- derivatives: bfloat16 [768, 256], replicated, may hold values from -0.375 to 0.375
- lift_operator: bfloat16 [256, 216], replicated, may hold values from -1 to 1
- emission_profile: bfloat16 [256, 32], replicated, may hold values from -0.046875 to 0.046875
- neighbours: int32 [6, 262144], P(None, ('group', 'sub')), may hold values from 0 to 3327, as said below
- sub_sends: int32 [4, 131072], P(None, ('group', 'sub')), may hold values from 0 to 2047, as said below
- group_sends: int32 [2, 32768], P(None, ('group', 'sub')), may hold values from 0 to 2047, as said below
- element_tile: int32 [262144], P(('group', 'sub')), may hold values from 0 to 4095
- tile_slot: int32 [4096], replicated, may hold values from 0 to 4095, as said below
Outputs:
- adjoint_next: float32 [4, 256, 262144], P(None, None, ('group', 'sub'))
- emission_grad: float32 [4096, 128], P(('group', 'sub'))
Inputs may be any that keep to these rules, and one draw needn't show every extreme that they name: `neighbours`: faces pair up symmetrically: face 2a + 1 of an element meets face 2a of exactly one element. Positions below 2048 name an element of the same partition; positions 2048 + r * 64 + j name slot j from partition r of the group, and are used only for faces 0 to 3; positions from 3072 on name the adjacent group's slots and are used only for faces 4 and 5. `sub_sends`: column (p * 16 + r) * 64 + j is partition p's slot j for partition r of its group. Between two distinct partitions of a group the same number of face pairs, 16 to 64, crosses in each of faces 0 and 1 and of faces 2 and 3, filling slots 0 onwards; in every group some pair has 64. Unused slots, and a partition's slots for itself, name element 0 and are read by nobody. `group_sends`: column p * 256 + j is partition p's slot j. Partitions of the same index q in adjacent groups share 256 // 2 to 256 face pairs, the same number for every group, filling slots 0 onwards; some q has 256. Unused slots name element 0 and are read by nobody. `tile_slot`: A permutation of the tiles onto the rows.
All inputs are finite; a program needn't handle non-finite values.
Results may differ from a plain program's by a relative error of at most 0.0032.
Values may be sent and summed in bfloat16 or wider, within the bound.
No kernel may reach another device: no remote copies, remote signals or barrier semaphores. Data moves between devices by JAX's collectives and lax.ppermute only.
A program may use at most 192 MiB of HBM per device.

v0:
```python
import jax
import jax.numpy as jnp
import numpy as np
from jax import lax
from jax.sharding import PartitionSpec as P

ORDER = 5


SECTION = 0.125


def passed_along(value, axis, steps):
    count = lax.axis_size(axis)
    pairs = [(source, (source + steps) % count) for source in range(count)]
    return lax.ppermute(value, axis, pairs)


def face_table(order):
    edge_nodes = order + 1
    coords_a, coords_b = np.meshgrid(np.arange(edge_nodes), np.arange(edge_nodes), indexing="ij")
    coords_a = coords_a.reshape(-1)
    coords_b = coords_b.reshape(-1)
    face_rows = []
    for axis_id in range(3):
        for level_id in (0, edge_nodes - 1):
            fixed_col = coords_a * 0 + level_id
            if axis_id == 0:
                triple = (fixed_col, coords_a, coords_b)
            elif axis_id == 1:
                triple = (coords_a, fixed_col, coords_b)
            else:
                triple = (coords_a, coords_b, fixed_col)
            face_rows.append((triple[0] * edge_nodes + triple[1]) * edge_nodes + triple[2])
    return np.stack(face_rows).astype(np.int32)


def pool_take(local_traces, received_part, positions):
    pool_rows = jnp.concatenate([local_traces, received_part], axis=2)
    return jnp.take(pool_rows, positions, axis=2)


def on_device(
    adjoint,
    velocity,
    face_speed,
    derivatives,
    lift_operator,
    emission_profile,
    neighbours,
    sub_sends,
    group_sends,
    element_tile,
    tile_slot,
):
    species, node_count, elements = adjoint.shape
    face_rows = jnp.asarray(face_table(ORDER))
    face_nodes = face_rows.shape[1]
    sub_span = sub_sends.shape[1]
    adjoint_lowered = adjoint.astype(jnp.bfloat16)
    traces = adjoint_lowered[:, face_rows, :]
    sub_out = jnp.stack(
        [jnp.take(traces[:, face_id], sub_sends[face_id], axis=2) for face_id in range(4)]
    )
    received = lax.all_to_all(sub_out, "sub", split_axis=3, concat_axis=3, tiled=True)
    upward = jnp.take(traces[:, 5], group_sends[1], axis=2)
    downward = jnp.take(traces[:, 4], group_sends[0], axis=2)
    from_below = passed_along(upward, "group", 1)
    from_above = passed_along(downward, "group", -1)
    gradient_terms = jnp.einsum(
        "hv,avr->ahr", derivatives, adjoint_lowered, preferred_element_type=jnp.float32
    )
    volume = (
        velocity[0] * gradient_terms[:, :node_count]
        + velocity[1] * gradient_terms[:, node_count : 2 * node_count]
        + velocity[2] * gradient_terms[:, 2 * node_count :]
    )
    outside_list = []
    for face_id in range(6):
        trace_id = face_id ^ 1
        positions = neighbours[face_id]
        if trace_id < 4:
            outside_list.append(pool_take(traces[:, trace_id], received[trace_id], positions))
        else:
            group_part = from_below if trace_id == 5 else from_above
            shifted = jnp.where(positions >= elements, positions - sub_span, positions)
            outside_list.append(pool_take(traces[:, trace_id], group_part, shifted))
    outside = jnp.stack(outside_list, axis=1)
    upwind = jnp.maximum(face_speed.astype(jnp.float32), 0.0).reshape(6, face_nodes, elements)
    face_flux_values = (upwind * (outside.astype(jnp.float32) - traces.astype(jnp.float32))).astype(
        jnp.bfloat16
    )
    face_flux_values = face_flux_values.reshape(species, 6 * face_nodes, elements)
    lifted_values = jnp.einsum(
        "dq,wqx->wdx", lift_operator, face_flux_values, preferred_element_type=jnp.float32
    )
    adjoint_next = adjoint + SECTION * (volume + lifted_values)
    next_lowered = adjoint_next.astype(jnp.bfloat16)
    contribution = jnp.einsum(
        "qvx,vj->xqj", next_lowered, emission_profile, preferred_element_type=jnp.float32
    ).reshape(elements, -1)
    tile_rows = jnp.take(tile_slot, element_tile)
    partial_sums = jax.ops.segment_sum(contribution, tile_rows, num_segments=tile_slot.shape[0])
    emission_grad = lax.psum_scatter(
        partial_sums, ("group", "sub"), scatter_dimension=0, tiled=True
    )
    return (adjoint_next, emission_grad)


def solution(mesh):
    placed = (
        P(None, None, ("group", "sub")),
        P(None, None, ("group", "sub")),
        P(None, ("group", "sub")),
        P(),
        P(),
        P(),
        P(None, ("group", "sub")),
        P(None, ("group", "sub")),
        P(None, ("group", "sub")),
        P(("group", "sub")),
        P(),
    )
    return jax.shard_map(
        on_device,
        mesh=mesh,
        in_specs=placed,
        out_specs=(P(None, None, ("group", "sub")), P(("group", "sub"), None)),
        check_vma=False,
    )
```

profile of v0, /device:TPU:0, one launch (start us, length us, event | category | flops | bytes accessed | tf_op | source)
XLA Modules:
  0.0 1100.0 jit_solution(9113211092727079033)
XLA Ops:
  8.8 10.8 copy.140
  19.6 12.1 %gather_fusion = bf16[216,4,2048]{2,1,0:T(4,128)(2,1)} fusion(bf16[4,256,2048]{2,0,1:T(4,128)(2,1)} %copy.140, s32[1024]{0:T(1024)S(1)} %get-tuple-element.47), kind=kCustom, calls=%fused_computation.12 | custom fusion | bytes 7078752 | tf_op jit(solution)/shard_map/gather | solution.py:61
  31.7 5.9 slice_bitcast_fusion
  48.5 5.1 gather_fusion.4
  57.4 9.1 gather_fusion.3
  66.5 5.3 select_bitcast_fusion.2
  71.8 9.1 gather_fusion.2
  80.9 6.1 select_bitcast_fusion.3
  86.9 9.1 gather_fusion.5
  96.1 5.3 select_bitcast_fusion
  101.4 5.5 copy_bitcast_fusion
  106.9 12.6 %reshape.210 = bf16[16,2,18432]{2,1,0:T(2,128)(2,1)} reshape(bf16[1024,4,4,36]{3,2,1,0:T(4,128)(2,1)} %copy_bitcast_fusion) | data formatting | bytes 2359296
  119.4 7.3 all-to-all-start
  147.7 12.2 %convolution_bitcast_fusion = f32[4,768,2048]{1,2,0:T(8,128)} fusion(bf16[4,256,2048]{2,0,1:T(4,128)(2,1)S(1)} %copy-done.3, bf16[768,256]{1,0:T(8,128)(2,1)S(1)} %copy-done), kind=kOutput, calls=%fused_computation.15 | convolution fusion | flops 3221225472 | bytes 29753344 | tf_op jit(solution)/shard_map/hv,avr->ahr/dot_general | solution.py:70
  159.9 11.8 %gather_fusion.1 = s32[2048]{0:T(1024)S(1)} fusion(s32[4096]{0:T(1024)S(1)} %copy-done.2, s32[2048]{0:T(1024)S(1)} %get-tuple-element.41), kind=kCustom, calls=%fused_computation.13 | custom fusion | bytes 24576 | tf_op jit(solution)/shard_map/jit(_take)/gather | solution.py:102
  171.8 8.7 copy.126
  195.1 16.1 %gather_fusion.11 = bf16[2048,4,36]{2,1,0:T(4,128)(2,1)} fusion(bf16[4,36,2304]{1,0,2:T(4,128)(2,1)} %copy.119, s32[2048]{0:T(1024)S(1)} %fusion.20), kind=kCustom, calls=%fused_computation.3.clone | custom fusion | bytes 1187840 | tf_op jit(solution)/shard_map/jit(_take)/gather | solution.py:40
  222.5 16.1 %gather_fusion.13 = bf16[2048,4,36]{2,1,0:T(4,128)(2,1)} fusion(bf16[4,36,2304]{1,0,2:T(4,128)(2,1)} %copy.123, s32[2048]{0:T(1024)S(1)} %fusion.21), kind=kCustom, calls=%fused_computation.11.clone | custom fusion | bytes 1187840 | tf_op jit(solution)/shard_map/jit(_take)/gather | solution.py:40
  242.9 15.5 %reshape.211 = bf16[1024,4,4,36]{3,2,1,0:T(4,128)(2,1)} reshape(bf16[16,2,18432]{2,1,0:T(2,128)(2,1)} %all-to-all-done) | data formatting | bytes 2359296
  266.8 5.5 copy.106
  272.3 16.3 %gather_fusion.6 = bf16[2048,4,36]{2,1,0:T(4,128)(2,1)} fusion(bf16[4,36,3072]{1,0,2:T(4,128)(2,1)} %copy.106, s32[2048]{0:T(1024)S(1)} %get-tuple-element.42), kind=kCustom, calls=%fused_computation.1.clone | custom fusion | bytes 1187840 | tf_op jit(solution)/shard_map/jit(_take)/gather | solution.py:40
  297.2 5.5 copy.109
  302.7 16.4 %gather_fusion.7 = bf16[2048,4,36]{2,1,0:T(4,128)(2,1)} fusion(bf16[4,36,3072]{1,0,2:T(4,128)(2,1)} %copy.109, s32[2048]{0:T(1024)S(1)} %get-tuple-element.43), kind=kCustom, calls=%fused_computation.7.clone | custom fusion | bytes 1187840 | tf_op jit(solution)/shard_map/jit(_take)/gather | solution.py:40
  327.6 5.5 copy.112
  333.1 16.4 %gather_fusion.8 = bf16[2048,4,36]{2,1,0:T(4,128)(2,1)} fusion(bf16[4,36,3072]{1,0,2:T(4,128)(2,1)} %copy.112, s32[2048]{0:T(1024)S(1)} %get-tuple-element.44), kind=kCustom, calls=%fused_computation.8.clone | custom fusion | bytes 1187840 | tf_op jit(solution)/shard_map/jit(_take)/gather | solution.py:40
  357.0 5.5 copy.115
  362.4 16.3 %gather_fusion.9 = bf16[2048,4,36]{2,1,0:T(4,128)(2,1)} fusion(bf16[4,36,3072]{1,0,2:T(4,128)(2,1)} %copy.115, s32[2048]{0:T(1024)S(1)} %fusion.19), kind=kCustom, calls=%fused_computation.9.clone | custom fusion | bytes 1187840 | tf_op jit(solution)/shard_map/jit(_take)/gather | solution.py:40
  393.6 7.3 fusion.5
  400.9 25.2 %fusion.3 = f32[4,256,2048]{1,2,0:T(8,128)} fusion(f32[4,256,2048]{1,2,0:T(8,128)} %copy.126, f32[4,768,2048]{1,2,0:T(8,128)} %convolution_bitcast_fusion, f32[256,2048]{0,1:T(8,128)} %copy.99, f32[256,2048]{0,1:T(8,128)} %copy.98, f32[256,2048]{0,1:T(8,128)S(1)} %copy.95, bf16[4,216,2048]{2,0,1:T(4,128)(2,1)} %fusion.5, bf16[256,216]{0,1:T(8,128)(2,1)S(1)} %copy-done.14), kind=kOutput, calls=%fused_computation.20 | convolution fusion | flops 922746880 | bytes 51884032 | tf_op jit(solution)/shard_map/dq,wqx->wdx/dot_general | solution.py:94
  431.1 12.9 %scatter_custom_fusion = f32[4096,128]{1,0:T(8,128)} fusion(s32[2048]{0:T(1024)S(1)} %and_select_fusion, f32[2048,128]{1,0:T(8,128)S(1)} %copy.128, f32[]{:T(128)} %constant.33.clone.1), kind=kCustom, calls=%fused_computation.41 | custom fusion | flops 262144 | bytes 2097156 | tf_op jit(solution)/shard_map/scatter-add | solution.py:103
  444.0 8.7 copy.129
  452.8 640.2 %reduce-scatter.2.cloned.1.call-done = f32[32,128]{1,0:T(8,128)} async-done(((f32[4096,128]{1,0:T(8,128)}), f32[32,128]{1,0:T(8,128)}) %reduce-scatter.2.cloned.1.call-update) | async-done | bytes 16400 | tf_op jit(solution)/shard_map/reduce_scatter | solution.py:104
  (118 shorter events, 120.0 us)
Async XLA Ops:
  7.2 140.5 %copy-start = (bf16[768,256]{1,0:T(8,128)(2,1)S(1)}, bf16[768,256]{1,0:T(8,128)(2,1)}, u32[]{:S(2)}) copy-start(bf16[768,256]{1,0:T(8,128)(2,1)} %param.23) | copy-start | bytes 1179652
  37.6 8.2 copy-start.6
  37.6 8.2 copy-start.7
  37.6 8.2 copy-start.5
  106.9 19.9 %copy-start.18 = (s32[2,256]{1,0:T(2,128)S(1)}, s32[2,256]{1,0:T(2,128)}, u32[]{:S(2)}) copy-start(s32[2,256]{1,0:T(2,128)} %param.28) | copy-start | bytes 6148
  106.9 20.0 %copy-start.9 = (bf16[4,36,2048]{2,0,1:T(4,128)(2,1)S(1)}, bf16[4,36,2048]{2,0,1:T(4,128)(2,1)}, u32[]{:S(2)}) copy-start(bf16[4,36,2048]{2,0,1:T(4,128)(2,1)} %get-tuple-element.21) | copy-start | bytes 1769476
  119.4 13.1 %copy-start.8 = (bf16[4,36,2048]{2,0,1:T(4,128)(2,1)S(1)}, bf16[4,36,2048]{2,0,1:T(4,128)(2,1)}, u32[]{:S(2)}) copy-start(bf16[4,36,2048]{2,0,1:T(4,128)(2,1)} %get-tuple-element.20) | copy-start | bytes 1769476
  119.4 123.4 %all-to-all-start = ((bf16[16,2,18432]{2,1,0:T(2,128)(2,1)}), bf16[16,2,18432]{2,1,0:T(2,128)(2,1)}, u32[]{:S(2)}, u32[]{:S(2)}) async-start(bf16[16,2,18432]{2,1,0:T(2,128)(2,1)} %reshape.210), calls=%async_computation | async-start | bytes 2359296 | tf_op jit(solution)/shard_map/all_to_all | solution.py:65
  126.8 966.2 %reduce-scatter.2.cloned.1.call-start = ((), (), s32[]{:S(2)}) async-start(), calls=%async_computation.2 | async-start | bytes 2113536 | tf_op jit(solution)/shard_map/reduce_scatter | solution.py:104
  126.9 14.3 %copy-start.15 = (s32[6,2048]{1,0:T(8,128)S(1)}, s32[6,2048]{1,0:T(8,128)}, u32[]{:S(2)}) copy-start(s32[6,2048]{1,0:T(8,128)} %param.26) | copy-start | bytes 147460
  126.9 14.5 %copy-start.16 = (s32[2048]{0:T(1024)S(1)}, s32[2048]{0:T(1024)}, u32[]{:S(2)}) copy-start(s32[2048]{0:T(1024)} %param.29) | copy-start | bytes 24580
  126.9 14.5 %copy-start.13 = (bf16[216,2048]{1,0:T(8,128)(2,1)S(1)}, bf16[216,2048]{1,0:T(8,128)(2,1)}, u32[]{:S(2)}) copy-start(bf16[216,2048]{1,0:T(8,128)(2,1)} %param.22) | copy-start | bytes 2654212
  132.4 55.7 %collective-permute-start = (bf16[4,36,256]{2,0,1:T(4,128)(2,1)S(1)}, bf16[4,36,256]{2,0,1:T(4,128)(2,1)S(1)}, u32[]{:S(2)}, u32[]{:S(2)}) collective-permute-start(bf16[4,36,256]{2,0,1:T(4,128)(2,1)S(1)} %select_bitcast_fusion.5), channel_id=1, source_target_pairs={{0,16},{16,32},{32,48},{48,64},{64,80},{80,96},{96,112},{112,0},{1... | collective-permute-start | bytes 221192 | tf_op jit(solution)/shard_map/ppermute | solution.py:16
  138.0 77.5 %collective-permute-start.1 = (bf16[4,36,256]{2,0,1:T(4,128)(2,1)S(1)}, bf16[4,36,256]{2,0,1:T(4,128)(2,1)S(1)}, u32[]{:S(2)}, u32[]{:S(2)}) collective-permute-start(bf16[4,36,256]{2,0,1:T(4,128)(2,1)S(1)} %select_bitcast_fusion.4), channel_id=1, source_target_pairs={{0,112},{16,0},{32,16},{48,32},{64,48},{80,64},{96,80},{112,96},{1... | collective-permute-start | bytes 221192 | tf_op jit(solution)/shard_map/ppermute | solution.py:16
  142.9 4.9 copy-start.3
  147.7 12.2 %copy-start.2 = (s32[4096]{0:T(1024)S(1)}, s32[4096]{0:T(1024)}, u32[]{:S(2)}) copy-start(s32[4096]{0:T(1024)} %param.30) | copy-start | bytes 49156
  378.8 9.6 copy-start.10
  383.3 4.7 copy-start.12
  383.3 5.5 copy-start.11
  384.8 4.4 copy-start.4
  393.6 7.3 copy-start.14
  400.9 25.2 %copy-start.17 = (bf16[256,32]{0,1:T(8,128)(2,1)S(1)}, bf16[256,32]{0,1:T(8,128)(2,1)}, u32[]{:S(2)}) copy-start(bf16[256,32]{0,1:T(8,128)(2,1)} %param.25) | copy-start | bytes 49156
  444.0 648.9 %copy-start.1 = (bf16[768,256]{1,0:T(8,128)(2,1)S(1)}, bf16[768,256]{1,0:T(8,128)(2,1)}, u32[]{:S(2)}) copy-start(bf16[768,256]{1,0:T(8,128)(2,1)} %param.23) | copy-start | bytes 1179652
Sparse Core Ops, SparseCore 0:
  444.2 648.7 reduce-scatter.1
where the time goes:
time: 1110 us; the launch traced here: 1100 us
  waiting for transfers between devices  640 us (58%)
  local copies, waits for them, and re-layouts  316 us (28%)
  other arithmetic  76.6 us (7%)
  matrix products  42.1 us (4%)
  between operations  14.7 us (1%)
    reduce_scatter x1, waiting for transfers between devices, on_device(): lax.psum_scatter(partial_sums, ('group', 'sub'), scatter_dimension=0, til...  640 us
    gather x12, local copies, waits for them, and re-layouts, pool_take(): return jnp.take(pool_rows, positions, axis=2)  123 us
    unnamed x47, local copies, waits for them, and re-layouts  63.7 us
    gather x4, local copies, waits for them, and re-layouts, on_device(): jnp.take(traces[:, face_id], sub_sends[face_id], axis=2)  32.4 us
    concatenate x6, local copies, waits for them, and re-layouts, pool_take(): pool_rows = jnp.concatenate([local_traces, received_part], axis=2)  31.4 us
    dot_general x1, matrix products, on_device(): jnp.einsum('dq,wqx->wdx', lift_operator, face_flux_values, preferred_elem...  25.2 us
  transfers between devices with their start and end apart: 4, of which 1 were waited for; matrix products, arithmetic and copies ran while one was open for 11% of the time, Pallas kernels for 0%

commit v1 on v0

v1 whole, which is shorter than its diff:
```python
import functools

import jax
import jax.numpy as jnp
import numpy as np
from jax import lax
from jax.experimental import pallas as pl
from jax.experimental.pallas import tpu as pltpu
from jax.sharding import PartitionSpec as P

ORDER = 5
SECTION = 0.125
PAD = 40
F32, BF16, I16, I32 = jnp.float32, jnp.bfloat16, jnp.int16, jnp.int32


def face_table(order):
    edge_nodes = order + 1
    coords_a, coords_b = np.meshgrid(np.arange(edge_nodes), np.arange(edge_nodes), indexing="ij")
    coords_a = coords_a.reshape(-1)
    coords_b = coords_b.reshape(-1)
    face_rows = []
    for axis_id in range(3):
        for level_id in (0, edge_nodes - 1):
            fixed_col = coords_a * 0 + level_id
            if axis_id == 0:
                triple = (fixed_col, coords_a, coords_b)
            elif axis_id == 1:
                triple = (coords_a, fixed_col, coords_b)
            else:
                triple = (coords_a, coords_b, fixed_col)
            face_rows.append((triple[0] * edge_nodes + triple[1]) * edge_nodes + triple[2])
    return np.stack(face_rows).astype(np.int32)


def node_selector(nodes):
    table = face_table(ORDER)
    out = np.zeros((6 * PAD, nodes), np.float32)
    for f in range(6):
        for k in range(table.shape[1]):
            out[f * PAD + k, table[f, k]] = 1.0
    return out


def row_spreader(face_nodes):
    out = np.zeros((6 * PAD, 6 * face_nodes), np.float32)
    for f in range(6):
        for k in range(face_nodes):
            out[f * PAD + k, f * face_nodes + k] = 1.0
    return out


def one_hot(count, positions):
    rows = lax.broadcasted_iota(I16, (count, positions.shape[1]), 0)
    return jnp.where(rows == positions.astype(I16), jnp.ones((), BF16), jnp.zeros((), BF16))


def dot(a, b):
    return jnp.dot(a, b, preferred_element_type=F32)


def send_kernel(adj_ref, sel_ref, ss_ref, gs_ref, pool_ref, send_ref, up_ref, down_ref, *, block):
    step = pl.program_id(0)
    cols = pl.ds(pl.multiple_of(step * block, block), block)
    for pair in range(2):
        first = dot(sel_ref[...], adj_ref[2 * pair].astype(BF16))
        second = dot(sel_ref[...], adj_ref[2 * pair + 1].astype(BF16))
        for f in range(6):
            rows = slice(f * PAD, (f + 1) * PAD)
            both = jnp.concatenate([first[rows], second[rows]], axis=0).astype(BF16)
            pool_ref[f, 2 * PAD * pair : 2 * PAD * (pair + 1), cols] = both

    @pl.when(step == pl.num_programs(0) - 1)
    def _():
        elements = pool_ref.shape[2]
        half = send_ref.shape[3] // 2
        low = lax.broadcasted_iota(I32, (4 * PAD, 2 * half), 1) < half
        for q in range(2):
            a = dot(pool_ref[2 * q], one_hot(elements, ss_ref[2 * q : 2 * q + 1, :]))
            b = dot(pool_ref[2 * q + 1], one_hot(elements, ss_ref[2 * q + 1 : 2 * q + 2, :]))
            for i in range(send_ref.shape[0] // 2):
                lanes = slice(2 * half * i, 2 * half * (i + 1))
                ai, bi = a[:, lanes], b[:, lanes]
                send_ref[2 * i, q] = jnp.where(low, ai, pltpu.roll(bi, half, 1)).astype(BF16)
                send_ref[2 * i + 1, q] = jnp.where(low, pltpu.roll(ai, half, 1), bi).astype(BF16)
        down_ref[...] = dot(pool_ref[4], one_hot(elements, gs_ref[0:1, :])).astype(BF16)
        up_ref[...] = dot(pool_ref[5], one_hot(elements, gs_ref[1:2, :])).astype(BF16)


def local_kernel(nbr_ref, pool_ref, tile_ref, slot_ref, out_ref, row_ref, *, chunk):
    f = pl.program_id(0)
    elements = pool_ref.shape[2]
    positions = nbr_ref[pl.ds(f, 1), :]
    for c in range(0, elements, chunk):
        hot = one_hot(elements, positions[:, c : c + chunk])
        out_ref[0, :, c : c + chunk] = dot(pool_ref[0], hot).astype(BF16)

    @pl.when(f == 0)
    def _():
        tiles = slot_ref.shape[1]
        slot = slot_ref[...]
        sub = lax.broadcasted_iota(I32, (16, tiles), 0)
        high = jnp.broadcast_to(jnp.right_shift(slot, 6), (16, tiles))
        lowd = jnp.broadcast_to(jnp.bitwise_and(slot, 63), (16, tiles))
        digits = jnp.where(sub == 0, high, jnp.where(sub == 1, lowd, 0)).astype(F32).astype(BF16)
        for c in range(0, elements, chunk):
            found = dot(digits, one_hot(tiles, tile_ref[:, c : c + chunk]))
            row_ref[:, c : c + chunk] = (found[0:1] * 64.0 + found[1:2]).astype(I32)


def volume_kernel(adj_ref, vel_ref, der_ref, out_ref):
    nodes = adj_ref.shape[1]
    for s in range(adj_ref.shape[0]):
        adj = adj_ref[s]
        g = dot(der_ref[...], adj.astype(BF16))
        vol = vel_ref[0].astype(F32) * g[:nodes]
        vol += vel_ref[1].astype(F32) * g[nodes : 2 * nodes]
        vol += vel_ref[2].astype(F32) * g[2 * nodes :]
        out_ref[s] = adj + SECTION * vol


def update_kernel(
    nbr_ref, pool_ref, loc_ref, recv_ref, below_ref, above_ref, fs_ref, spread_ref, lift_ref, prof_ref, base_ref,
    next_ref, contrib_ref, rpool, lift_pad, flux, *, elements,
):
    step = pl.program_id(0)
    peers, _, _, width = recv_ref.shape
    half = width // 2
    species = base_ref.shape[0]

    @pl.when(step == 0)
    def _():
        low = lax.broadcasted_iota(I32, (4 * PAD, width), 1) < half
        for q in range(2):
            for i in range(peers // 2):
                lanes = slice(width * i, width * (i + 1))
                x = recv_ref[2 * i, q].astype(F32)
                y = recv_ref[2 * i + 1, q].astype(F32)
                rpool[2 * q, :, lanes] = jnp.where(low, x, pltpu.roll(y, half, 1)).astype(BF16)
                rpool[2 * q + 1, :, lanes] = jnp.where(low, pltpu.roll(x, half, 1), y).astype(BF16)
        lift_pad[...] = lax.dot_general(
            lift_ref[...], spread_ref[...], (((1,), (1,)), ((), ())), preferred_element_type=F32
        ).astype(BF16)

    upwind = dot(spread_ref[...], jnp.maximum(fs_ref[...], jnp.zeros((), BF16)))
    slots = peers * half
    for q in range(3):
        parts = []
        for f in (2 * q, 2 * q + 1):
            t = f ^ 1
            if t < 4:
                hot = one_hot(slots, nbr_ref[f : f + 1, :] - elements)
                far = dot(rpool[t], hot)
            else:
                source = below_ref if t == 5 else above_ref
                hot = one_hot(source.shape[1], nbr_ref[f : f + 1, :] - (elements + slots))
                far = dot(source[...], hot)
            gap = (loc_ref[f].astype(F32) + far) - pool_ref[f].astype(F32)
            up = upwind[f * PAD : (f + 1) * PAD]
            parts.append([up * gap[s * PAD : (s + 1) * PAD] for s in range(species)])
        for s in range(species):
            both = jnp.concatenate([parts[0][s], parts[1][s]], axis=0).astype(BF16)
            flux[s, 2 * PAD * q : 2 * PAD * (q + 1), :] = both
    terms = []
    for s in range(species):
        value = base_ref[s] + SECTION * dot(lift_pad[...], flux[s])
        next_ref[s] = value
        terms.append(
            lax.dot_general(
                prof_ref[...], value.astype(BF16), (((0,), (0,)), ((), ())), preferred_element_type=F32
            )
        )
    contrib = jnp.transpose(jnp.concatenate(terms, axis=0))
    high = contrib.astype(BF16)
    contrib_ref[:, : contrib.shape[1]] = high
    contrib_ref[:, contrib.shape[1] :] = (contrib - high.astype(F32)).astype(BF16)


def scatter_kernel(row_ref, contrib_ref, out_ref):
    block, width = out_ref.shape
    first = pl.program_id(0) * block
    hot = one_hot(block, row_ref[...] - first)
    both = dot(hot, contrib_ref[...])
    out_ref[...] = (both[:, :width] + both[:, width:]).astype(BF16)


def whole(*shape):
    return pl.BlockSpec(shape, lambda i: (0,) * len(shape))


def params():
    return pltpu.CompilerParams(vmem_limit_bytes=48 * 1024 * 1024)


def cost(flops, nbytes):
    return pl.CostEstimate(flops=flops, bytes_accessed=nbytes, transcendentals=0)


def on_device(
    adjoint, velocity, face_speed, derivatives, lift_operator, emission_profile,
    neighbours, sub_sends, group_sends, element_tile, tile_slot,
):
    species, nodes, elements = adjoint.shape
    peers = lax.axis_size("sub")
    groups = lax.axis_size("group")
    slots = sub_sends.shape[1]
    half = slots // peers
    vcap = group_sends.shape[1]
    tiles = tile_slot.shape[0]
    heights = emission_profile.shape[1]
    face_rows = face_speed.shape[0]
    sel = jnp.asarray(node_selector(nodes), BF16)
    spread = jnp.asarray(row_spreader(face_rows // 6), BF16)
    rows = species * PAD
    sds = jax.ShapeDtypeStruct
    block = 512
    steps = elements // block

    pool, send, up, down = pl.pallas_call(
        functools.partial(send_kernel, block=block),
        grid=(steps,),
        in_specs=[
            pl.BlockSpec((species, nodes, block), lambda i: (0, 0, i)),
            whole(6 * PAD, nodes), whole(4, slots), whole(2, vcap),
        ],
        out_specs=[whole(6, rows, elements), whole(peers, 2, rows, 2 * half), whole(rows, vcap), whole(rows, vcap)],
        out_shape=[
            sds((6, rows, elements), BF16), sds((peers, 2, rows, 2 * half), BF16),
            sds((rows, vcap), BF16), sds((rows, vcap), BF16),
        ],
        compiler_params=params(),
        cost_estimate=cost(12_000_000_000, 14_000_000),
        name="sends",
    )(adjoint, sel, sub_sends, group_sends)

    received = lax.all_to_all(send, "sub", split_axis=0, concat_axis=0, tiled=True)
    ring_up = [(g, (g + 1) % groups) for g in range(groups)]
    ring_down = [(g, (g - 1) % groups) for g in range(groups)]
    from_below = lax.ppermute(up, "group", ring_up)
    from_above = lax.ppermute(down, "group", ring_down)

    local, tile_rows = pl.pallas_call(
        functools.partial(local_kernel, chunk=1024),
        grid=(6,),
        in_specs=[
            whole(6, elements),
            pl.BlockSpec((1, rows, elements), lambda f: (f + 1 - 2 * (f % 2), 0, 0)),
            whole(1, elements), whole(1, tiles),
        ],
        out_specs=[pl.BlockSpec((1, rows, elements), lambda f: (f, 0, 0)), whole(1, elements)],
        out_shape=[sds((6, rows, elements), BF16), sds((1, elements), I32)],
        compiler_params=params(),
        cost_estimate=cost(12_000_000_000, 8_000_000),
        name="local",
    )(neighbours, pool, element_tile.reshape(1, elements), tile_slot.reshape(1, tiles))

    base = pl.pallas_call(
        volume_kernel,
        grid=(steps,),
        in_specs=[
            pl.BlockSpec((species, nodes, block), lambda i: (0, 0, i)),
            pl.BlockSpec((3, nodes, block), lambda i: (0, 0, i)),
            whole(3 * nodes, nodes),
        ],
        out_specs=pl.BlockSpec((species, nodes, block), lambda i: (0, 0, i)),
        out_shape=sds((species, nodes, elements), F32),
        compiler_params=params(),
        cost_estimate=cost(3_200_000_000, 20_000_000),
        name="volume",
    )(adjoint, velocity, derivatives)

    adjoint_next, contrib = pl.pallas_call(
        functools.partial(update_kernel, elements=elements),
        grid=(steps,),
        in_specs=[
            pl.BlockSpec((6, block), lambda i: (0, i)),
            pl.BlockSpec((6, rows, block), lambda i: (0, 0, i)),
            pl.BlockSpec((6, rows, block), lambda i: (0, 0, i)),
            whole(peers, 2, rows, 2 * half), whole(rows, vcap), whole(rows, vcap),
            pl.BlockSpec((face_rows, block), lambda i: (0, i)),
            whole(6 * PAD, face_rows), whole(nodes, face_rows), whole(nodes, heights),
            pl.BlockSpec((species, nodes, block), lambda i: (0, 0, i)),
        ],
        out_specs=[
            pl.BlockSpec((species, nodes, block), lambda i: (0, 0, i)),
            pl.BlockSpec((block, 2 * species * heights), lambda i: (i, 0)),
        ],
        out_shape=[sds((species, nodes, elements), F32), sds((elements, 2 * species * heights), BF16)],
        scratch_shapes=[
            pltpu.VMEM((4, rows, slots), BF16), pltpu.VMEM((nodes, 6 * PAD), BF16),
            pltpu.VMEM((species, 6 * PAD, block), BF16),
        ],
        compiler_params=params(),
        cost_estimate=cost(8_000_000_000, 28_000_000),
        name="update",
    )(
        neighbours, pool, local, received, from_below, from_above, face_speed, spread,
        lift_operator, emission_profile, base,
    )

    width = species * heights
    row_block = 512
    partial = pl.pallas_call(
        scatter_kernel,
        grid=(tiles // row_block,),
        in_specs=[whole(1, elements), whole(elements, 2 * width)],
        out_specs=pl.BlockSpec((row_block, width), lambda i: (i, 0)),
        out_shape=sds((tiles, width), BF16),
        compiler_params=params(),
        cost_estimate=cost(4_300_000_000, 2_000_000),
        name="scatter",
    )(tile_rows, contrib)

    devices = groups * peers
    pieces = lax.all_to_all(
        partial.reshape(devices, tiles // devices, width), ("group", "sub"), split_axis=0, concat_axis=0
    )
    emission_grad = jnp.sum(pieces.astype(F32), axis=0)
    return adjoint_next, emission_grad


def solution(mesh):
    both = ("group", "sub")
    placed = (
        P(None, None, both), P(None, None, both), P(None, both), P(), P(), P(),
        P(None, both), P(None, both), P(None, both), P(both), P(),
    )
    return jax.shard_map(
        on_device,
        mesh=mesh,
        in_specs=placed,
        out_specs=(P(None, None, both), P(both, None)),
        check_vma=False,
    )
```

time: 1110 us -> 98.1 us (0.09)
  waiting for transfers between devices: 640 us -> 0.01 us
  local copies, waits for them, and re-layouts: 316 us -> 6.31 us
  other arithmetic: 76.6 us -> 0.8 us
  Pallas kernels: 0 us -> 50.7 us
  matrix products: 42.1 us -> 0 us
  blocking collectives: 0 us -> 28.6 us
  between operations: 14.7 us -> 0.79 us
    reduce_scatter x1 -> x0, waiting for transfers between devices: 640 us -> none  [on_device(): lax.psum_scatter(partial_sums, ('group', 'sub'), scatter_dimension=0, til...]
    gather x22 -> x0, local copies, waits for them, and re-layouts: 185 us -> none  [the longest x12 123 us: pool_take(): return jnp.take(pool_rows, positions, axis=2)]
    unnamed x47 -> x30, local copies, waits for them, and re-layouts: 63.7 us -> 6.31 us
    pallas_call x0 -> x5, Pallas kernels: none -> 50.7 us  [the longest x1 13.6 us: on_device(): pl.pallas_call(functools.partial(update_kernel, elements=elements), grid=...]
    dot_general x3 -> x0, matrix products: 42.1 us -> none  [the longest x1 25.2 us: on_device(): jnp.einsum('dq,wqx->wdx', lift_operator, face_flux_values, preferred_elem...]
    concatenate x6 -> x0, local copies, waits for them, and re-layouts: 31.4 us -> none  [pool_take(): pool_rows = jnp.concatenate([local_traces, received_part], axis=2)]
    all_to_all x0 -> x1, blocking collectives: none -> 28.6 us  [on_device(): lax.all_to_all(partial.reshape(devices, tiles // devices, width), ('group...]
    squeeze x7 -> x0, local copies, waits for them, and re-layouts: 22.1 us -> none  [the longest x3 11.2 us: on_device(): outside_list.append(pool_take(traces[:, trace_id], group_part, shifted))]
  transfers between devices with their start and end apart: 4 -> 3, of which waited for: 1 -> 0; matrix products, arithmetic and copies ran while one was open for 11% -> 0% of each run, Pallas kernels for 0% -> 23%
where the time goes in v1:
time: 98.1 us; the launch traced here: 97.5 us
  Pallas kernels  50.7 us (52%)
  blocking collectives  28.6 us (29%)
  starting transfers between devices  10.4 us (11%)
  local copies, waits for them, and re-layouts  6.31 us (6%)
    all_to_all x1, blocking collectives, on_device(): lax.all_to_all(partial.reshape(devices, tiles // devices, width), ('group...  28.6 us
    pallas_call x1, Pallas kernels, on_device(): pl.pallas_call(functools.partial(update_kernel, elements=elements), grid=...  13.6 us
    pallas_call x1, Pallas kernels, on_device(): pl.pallas_call(functools.partial(local_kernel, chunk=1024), grid=(6,), in...  12.9 us
    pallas_call x1, Pallas kernels, on_device(): pl.pallas_call(volume_kernel, grid=(steps,), in_specs=[pl.BlockSpec((spec...  9.37 us
    pallas_call x1, Pallas kernels, on_device(): pl.pallas_call(functools.partial(send_kernel, block=block), grid=(steps,)...  9.17 us
    all_to_all x1, starting transfers between devices, on_device(): lax.all_to_all(send, 'sub', split_axis=0, concat_axis=0, tiled=True)  7.15 us
    unnamed x30, local copies, waits for them, and re-layouts  6.31 us
    pallas_call x1, Pallas kernels, on_device(): pl.pallas_call(scatter_kernel, grid=(tiles // row_block,), in_specs=[whol...  5.71 us
  transfers between devices with their start and end apart: 3, of which 0 were waited for; matrix products, arithmetic and copies ran while one was open for 0% of the time, Pallas kernels for 23%

profile of v1, /device:TPU:0, one launch (start us, length us, event | category | flops | bytes accessed | tf_op | source)
XLA Modules:
  0.0 97.5 jit_solution(2623120942372970641)
XLA Ops:
  0.6 0.0 copy-start.3
  0.6 0.0 copy-start.4
  0.7 0.7 copy-done.4
  1.4 0.7 copy-done.7
  2.1 0.9 copy-done.9
  3.0 9.2 %sends.1 = (bf16[6,160,2048]{2,1,0:T(8,128)(2,1)S(1)}, bf16[16,2,160,128]{3,2,1,0:T(8,128)(2,1)}, bf16[160,256]{1,0:T(8,128)(2,1)S(1)}, bf16[160,256]{1,0:T(8,128)(2,1)S(1)}) custom-call(f32[4,256,2048]{2,1,0:T(8,128)} %adj_ref.3, bf16[240,256]{1,0:T(8,128)(2,1)S(1)} %copy-done.9, s32[4,1024]{1,0:T(4,128)S(1)} %copy-done.4, s32[2,256]{1,0:T(2,128)S(1)} %copy-done.7), custom_call_target="tpu_custom_call" | custom-call | flops 12000000000 | bytes 14000000 | tf_op jit(solution)/shard_map/sends/pallas_call | solution.py:219
  12.1 1.9 %copy-done.10 = bf16[6,160,2048]{2,1,0:T(8,128)(2,1)} copy-done((bf16[6,160,2048]{2,1,0:T(8,128)(2,1)}, bf16[6,160,2048]{2,1,0:T(8,128)(2,1)S(1)}, u32[]{:S(2)}) %copy-start.10) | copy-done | bytes 3932184
  14.0 7.1 %all-to-all-start = ((bf16[16,2,160,128]{3,2,1,0:T(8,128)(2,1)}), bf16[16,2,160,128]{3,2,1,0:T(8,128)(2,1)S(1)}, u32[]{:S(2)}, u32[]{:S(2)}) async-start(bf16[16,2,160,128]{3,2,1,0:T(8,128)(2,1)} %get-tuple-element.12), calls=%async_computation | async-start | bytes 2621440 | tf_op jit(solution)/shard_map/all_to_all | solution.py:236
  21.2 0.0 collective-permute-start
  21.2 3.2 %collective-permute-start.1 = (bf16[160,256]{1,0:T(8,128)(2,1)S(1)}, bf16[160,256]{1,0:T(8,128)(2,1)S(1)}, u32[]{:S(2)}, u32[]{:S(2)}) collective-permute-start(bf16[160,256]{1,0:T(8,128)(2,1)S(1)} %get-tuple-element.14), channel_id=1, source_target_pairs={{0,112},{16,0},{32,16},{48,32},{64,48},{80,64},{96,80},{112,96},{1... | collective-permute-start | bytes 245768 | tf_op jit(solution)/shard_map/ppermute | solution.py:240
  24.4 0.0 copy-done.3
  24.4 0.0 copy-done.5
  24.4 0.0 copy-done.6
  24.4 0.0 copy-start.1
  24.4 12.9 %local.1 = (bf16[6,160,2048]{2,1,0:T(8,128)(2,1)S(1)}, s32[1,2048]{1,0:T(1,128)S(1)}) custom-call(s32[6,2048]{1,0:T(8,128)S(1)} %copy-done.3, bf16[6,160,2048]{2,1,0:T(8,128)(2,1)} %copy-done.10, s32[1,2048]{1,0:T(1,128)S(1)} %bitcast.5, s32[1,4096]{1,0:T(1,128)S(1)} %bitcast.4), custom_call_target="tpu_custom_call" | custom-call | flops 12000000000 | bytes 8000000 | tf_op jit(solution)/shard_map/local/pallas_call | solution.py:242
  37.3 0.0 copy-start.11
  37.3 1.9 %copy-done.11 = bf16[6,160,2048]{2,1,0:T(8,128)(2,1)} copy-done((bf16[6,160,2048]{2,1,0:T(8,128)(2,1)}, bf16[6,160,2048]{2,1,0:T(8,128)(2,1)S(1)}, u32[]{:S(2)}) %copy-start.11) | copy-done | bytes 3932184
  39.2 0.0 copy-done
  39.2 0.0 copy-done.1
  39.2 0.0 copy-start.2
  39.2 0.0 copy-start.8
  39.2 9.4 %volume.1.base_ref = f32[4,256,2048]{2,1,0:T(8,128)} custom-call(f32[4,256,2048]{2,1,0:T(8,128)} %adj_ref.3, bf16[3,256,2048]{2,1,0:T(8,128)(2,1)S(1)} %copy-done, bf16[768,256]{1,0:T(8,128)(2,1)S(1)} %copy-done.1), custom_call_target="tpu_custom_call" | custom-call | flops 3200000000 | bytes 20000000 | tf_op jit(solution)/shard_map/volume/pallas_call | solution.py:257
  48.6 0.0 copy-done.13
  48.6 0.1 copy.16.prof_ref
  48.7 0.1 copy.15.lift_ref
  48.8 0.0 collective-permute-done.below_ref
  48.8 0.0 collective-permute-done.1.above_ref
  48.8 0.0 all-to-all-done.recv_ref
  48.9 13.6 %update.1 = (f32[4,256,2048]{2,1,0:T(8,128)}, bf16[2048,256]{1,0:T(8,128)(2,1)S(1)}) custom-call(s32[6,2048]{1,0:T(8,128)S(1)} %copy-done.3, bf16[6,160,2048]{2,1,0:T(8,128)(2,1)} %copy-done.10, bf16[6,160,2048]{2,1,0:T(8,128)(2,1)} %copy-done.11, bf16[16,2,160,128]{3,2,1,0:T(8,128)(2,1)S(1)} %all-to-all-done.recv_ref, ...), custom_call_target="tpu_custom_call" | custom-call | flops 8000000000 | bytes 28000000 | tf_op jit(solution)/shard_map/update/pallas_call | solution.py:272
  62.4 5.7 %scatter.1 = bf16[4096,128]{1,0:T(8,128)(2,1)S(1)} custom-call(s32[1,2048]{1,0:T(1,128)S(1)} %get-tuple-element.16.row_ref, bf16[2048,256]{1,0:T(8,128)(2,1)S(1)} %get-tuple-element.17.contrib_ref), custom_call_target="tpu_custom_call" | custom-call | flops 4300000256 | bytes 2000000 | tf_op jit(solution)/shard_map/scatter/pallas_call | solution.py:303
  68.1 28.6 %all_to_all.10 = bf16[128,32,128]{2,1,0:T(8,128)(2,1)S(1)} all-to-all(bf16[128,32,128]{2,1,0:T(8,128)(2,1)S(1)} %bitcast.3), channel_id=1, replica_groups=mesh['group'=8,'sub'=16] {'group','sub'}, dimensions={0} | all-to-all | bytes 2097152 | tf_op jit(solution)/shard_map/all_to_all | solution.py:315
  96.7 0.8 convert_reduce_fusion
  (11 shorter events, 0.0 us)
Async XLA Ops:
  0.6 23.8 %copy-start.3 = (s32[6,2048]{1,0:T(8,128)S(1)}, s32[6,2048]{1,0:T(8,128)}, u32[]{:S(2)}) copy-start(s32[6,2048]{1,0:T(8,128)} %nbr_ref.3) | copy-start | bytes 147460
  0.6 0.7 copy-start.4
  1.4 0.7 copy-start.7
  2.1 0.9 copy-start.9
  3.0 21.4 %copy-start.5 = (s32[4096]{0:T(1024)S(1)}, s32[4096]{0:T(1024)}, u32[]{:S(2)}) copy-start(s32[4096]{0:T(1024)} %param.23) | copy-start | bytes 49156
  3.0 21.4 %copy-start.6 = (s32[2048]{0:T(1024)S(1)}, s32[2048]{0:T(1024)}, u32[]{:S(2)}) copy-start(s32[2048]{0:T(1024)} %param.22) | copy-start | bytes 24580
  12.1 1.9 %copy-start.10 = (bf16[6,160,2048]{2,1,0:T(8,128)(2,1)}, bf16[6,160,2048]{2,1,0:T(8,128)(2,1)S(1)}, u32[]{:S(2)}) copy-start(bf16[6,160,2048]{2,1,0:T(8,128)(2,1)S(1)} %get-tuple-element.10.pool_ref) | copy-start | bytes 11796484
  14.0 34.8 %all-to-all-start = ((bf16[16,2,160,128]{3,2,1,0:T(8,128)(2,1)}), bf16[16,2,160,128]{3,2,1,0:T(8,128)(2,1)S(1)}, u32[]{:S(2)}, u32[]{:S(2)}) async-start(bf16[16,2,160,128]{3,2,1,0:T(8,128)(2,1)} %get-tuple-element.12), calls=%async_computation | async-start | bytes 2621440 | tf_op jit(solution)/shard_map/all_to_all | solution.py:236
  21.2 27.6 %collective-permute-start = (bf16[160,256]{1,0:T(8,128)(2,1)S(1)}, bf16[160,256]{1,0:T(8,128)(2,1)S(1)}, u32[]{:S(2)}, u32[]{:S(2)}) collective-permute-start(bf16[160,256]{1,0:T(8,128)(2,1)S(1)} %get-tuple-element.13), channel_id=1, source_target_pairs={{0,16},{16,32},{32,48},{48,64},{64,80},{80,96},{96,112},{112,0},{1... | collective-permute-start | bytes 245768 | tf_op jit(solution)/shard_map/ppermute | solution.py:239
  21.2 27.6 %collective-permute-start.1 = (bf16[160,256]{1,0:T(8,128)(2,1)S(1)}, bf16[160,256]{1,0:T(8,128)(2,1)S(1)}, u32[]{:S(2)}, u32[]{:S(2)}) collective-permute-start(bf16[160,256]{1,0:T(8,128)(2,1)S(1)} %get-tuple-element.14), channel_id=1, source_target_pairs={{0,112},{16,0},{32,16},{48,32},{64,48},{80,64},{96,80},{112,96},{1... | collective-permute-start | bytes 245768 | tf_op jit(solution)/shard_map/ppermute | solution.py:240
  24.4 14.8 %copy-start = (bf16[3,256,2048]{2,1,0:T(8,128)(2,1)S(1)}, bf16[3,256,2048]{2,1,0:T(8,128)(2,1)}, u32[]{:S(2)}) copy-start(bf16[3,256,2048]{2,1,0:T(8,128)(2,1)} %vel_ref.1) | copy-start | bytes 9437188
  24.4 14.8 %copy-start.1 = (bf16[768,256]{1,0:T(8,128)(2,1)S(1)}, bf16[768,256]{1,0:T(8,128)(2,1)}, u32[]{:S(2)}) copy-start(bf16[768,256]{1,0:T(8,128)(2,1)} %der_ref.1) | copy-start | bytes 1179652
  37.3 1.9 %copy-start.11 = (bf16[6,160,2048]{2,1,0:T(8,128)(2,1)}, bf16[6,160,2048]{2,1,0:T(8,128)(2,1)S(1)}, u32[]{:S(2)}) copy-start(bf16[6,160,2048]{2,1,0:T(8,128)(2,1)S(1)} %get-tuple-element.11.loc_ref) | copy-start | bytes 11796484
  39.2 9.4 %copy-start.13 = (bf16[256,32]{0,1:T(8,128)(2,1)S(1)}, bf16[256,32]{0,1:T(8,128)(2,1)}, u32[]{:S(2)}) copy-start(bf16[256,32]{0,1:T(8,128)(2,1)} %param.18) | copy-start | bytes 49156
  39.2 9.5 %copy-start.12 = (bf16[256,216]{0,1:T(8,128)(2,1)S(1)}, bf16[256,216]{0,1:T(8,128)(2,1)}, u32[]{:S(2)}) copy-start(bf16[256,216]{0,1:T(8,128)(2,1)} %param.17) | copy-start | bytes 331780
  39.2 9.7 %copy-start.2 = (bf16[216,2048]{1,0:T(8,128)(2,1)S(1)}, bf16[216,2048]{1,0:T(8,128)(2,1)}, u32[]{:S(2)}) copy-start(bf16[216,2048]{1,0:T(8,128)(2,1)} %fs_ref.1) | copy-start | bytes 2654212
  39.2 9.7 %copy-start.8 = (bf16[240,216]{1,0:T(8,128)(2,1)S(1)}, bf16[240,216]{1,0:T(8,128)(2,1)}, u32[]{:S(2)}) copy-start(bf16[240,216]{1,0:T(8,128)(2,1)} %constant.7.clone.spread_ref) | copy-start | bytes 311044

commit v2 on v1

v2 whole, which is shorter than its diff:
```python
import functools

import jax
import jax.numpy as jnp
import numpy as np
from jax import lax
from jax.experimental import pallas as pl
from jax.experimental.pallas import tpu as pltpu
from jax.sharding import Mesh, PartitionSpec as P

ORDER = 5
SECTION = 0.125
MIB = 1024 * 1024
PAD = 40
F32, BF16, I16, I32 = jnp.float32, jnp.bfloat16, jnp.int16, jnp.int32


def face_table(order):
    edge_nodes = order + 1
    coords_a, coords_b = np.meshgrid(np.arange(edge_nodes), np.arange(edge_nodes), indexing="ij")
    coords_a = coords_a.reshape(-1)
    coords_b = coords_b.reshape(-1)
    face_rows = []
    for axis_id in range(3):
        for level_id in (0, edge_nodes - 1):
            fixed_col = coords_a * 0 + level_id
            if axis_id == 0:
                triple = (fixed_col, coords_a, coords_b)
            elif axis_id == 1:
                triple = (coords_a, fixed_col, coords_b)
            else:
                triple = (coords_a, coords_b, fixed_col)
            face_rows.append((triple[0] * edge_nodes + triple[1]) * edge_nodes + triple[2])
    return np.stack(face_rows).astype(np.int32)


def node_selector(nodes):
    table = face_table(ORDER)
    out = np.zeros((6 * PAD, nodes), np.float32)
    for f in range(6):
        for k in range(table.shape[1]):
            out[f * PAD + k, table[f, k]] = 1.0
    return out


def row_spreader(face_nodes):
    out = np.zeros((6 * PAD, 6 * face_nodes), np.float32)
    for f in range(6):
        for k in range(face_nodes):
            out[f * PAD + k, f * face_nodes + k] = 1.0
    return out


def one_hot(count, positions):
    rows = lax.broadcasted_iota(I16, (count, positions.shape[1]), 0)
    return jnp.where(rows == positions.astype(I16), jnp.ones((), BF16), jnp.zeros((), BF16))


def dot(a, b):
    return jnp.dot(a, b, preferred_element_type=F32)


def send_kernel(adj_ref, sel_ref, ss_ref, gs_ref, pool_ref, send_ref, up_ref, down_ref, *, block):
    step = pl.program_id(0)
    cols = pl.ds(pl.multiple_of(step * block, block), block)
    for pair in range(2):
        picked = [dot(sel_ref[...], adj_ref[s].astype(BF16)) for s in (2 * pair, 2 * pair + 1)]
        for f in range(6):
            rows = slice(f * PAD, (f + 1) * PAD)
            both = jnp.concatenate([picked[0][rows], picked[1][rows]], axis=0).astype(BF16)
            pool_ref[f, 2 * PAD * pair : 2 * PAD * (pair + 1), cols] = both

    @pl.when(step == pl.num_programs(0) - 1)
    def _():
        elements = pool_ref.shape[2]
        half = send_ref.shape[3] // 2
        low = lax.broadcasted_iota(I32, (4 * PAD, 2 * half), 1) < half
        for q in range(2):
            a = dot(pool_ref[2 * q], one_hot(elements, ss_ref[2 * q : 2 * q + 1, :]))
            b = dot(pool_ref[2 * q + 1], one_hot(elements, ss_ref[2 * q + 1 : 2 * q + 2, :]))
            for i in range(send_ref.shape[0] // 2):
                lanes = slice(2 * half * i, 2 * half * (i + 1))
                ai, bi = a[:, lanes], b[:, lanes]
                send_ref[2 * i, q] = jnp.where(low, ai, pltpu.roll(bi, half, 1)).astype(BF16)
                send_ref[2 * i + 1, q] = jnp.where(low, pltpu.roll(ai, half, 1), bi).astype(BF16)
        down_ref[...] = dot(pool_ref[4], one_hot(elements, gs_ref[0:1, :])).astype(BF16)
        up_ref[...] = dot(pool_ref[5], one_hot(elements, gs_ref[1:2, :])).astype(BF16)


def local_kernel(
    adj_ref, vel_ref, der_ref, nbr_ref, pool_hbm, tile_ref, slot_ref, base_ref, gap_ref, row_ref, pool, mixed, sems,
):
    step = pl.program_id(0)
    species, nodes, block = adj_ref.shape
    group = 16
    copies = [pltpu.make_async_copy(pool_hbm.at[f], pool.at[f], sems.at[f]) for f in range(6)]

    @pl.when(step == 0)
    def _():
        for copy in copies:
            copy.start()
        for d in range(3):
            for b in range(nodes // group):
                rows = der_ref[d * nodes + b * group : d * nodes + (b + 1) * group, :]
                mixed[(3 * b + d) * group : (3 * b + d + 1) * group, :] = rows * jnp.asarray(SECTION, BF16)

    for s in range(species):
        g = dot(mixed[...], adj_ref[s].astype(BF16))
        for b in range(nodes // group):
            rows = slice(b * group, (b + 1) * group)
            total = adj_ref[s, rows]
            for d in range(3):
                total += vel_ref[d, rows].astype(F32) * g[(3 * b + d) * group : (3 * b + d + 1) * group]
            base_ref[s, rows] = total

    @pl.when(step == 0)
    def _():
        high = slot_ref.shape[0]
        elements = tile_ref.shape[1]
        slot = jnp.transpose(slot_ref[...].astype(F32))
        upper = jnp.floor(slot * (1.0 / 64.0))
        digits = jnp.concatenate([upper, slot - 64.0 * upper], axis=0).astype(BF16)
        lanes = slot_ref.shape[1]
        for c in range(0, elements, block):
            tile = tile_ref[:, c : c + block]
            shift = lanes.bit_length() - 1
            found = dot(digits, one_hot(high, jnp.right_shift(tile, shift)))
            rows = 64.0 * found[:lanes] + found[lanes:]
            within = lax.broadcasted_iota(I32, rows.shape, 0) == jnp.bitwise_and(tile, lanes - 1)
            row_ref[:, c : c + block] = jnp.sum(jnp.where(within, rows, 0.0), axis=0, keepdims=True).astype(I32)
        for copy in copies:
            copy.wait()

    cols = pl.ds(pl.multiple_of(step * block, block), block)
    for f in range(6):
        hot = one_hot(pool.shape[2], nbr_ref[f : f + 1, :])
        gap_ref[f] = dot(pool[f ^ 1], hot) - pool[f, :, cols].astype(F32)


def update_kernel(
    nbr_ref, gap_ref, recv_ref, below_ref, above_ref, fs_ref, spread_ref, lift_ref, prof_ref, base_ref,
    next_ref, contrib_ref, rpool, lift_pad, flux, *, elements,
):
    step = pl.program_id(0)
    peers, _, _, width = recv_ref.shape
    half = width // 2
    species = base_ref.shape[0]

    @pl.when(step == 0)
    def _():
        low = lax.broadcasted_iota(I32, (4 * PAD, width), 1) < half
        for q in range(2):
            for i in range(peers // 2):
                lanes = slice(width * i, width * (i + 1))
                x = recv_ref[2 * i, q].astype(F32)
                y = recv_ref[2 * i + 1, q].astype(F32)
                rpool[2 * q, :, lanes] = jnp.where(low, x, pltpu.roll(y, half, 1)).astype(BF16)
                rpool[2 * q + 1, :, lanes] = jnp.where(low, pltpu.roll(x, half, 1), y).astype(BF16)
        lift_pad[...] = (SECTION * jnp.transpose(dot(spread_ref[...], lift_ref[...]))).astype(BF16)

    upwind = dot(spread_ref[...], jnp.maximum(fs_ref[...], jnp.zeros((), BF16)))
    slots = peers * half
    for q in range(3):
        parts = []
        for f in (2 * q, 2 * q + 1):
            t = f ^ 1
            if t < 4:
                hot = one_hot(slots, nbr_ref[f : f + 1, :] - elements)
                far = dot(rpool[t], hot)
            else:
                source = below_ref if t == 5 else above_ref
                hot = one_hot(source.shape[1], nbr_ref[f : f + 1, :] - (elements + slots))
                far = dot(source[...], hot)
            gap = gap_ref[f] + far
            up = upwind[f * PAD : (f + 1) * PAD]
            parts.append([up * gap[s * PAD : (s + 1) * PAD] for s in range(species)])
        for s in range(species):
            both = jnp.concatenate([parts[0][s], parts[1][s]], axis=0).astype(BF16)
            flux[s, 2 * PAD * q : 2 * PAD * (q + 1), :] = both
    terms = []
    for s in range(species):
        value = base_ref[s] + dot(lift_pad[...], flux[s])
        next_ref[s] = value
        terms.append(dot(prof_ref[...], value.astype(BF16)))
    contrib = jnp.transpose(jnp.concatenate(terms, axis=0))
    high = contrib.astype(BF16)
    contrib_ref[:, : contrib.shape[1]] = high
    contrib_ref[:, contrib.shape[1] :] = (contrib - high.astype(F32)).astype(BF16)


def scatter_kernel(row_ref, contrib_ref, out_ref, *, other):
    block, width = out_ref.shape
    core = lax.axis_index("core")
    half = 1 - core if other else core
    first = (2 * pl.program_id(0) + half) * block
    hot = one_hot(block, row_ref[...] - first)
    both = dot(hot, contrib_ref[...])
    out_ref[...] = both[:, :width] + both[:, width:]


def whole(*shape):
    return pl.BlockSpec(shape, lambda i: (0,) * len(shape))


def params(mib):
    return pltpu.CompilerParams(vmem_limit_bytes=mib * MIB)


def cost(flops, nbytes):
    return pl.CostEstimate(flops=flops, bytes_accessed=nbytes, transcendentals=0)


def on_device(
    adjoint, velocity, face_speed, derivatives, lift_operator, emission_profile,
    neighbours, sub_sends, group_sends, element_tile, tile_slot,
):
    species, nodes, elements = adjoint.shape
    peers = lax.axis_size("sub")
    groups = lax.axis_size("z") * lax.axis_size("core")
    slots = sub_sends.shape[1]
    half = slots // peers
    vcap = group_sends.shape[1]
    tiles = tile_slot.shape[0]
    heights = emission_profile.shape[1]
    face_rows = face_speed.shape[0]
    sel = jnp.asarray(node_selector(nodes), BF16)
    spread = jnp.asarray(row_spreader(face_rows // 6), BF16)
    rows = species * PAD
    sds = jax.ShapeDtypeStruct
    block = 512
    steps = elements // block

    pool, send, up, down = pl.pallas_call(
        functools.partial(send_kernel, block=block),
        grid=(steps,),
        in_specs=[
            pl.BlockSpec((species, nodes, block), lambda i: (0, 0, i)),
            whole(6 * PAD, nodes), whole(4, slots), whole(2, vcap),
        ],
        out_specs=[whole(6, rows, elements), whole(peers, 2, rows, 2 * half), whole(rows, vcap), whole(rows, vcap)],
        out_shape=[
            sds((6, rows, elements), BF16), sds((peers, 2, rows, 2 * half), BF16),
            sds((rows, vcap), BF16), sds((rows, vcap), BF16),
        ],
        compiler_params=params(60),
        cost_estimate=cost(12_000_000_000, 14_000_000),
        name="sends",
    )(adjoint, sel, sub_sends, group_sends)

    received = lax.all_to_all(send, "sub", split_axis=0, concat_axis=0, tiled=True)
    ring_up = [(g, (g + 1) % groups) for g in range(groups)]
    ring_down = [(g, (g - 1) % groups) for g in range(groups)]
    from_below = lax.ppermute(up, ("z", "core"), ring_up)
    from_above = lax.ppermute(down, ("z", "core"), ring_down)

    base, gap, tile_rows = pl.pallas_call(
        local_kernel,
        grid=(steps,),
        in_specs=[
            pl.BlockSpec((species, nodes, block), lambda i: (0, 0, i)),
            pl.BlockSpec((3, nodes, block), lambda i: (0, 0, i)),
            whole(3 * nodes, nodes),
            pl.BlockSpec((6, block), lambda i: (0, i)),
            pl.BlockSpec(memory_space=pl.ANY),
            whole(1, elements), whole(tiles // 128, 128),
        ],
        out_specs=[
            pl.BlockSpec((species, nodes, block), lambda i: (0, 0, i)),
            pl.BlockSpec((6, rows, block), lambda i: (0, 0, i)),
            whole(1, elements),
        ],
        out_shape=[
            sds((species, nodes, elements), F32), sds((6, rows, elements), F32), sds((1, elements), I32),
        ],
        scratch_shapes=[
            pltpu.VMEM((6, rows, elements), BF16), pltpu.VMEM((3 * nodes, nodes), BF16), pltpu.SemaphoreType.DMA((6,)),
        ],
        compiler_params=params(60),
        cost_estimate=cost(16_000_000_000, 32_000_000),
        name="local",
    )(
        adjoint, velocity, derivatives, neighbours, pool, element_tile.reshape(1, elements),
        tile_slot.reshape(tiles // 128, 128),
    )

    adjoint_next, contrib = pl.pallas_call(
        functools.partial(update_kernel, elements=elements),
        grid=(steps,),
        in_specs=[
            pl.BlockSpec((6, block), lambda i: (0, i)),
            pl.BlockSpec((6, rows, block), lambda i: (0, 0, i)),
            whole(peers, 2, rows, 2 * half), whole(rows, vcap), whole(rows, vcap),
            pl.BlockSpec((face_rows, block), lambda i: (0, i)),
            whole(6 * PAD, face_rows), whole(face_rows, nodes), whole(heights, nodes),
            pl.BlockSpec((species, nodes, block), lambda i: (0, 0, i)),
        ],
        out_specs=[
            pl.BlockSpec((species, nodes, block), lambda i: (0, 0, i)),
            pl.BlockSpec((block, 2 * species * heights), lambda i: (i, 0)),
        ],
        out_shape=[sds((species, nodes, elements), F32), sds((elements, 2 * species * heights), BF16)],
        scratch_shapes=[
            pltpu.VMEM((4, rows, slots), BF16), pltpu.VMEM((nodes, 6 * PAD), BF16),
            pltpu.VMEM((species, 6 * PAD, block), BF16),
        ],
        compiler_params=params(56),
        cost_estimate=cost(8_000_000_000, 28_000_000),
        name="update",
    )(
        neighbours, gap, received, from_below, from_above, face_speed, spread,
        lift_operator.T, emission_profile.T, base,
    )

    width = species * heights
    row_block = tiles // groups

    def scattered(other):
        return pl.pallas_call(
            functools.partial(scatter_kernel, other=other),
            grid=(groups // 2,),
            in_specs=[whole(1, elements), whole(elements, 2 * width)],
            out_specs=pl.BlockSpec((row_block, width), lambda i: (i, 0)),
            out_shape=sds((tiles // 2, width), F32),
            compiler_params=params(16),
            cost_estimate=cost(2_100_000_000, 2_000_000),
            name="scatter_other" if other else "scatter_own",
        )(tile_rows, contrib)

    theirs = lax.ppermute(scattered(True), "core", [(0, 1), (1, 0)])
    partial = (scattered(False) + theirs).astype(BF16)
    chips = groups * peers // 2
    pieces = lax.all_to_all(
        partial.reshape(chips, tiles // 2 // chips, width), ("z", "sub"), split_axis=0, concat_axis=0
    )
    emission_grad = jnp.sum(pieces.astype(F32), axis=0)
    return adjoint_next, emission_grad


def solution(mesh):
    groups, peers = mesh.devices.shape
    mesh = Mesh(mesh.devices.reshape(groups // 2, 2, peers), ("z", "core", "sub"))
    both = ("z", "core", "sub")
    placed = (
        P(None, None, both), P(None, None, both), P(None, both), P(), P(), P(),
        P(None, both), P(None, both), P(None, both), P(both), P(),
    )
    return jax.shard_map(
        on_device,
        mesh=mesh,
        in_specs=placed,
        out_specs=(P(None, None, both), P(both, None)),
        check_vma=False,
    )
```

time: 98.1 us -> 87.2 us (0.89)
  blocking collectives: 28.6 us -> 23.9 us
  local copies, waits for them, and re-layouts: 6.31 us -> 2.29 us
  Pallas kernels: 50.7 us -> 48.7 us
    all_to_all x1, blocking collectives: 28.6 us -> 23.9 us  [on_device(): lax.all_to_all(partial.reshape(chips, tiles // 2 // chips, width), ('z',...]
    pallas_call x3, Pallas kernels: 27.9 us -> 23.5 us  [the longest x1 17.8 us: on_device(): pl.pallas_call(local_kernel, grid=(steps,), in_specs=[pl.BlockSpec((speci...]
    unnamed x30 -> x10, local copies, waits for them, and re-layouts: 6.31 us -> 2.29 us
    pallas_call x1, Pallas kernels: 9.17 us -> 10.6 us  [on_device(): pl.pallas_call(functools.partial(send_kernel, block=block), grid=(steps,)...]
    pallas_call x1, Pallas kernels: 13.6 us -> 14.6 us  [on_device(): pl.pallas_call(functools.partial(update_kernel, elements=elements), grid=...]
    ppermute x2 -> x3, starting transfers between devices: 3.23 us -> 3.31 us  [the longest x1 3.21 us: on_device(): from_above = lax.ppermute(down, ('z', 'core'), ring_down)]
  transfers between devices with their start and end apart: 3 -> 4, of which waited for: 0 -> 0; matrix products, arithmetic and copies ran while one was open for 0% -> 0% of each run, Pallas kernels for 23% -> 24%
where the time goes in v2:
time: 87.2 us; the launch traced here: 86.9 us
  Pallas kernels  48.7 us (56%)
  blocking collectives  23.9 us (27%)
  starting transfers between devices  10.5 us (12%)
  local copies, waits for them, and re-layouts  2.29 us (3%)
    all_to_all x1, blocking collectives, on_device(): lax.all_to_all(partial.reshape(chips, tiles // 2 // chips, width), ('z',...  23.9 us
    pallas_call x1, Pallas kernels, on_device(): pl.pallas_call(local_kernel, grid=(steps,), in_specs=[pl.BlockSpec((speci...  17.8 us
    pallas_call x1, Pallas kernels, on_device(): pl.pallas_call(functools.partial(update_kernel, elements=elements), grid=...  14.6 us
    pallas_call x1, Pallas kernels, on_device(): pl.pallas_call(functools.partial(send_kernel, block=block), grid=(steps,)...  10.6 us
    all_to_all x1, starting transfers between devices, on_device(): lax.all_to_all(send, 'sub', split_axis=0, concat_axis=0, tiled=True)  7.15 us
    pallas_call x2, Pallas kernels, scattered(): pl.pallas_call(functools.partial(scatter_kernel, other=other), grid=(grou...  5.73 us
    ppermute x1, starting transfers between devices, on_device(): from_above = lax.ppermute(down, ('z', 'core'), ring_down)  3.21 us
    unnamed x10, local copies, waits for them, and re-layouts  2.29 us
  transfers between devices with their start and end apart: 4, of which 0 were waited for; matrix products, arithmetic and copies ran while one was open for 0% of the time, Pallas kernels for 24%

profile of v2, /device:TPU:0, one launch (start us, length us, event | category | flops | bytes accessed | tf_op | source)
XLA Modules:
  0.0 86.9 jit_solution(7850477039421887106)
XLA Ops:
  0.6 10.6 %sends.1 = (bf16[6,160,2048]{2,1,0:T(8,128)(2,1)}, bf16[16,2,160,128]{3,2,1,0:T(8,128)(2,1)}, bf16[160,256]{1,0:T(8,128)(2,1)}, bf16[160,256]{1,0:T(8,128)(2,1)}) custom-call(f32[4,256,2048]{2,1,0:T(8,128)} %adj_ref.3, bf16[240,256]{1,0:T(8,128)(2,1)} %constant.6.clone.sel_ref, s32[4,1024]{1,0:T(4,128)} %ss_ref.1, s32[2,256]{1,0:T(2,128)} %gs_ref.1), custom_call_target="tpu_custom_call" | custom-call | flops 12000000000 | bytes 14000000 | tf_op jit(solution)/shard_map/sends/pallas_call | solution.py:233
  11.2 7.1 %all-to-all-start = ((bf16[16,2,160,128]{3,2,1,0:T(8,128)(2,1)}), bf16[16,2,160,128]{3,2,1,0:T(8,128)(2,1)S(1)}, u32[]{:S(2)}, u32[]{:S(2)}) async-start(bf16[16,2,160,128]{3,2,1,0:T(8,128)(2,1)} %get-tuple-element.13), calls=%async_computation | async-start | bytes 2621440 | tf_op jit(solution)/shard_map/all_to_all | solution.py:250
  18.4 0.0 collective-permute-start
  18.4 3.2 %collective-permute-start.1 = (bf16[160,256]{1,0:T(8,128)(2,1)}, bf16[160,256]{1,0:T(8,128)(2,1)S(1)}, u32[]{:S(2)}, u32[]{:S(2)}) collective-permute-start(bf16[160,256]{1,0:T(8,128)(2,1)} %get-tuple-element.15), channel_id=1, source_target_pairs={{0,112},{16,0},{32,16},{48,32},{64,48},{80,64},{96,80},{112,96},{1... | collective-permute-start | bytes 245768 | tf_op jit(solution)/shard_map/ppermute | solution.py:254
  21.6 17.8 %local.1 = (f32[4,256,2048]{2,1,0:T(8,128)}, f32[6,160,2048]{2,1,0:T(8,128)}, s32[1,2048]{1,0:T(1,128)}) custom-call(f32[4,256,2048]{2,1,0:T(8,128)} %adj_ref.3, bf16[3,256,2048]{2,1,0:T(8,128)(2,1)} %vel_ref.1, bf16[768,256]{1,0:T(8,128)(2,1)} %der_ref.1, s32[6,2048]{1,0:T(8,128)} %nbr_ref.3, bf16[6,160,2048]{2,1,0:T(8,128)(2,1)} %get-tuple-element.11.pool_hbm, ...), custom_call_target="tpu_custom_call" | custom-call | flops 16000000000 | bytes 32000000 | tf_op jit(solution)/shard_map/local/pallas_call | solution.py:256
  39.4 0.0 collective-permute-done.below_ref
  39.4 0.0 copy-start.3
  39.4 0.0 collective-permute-done.1.above_ref
  39.4 0.0 copy-start.4
  39.4 0.0 all-to-all-done.recv_ref
  39.4 0.0 copy-start.2
  39.5 0.6 copy-done.3
  40.0 0.0 copy-done.4
  40.1 0.5 copy-done.2
  40.5 0.0 copy-start.1
  40.5 14.6 %update.1 = (f32[4,256,2048]{2,1,0:T(8,128)}, bf16[2048,256]{1,0:T(8,128)(2,1)}) custom-call(s32[6,2048]{1,0:T(8,128)} %nbr_ref.3, f32[6,160,2048]{2,1,0:T(8,128)} %get-tuple-element.12.gap_ref, bf16[16,2,160,128]{3,2,1,0:T(8,128)(2,1)} %copy-done.2, bf16[160,256]{1,0:T(8,128)(2,1)} %copy-done.3, bf16[160,256]{1,0:T(8,128)(2,1)} %copy-done.4, ...), custom_call_target="tpu_custom_call" | custom-call | flops 8000000000 | bytes 28000000 | tf_op jit(solution)/shard_map/update/pallas_call | solution.py:286
  55.1 0.0 copy-done.1
  55.1 0.0 copy-start
  55.1 1.2 %copy-done = bf16[2048,256]{1,0:T(8,128)(2,1)S(1)} copy-done((bf16[2048,256]{1,0:T(8,128)(2,1)S(1)}, bf16[2048,256]{1,0:T(8,128)(2,1)}, u32[]{:S(2)}) %copy-start) | copy-done | bytes 1048600
  56.3 2.9 %scatter_other.1 = f32[2048,128]{1,0:T(8,128)S(1)} custom-call(s32[1,2048]{1,0:T(1,128)S(1)} %copy-done.1, bf16[2048,256]{1,0:T(8,128)(2,1)S(1)} %copy-done), custom_call_target="tpu_custom_call" | custom-call | flops 2100000000 | bytes 2000000 | tf_op jit(solution)/shard_map/scatter_other/pallas_call | solution.py:318
  59.2 0.1 collective-permute-start.2
  59.3 2.9 %scatter_own.1 = f32[2048,128]{1,0:T(8,128)S(1)} custom-call(s32[1,2048]{1,0:T(1,128)S(1)} %copy-done.1, bf16[2048,256]{1,0:T(8,128)(2,1)S(1)} %copy-done), custom_call_target="tpu_custom_call" | custom-call | flops 2100000000 | bytes 2000000 | tf_op jit(solution)/shard_map/scatter_own/pallas_call | solution.py:318
  62.2 0.0 collective-permute-done.2
  62.2 0.1 add_convert_fusion
  62.3 23.9 %all_to_all.10 = bf16[64,32,128]{2,1,0:T(8,128)(2,1)S(1)} all-to-all(bf16[64,32,128]{2,1,0:T(8,128)(2,1)S(1)} %bitcast.5), channel_id=1, replica_groups=mesh['z'=4,'core'=2,'sub'=16] {'z','sub'}, dimensions={0} | all-to-all | bytes 1048576 | tf_op jit(solution)/shard_map/all_to_all | solution.py:332
  86.2 0.7 convert_reduce_fusion
Async XLA Ops:
  11.2 28.2 %all-to-all-start = ((bf16[16,2,160,128]{3,2,1,0:T(8,128)(2,1)}), bf16[16,2,160,128]{3,2,1,0:T(8,128)(2,1)S(1)}, u32[]{:S(2)}, u32[]{:S(2)}) async-start(bf16[16,2,160,128]{3,2,1,0:T(8,128)(2,1)} %get-tuple-element.13), calls=%async_computation | async-start | bytes 2621440 | tf_op jit(solution)/shard_map/all_to_all | solution.py:250
  18.4 21.0 %collective-permute-start = (bf16[160,256]{1,0:T(8,128)(2,1)}, bf16[160,256]{1,0:T(8,128)(2,1)S(1)}, u32[]{:S(2)}, u32[]{:S(2)}) collective-permute-start(bf16[160,256]{1,0:T(8,128)(2,1)} %get-tuple-element.14), channel_id=1, source_target_pairs={{0,16},{16,32},{32,48},{48,64},{64,80},{80,96},{96,112},{112,0},{1... | collective-permute-start | bytes 245768 | tf_op jit(solution)/shard_map/ppermute | solution.py:253
  18.4 21.0 %collective-permute-start.1 = (bf16[160,256]{1,0:T(8,128)(2,1)}, bf16[160,256]{1,0:T(8,128)(2,1)S(1)}, u32[]{:S(2)}, u32[]{:S(2)}) collective-permute-start(bf16[160,256]{1,0:T(8,128)(2,1)} %get-tuple-element.15), channel_id=1, source_target_pairs={{0,112},{16,0},{32,16},{48,32},{64,48},{80,64},{96,80},{112,96},{1... | collective-permute-start | bytes 245768 | tf_op jit(solution)/shard_map/ppermute | solution.py:254
  39.4 0.6 copy-start.3
  39.4 0.6 copy-start.4
  39.4 1.1 %copy-start.2 = (bf16[16,2,160,128]{3,2,1,0:T(8,128)(2,1)}, bf16[16,2,160,128]{3,2,1,0:T(8,128)(2,1)S(1)}, u32[]{:S(2)}) copy-start(bf16[16,2,160,128]{3,2,1,0:T(8,128)(2,1)S(1)} %all-to-all-done.recv_ref) | copy-start | bytes 3932164
  40.5 14.6 %copy-start.1 = (s32[1,2048]{1,0:T(1,128)S(1)}, s32[1,2048]{1,0:T(1,128)}, u32[]{:S(2)}) copy-start(s32[1,2048]{1,0:T(1,128)} %get-tuple-element.18.row_ref) | copy-start | bytes 24580
  55.1 1.2 %copy-start = (bf16[2048,256]{1,0:T(8,128)(2,1)S(1)}, bf16[2048,256]{1,0:T(8,128)(2,1)}, u32[]{:S(2)}) copy-start(bf16[2048,256]{1,0:T(8,128)(2,1)} %get-tuple-element.19.contrib_ref) | copy-start | bytes 3145732
  59.2 3.0 %collective-permute-start.2 = (f32[2048,128]{1,0:T(8,128)S(1)}, f32[2048,128]{1,0:T(8,128)S(1)}, u32[]{:S(2)}, u32[]{:S(2)}) collective-permute-start(f32[2048,128]{1,0:T(8,128)S(1)} %scatter_other.1), channel_id=1, source_target_pairs={{0,16},{16,0},{1,17},{17,1},{2,18},{18,2},{3,19},{19,3},{4,20},{20... | collective-permute-start | bytes 3145736 | tf_op jit(solution)/shard_map/ppermute | solution.py:329

commit v3 on v2

--- a/solution.py
+++ b/solution.py
@@ -11,7 +11,9 @@
 ORDER = 5
 SECTION = 0.125
 MIB = 1024 * 1024
-PAD = 40
+UPDATE_MIB = 56
+MAIN = 32
+REST = 4
 F32, BF16, I16, I32 = jnp.float32, jnp.bfloat16, jnp.int16, jnp.int32
 
 
@@ -34,21 +36,40 @@
     return np.stack(face_rows).astype(np.int32)
 
 
-def node_selector(nodes):
+def picker(columns, lines):
+    out = np.zeros((len(lines), columns), np.float32)
+    for row, column in enumerate(lines):
+        if column is not None:
+            out[row, column] = 1.0
+    return jnp.asarray(out, BF16)
+
+
+def main_picker(faces, first, last):
     table = face_table(ORDER)
-    out = np.zeros((6 * PAD, nodes), np.float32)
-    for f in range(6):
-        for k in range(table.shape[1]):
-            out[f * PAD + k, table[f, k]] = 1.0
-    return out
-
-
-def row_spreader(face_nodes):
-    out = np.zeros((6 * PAD, 6 * face_nodes), np.float32)
-    for f in range(6):
-        for k in range(face_nodes):
-            out[f * PAD + k, f * face_nodes + k] = 1.0
-    return out
+    return picker(last - first, [table[f, k] - first for f in faces for k in range(MAIN)])
+
+
+def rest_picker(species, faces, first, last):
+    table = face_table(ORDER)
+    return jnp.stack([
+        picker(last - first, [
+            table[f, MAIN + j] - first if t == s else None
+            for f in faces for t in range(species) for j in range(REST)
+        ])
+        for s in range(species)
+    ])
+
+
+def speed_picker(species, face_nodes):
+    lines = [f * face_nodes + k for f in range(6) for k in range(MAIN)]
+    lines += [f * face_nodes + MAIN + j for f in range(6) for _ in range(species) for j in range(REST)]
+    return picker(6 * face_nodes, lines)
+
+
+def lift_picker(face_nodes):
+    lines = [f * face_nodes + k for f in range(6) for k in range(MAIN)]
+    lines += [f * face_nodes + MAIN + j for f in range(6) for j in range(REST)]
+    return picker(6 * face_nodes, lines)
 
 
 def one_hot(count, positions):
@@ -60,31 +81,56 @@
     return jnp.dot(a, b, preferred_element_type=F32)
 
 
-def send_kernel(adj_ref, sel_ref, ss_ref, gs_ref, pool_ref, send_ref, up_ref, down_ref, *, block):
-    step = pl.program_id(0)
-    cols = pl.ds(pl.multiple_of(step * block, block), block)
-    for pair in range(2):
-        picked = [dot(sel_ref[...], adj_ref[s].astype(BF16)) for s in (2 * pair, 2 * pair + 1)]
-        for f in range(6):
-            rows = slice(f * PAD, (f + 1) * PAD)
-            both = jnp.concatenate([picked[0][rows], picked[1][rows]], axis=0).astype(BF16)
-            pool_ref[f, 2 * PAD * pair : 2 * PAD * (pair + 1), cols] = both
-
-    @pl.when(step == pl.num_programs(0) - 1)
-    def _():
-        elements = pool_ref.shape[2]
-        half = send_ref.shape[3] // 2
-        low = lax.broadcasted_iota(I32, (4 * PAD, 2 * half), 1) < half
-        for q in range(2):
-            a = dot(pool_ref[2 * q], one_hot(elements, ss_ref[2 * q : 2 * q + 1, :]))
-            b = dot(pool_ref[2 * q + 1], one_hot(elements, ss_ref[2 * q + 1 : 2 * q + 2, :]))
-            for i in range(send_ref.shape[0] // 2):
-                lanes = slice(2 * half * i, 2 * half * (i + 1))
-                ai, bi = a[:, lanes], b[:, lanes]
-                send_ref[2 * i, q] = jnp.where(low, ai, pltpu.roll(bi, half, 1)).astype(BF16)
-                send_ref[2 * i + 1, q] = jnp.where(low, pltpu.roll(ai, half, 1), bi).astype(BF16)
-        down_ref[...] = dot(pool_ref[4], one_hot(elements, gs_ref[0:1, :])).astype(BF16)
-        up_ref[...] = dot(pool_ref[5], one_hot(elements, gs_ref[1:2, :])).astype(BF16)
+LOW, MID, HIGH = (0, 40), (40, 176), (176, 216)
+
+
+def send_kernel(
+    adj_hbm, main_ref, rest_ref, far_main_ref, far_rest_ref, ss_ref, gs_ref,
+    pool_ref, send_ref, up_ref, down_ref, adj, sems,
+):
+    species = adj.shape[0]
+    rows, elements = pool_ref.shape[1:]
+    half = send_ref.shape[3] // 2
+    copies = [
+        pltpu.make_async_copy(adj_hbm.at[:, a:b, :], adj.at[:, a:b, :], sems.at[i])
+        for i, (a, b) in enumerate((LOW, HIGH, MID))
+    ]
+    for copy in copies:
+        copy.start()
+    low = lax.broadcasted_iota(I32, (rows, 2 * half), 1) < half
+
+    def exchange(q):
+        a = dot(pool_ref[2 * q], one_hot(elements, ss_ref[2 * q : 2 * q + 1, :]))
+        b = dot(pool_ref[2 * q + 1], one_hot(elements, ss_ref[2 * q + 1 : 2 * q + 2, :]))
+        for i in range(send_ref.shape[0] // 2):
+            lanes = slice(2 * half * i, 2 * half * (i + 1))
+            ai, bi = a[:, lanes], b[:, lanes]
+            send_ref[2 * i, q] = jnp.where(low, ai, pltpu.roll(bi, half, 1)).astype(BF16)
+            send_ref[2 * i + 1, q] = jnp.where(low, pltpu.roll(ai, half, 1), bi).astype(BF16)
+
+    copies[0].wait()
+    copies[1].wait()
+    chunk = 1024
+    for f, (first, last) in enumerate((LOW, HIGH)):
+        for c in range(0, elements, chunk):
+            parts = [adj[s, first:last, c : c + chunk].astype(BF16) for s in range(species)]
+            rest = sum(dot(rest_ref[f, s], parts[s]) for s in range(species))
+            mains = [dot(main_ref[f], parts[s]) for s in range(species)]
+            pool_ref[f, :, c : c + chunk] = jnp.concatenate(mains + [rest], axis=0).astype(BF16)
+    exchange(0)
+    copies[2].wait()
+    chunk = 512
+    for c in range(0, elements, chunk):
+        parts = [adj[s, :, c : c + chunk].astype(BF16) for s in range(species)]
+        rest = sum(dot(far_rest_ref[s], parts[s]) for s in range(species))
+        mains = [dot(far_main_ref[...], parts[s]) for s in range(species)]
+        for i in range(4):
+            pieces = [m[MAIN * i : MAIN * (i + 1)] for m in mains]
+            pieces.append(rest[species * REST * i : species * REST * (i + 1)])
+            pool_ref[2 + i, :, c : c + chunk] = jnp.concatenate(pieces, axis=0).astype(BF16)
+    exchange(1)
+    down_ref[...] = dot(pool_ref[4], one_hot(elements, gs_ref[0:1, :])).astype(BF16)
+    up_ref[...] = dot(pool_ref[5], one_hot(elements, gs_ref[1:2, :])).astype(BF16)
 
 
 def local_kernel(
@@ -138,17 +184,25 @@
 
 
 def update_kernel(
-    nbr_ref, gap_ref, recv_ref, below_ref, above_ref, fs_ref, spread_ref, lift_ref, prof_ref, base_ref,
-    next_ref, contrib_ref, rpool, lift_pad, flux, *, elements,
+    nbr_ref, gap_ref, recv_ref, below_ref, above_ref, fs_ref, speed_ref, order_ref, lift_ref, prof_ref, base_ref,
+    next_ref, contrib_ref, rpool, lift_sorted, flux, low_next, *, elements,
 ):
     step = pl.program_id(0)
-    peers, _, _, width = recv_ref.shape
+    peers, _, rows, width = recv_ref.shape
     half = width // 2
-    species = base_ref.shape[0]
+    species, nodes, block = base_ref.shape
+
+    def contribute(index):
+        terms = [dot(prof_ref[...], low_next[s]) for s in range(species)]
+        contrib = jnp.transpose(jnp.concatenate(terms, axis=0))
+        high = contrib.astype(BF16)
+        lines = pl.ds(pl.multiple_of(index * block, block), block)
+        contrib_ref[lines, : contrib.shape[1]] = high
+        contrib_ref[lines, contrib.shape[1] :] = (contrib - high.astype(F32)).astype(BF16)
 
     @pl.when(step == 0)
     def _():
-        low = lax.broadcasted_iota(I32, (4 * PAD, width), 1) < half
+        low = lax.broadcasted_iota(I32, (rows, width), 1) < half
         for q in range(2):
             for i in range(peers // 2):
                 lanes = slice(width * i, width * (i + 1))
@@ -156,36 +210,47 @@
                 y = recv_ref[2 * i + 1, q].astype(F32)
                 rpool[2 * q, :, lanes] = jnp.where(low, x, pltpu.roll(y, half, 1)).astype(BF16)
                 rpool[2 * q + 1, :, lanes] = jnp.where(low, pltpu.roll(x, half, 1), y).astype(BF16)
-        lift_pad[...] = (SECTION * jnp.transpose(dot(spread_ref[...], lift_ref[...]))).astype(BF16)
-
-    upwind = dot(spread_ref[...], jnp.maximum(fs_ref[...], jnp.zeros((), BF16)))
+        lift_sorted[...] = (SECTION * jnp.transpose(dot(order_ref[...], lift_ref[...]))).astype(BF16)
+        low_next[...] = jnp.zeros_like(low_next)
+
+    contribute(jnp.maximum(step - 1, 0))
+    upwind = dot(speed_ref[...], jnp.maximum(fs_ref[...], jnp.zeros((), BF16)))
     slots = peers * half
+    first = lax.broadcasted_iota(I32, (2 * REST, block), 0) < REST
+    tails = [[] for _ in range(species)]
     for q in range(3):
-        parts = []
+        mains, rests = [], []
         for f in (2 * q, 2 * q + 1):
             t = f ^ 1
             if t < 4:
-                hot = one_hot(slots, nbr_ref[f : f + 1, :] - elements)
-                far = dot(rpool[t], hot)
+                far = dot(rpool[t], one_hot(slots, nbr_ref[f : f + 1, :] - elements))
             else:
                 source = below_ref if t == 5 else above_ref
                 hot = one_hot(source.shape[1], nbr_ref[f : f + 1, :] - (elements + slots))
                 far = dot(source[...], hot)
             gap = gap_ref[f] + far
-            up = upwind[f * PAD : (f + 1) * PAD]
-            parts.append([up * gap[s * PAD : (s + 1) * PAD] for s in range(species)])
+            speed = upwind[MAIN * f : MAIN * (f + 1)]
+            mains.append([speed * gap[MAIN * s : MAIN * (s + 1)] for s in range(species)])
+            line = 6 * MAIN + species * REST * f
+            rests.append(upwind[line : line + species * REST] * gap[species * MAIN :])
         for s in range(species):
-            both = jnp.concatenate([parts[0][s], parts[1][s]], axis=0).astype(BF16)
-            flux[s, 2 * PAD * q : 2 * PAD * (q + 1), :] = both
-    terms = []
+            both = jnp.concatenate([mains[0][s], mains[1][s]], axis=0).astype(BF16)
+            flux[s, 2 * MAIN * q : 2 * MAIN * (q + 1), :] = both
+        for v in range(species // 2):
+            a = rests[0][2 * REST * v : 2 * REST * (v + 1)]
+            b = rests[1][2 * REST * v : 2 * REST * (v + 1)]
+            tails[2 * v].append(jnp.where(first, a, pltpu.roll(b, REST, 0)))
+            tails[2 * v + 1].append(jnp.where(first, pltpu.roll(a, REST, 0), b))
     for s in range(species):
-        value = base_ref[s] + dot(lift_pad[...], flux[s])
+        flux[s, 6 * MAIN :, :] = jnp.concatenate(tails[s], axis=0).astype(BF16)
+    for s in range(species):
+        value = base_ref[s] + dot(lift_sorted[...], flux[s])
         next_ref[s] = value
-        terms.append(dot(prof_ref[...], value.astype(BF16)))
-    contrib = jnp.transpose(jnp.concatenate(terms, axis=0))
-    high = contrib.astype(BF16)
-    contrib_ref[:, : contrib.shape[1]] = high
-    contrib_ref[:, contrib.shape[1] :] = (contrib - high.astype(F32)).astype(BF16)
+        low_next[s] = value.astype(BF16)
+
+    @pl.when(step == pl.num_programs(0) - 1)
+    def _():
+        contribute(step)
 
 
 def scatter_kernel(row_ref, contrib_ref, out_ref, *, other):
@@ -223,29 +288,32 @@
     tiles = tile_slot.shape[0]
     heights = emission_profile.shape[1]
     face_rows = face_speed.shape[0]
-    sel = jnp.asarray(node_selector(nodes), BF16)
-    spread = jnp.asarray(row_spreader(face_rows // 6), BF16)
-    rows = species * PAD
+    rows = species * (MAIN + REST)
     sds = jax.ShapeDtypeStruct
     block = 512
     steps = elements // block
 
+    near = [((f,),) + span for f, span in enumerate((LOW, HIGH))]
+    near_main = jnp.stack([main_picker(*where) for where in near])
+    near_rest = jnp.stack([rest_picker(species, *where) for where in near])
+    far_faces = ((2, 3, 4, 5), 0, HIGH[1])
+    vmem = pl.BlockSpec(memory_space=pltpu.VMEM)
     pool, send, up, down = pl.pallas_call(
-        functools.partial(send_kernel, block=block),
-        grid=(steps,),
-        in_specs=[
-            pl.BlockSpec((species, nodes, block), lambda i: (0, 0, i)),
-            whole(6 * PAD, nodes), whole(4, slots), whole(2, vcap),
-        ],
-        out_specs=[whole(6, rows, elements), whole(peers, 2, rows, 2 * half), whole(rows, vcap), whole(rows, vcap)],
+        send_kernel,
+        in_specs=[pl.BlockSpec(memory_space=pl.ANY)] + [vmem] * 6,
+        out_specs=[vmem] * 4,
         out_shape=[
             sds((6, rows, elements), BF16), sds((peers, 2, rows, 2 * half), BF16),
             sds((rows, vcap), BF16), sds((rows, vcap), BF16),
         ],
+        scratch_shapes=[pltpu.VMEM((species, HIGH[1], elements), F32), pltpu.SemaphoreType.DMA((3,))],
         compiler_params=params(60),
         cost_estimate=cost(12_000_000_000, 14_000_000),
         name="sends",
-    )(adjoint, sel, sub_sends, group_sends)
+    )(
+        adjoint, near_main, near_rest, main_picker(*far_faces), rest_picker(species, *far_faces),
+        sub_sends, group_sends,
+    )
 
     received = lax.all_to_all(send, "sub", split_axis=0, concat_axis=0, tiled=True)
     ring_up = [(g, (g + 1) % groups) for g in range(groups)]
@@ -283,6 +351,7 @@
         tile_slot.reshape(tiles // 128, 128),
     )
 
+    face_nodes = face_rows // 6
     adjoint_next, contrib = pl.pallas_call(
         functools.partial(update_kernel, elements=elements),
         grid=(steps,),
@@ -291,24 +360,24 @@
             pl.BlockSpec((6, rows, block), lambda i: (0, 0, i)),
             whole(peers, 2, rows, 2 * half), whole(rows, vcap), whole(rows, vcap),
             pl.BlockSpec((face_rows, block), lambda i: (0, i)),
-            whole(6 * PAD, face_rows), whole(face_rows, nodes), whole(heights, nodes),
+            whole(2 * rows, face_rows), whole(face_rows, face_rows), whole(face_rows, nodes), whole(heights, nodes),
             pl.BlockSpec((species, nodes, block), lambda i: (0, 0, i)),
         ],
         out_specs=[
             pl.BlockSpec((species, nodes, block), lambda i: (0, 0, i)),
-            pl.BlockSpec((block, 2 * species * heights), lambda i: (i, 0)),
+            whole(elements, 2 * species * heights),
         ],
         out_shape=[sds((species, nodes, elements), F32), sds((elements, 2 * species * heights), BF16)],
         scratch_shapes=[
-            pltpu.VMEM((4, rows, slots), BF16), pltpu.VMEM((nodes, 6 * PAD), BF16),
-            pltpu.VMEM((species, 6 * PAD, block), BF16),
-        ],
-        compiler_params=params(56),
+            pltpu.VMEM((4, rows, slots), BF16), pltpu.VMEM((nodes, face_rows), BF16),
+            pltpu.VMEM((species, face_rows, block), BF16), pltpu.VMEM((species, nodes, block), BF16),
+        ],
+        compiler_params=params(UPDATE_MIB),
         cost_estimate=cost(8_000_000_000, 28_000_000),
         name="update",
     )(
-        neighbours, gap, received, from_below, from_above, face_speed, spread,
-        lift_operator.T, emission_profile.T, base,
+        neighbours, gap, received, from_below, from_above, face_speed, speed_picker(species, face_nodes),
+        lift_picker(face_nodes), lift_operator.T, emission_profile.T, base,
     )
 
     width = species * heights

time: 87.2 us -> 83.8 us (0.961)
  Pallas kernels: 48.7 us -> 45.3 us
    pallas_call x1, Pallas kernels: 10.6 us -> 8.43 us  [on_device(): pl.pallas_call(send_kernel, in_specs=[pl.BlockSpec(memory_space=pl.ANY)]...]
    pallas_call x1, Pallas kernels: 17.8 us -> 16.9 us  [on_device(): pl.pallas_call(local_kernel, grid=(steps,), in_specs=[pl.BlockSpec((speci...]
where the time goes in v3:
time: 83.8 us; the launch traced here: 83.5 us
  Pallas kernels  45.3 us (54%)
  blocking collectives  23.9 us (29%)
  starting transfers between devices  10.5 us (13%)
  local copies, waits for them, and re-layouts  2.26 us (3%)
    all_to_all x1, blocking collectives, on_device(): lax.all_to_all(partial.reshape(chips, tiles // 2 // chips, width), ('z',...  23.9 us
    pallas_call x1, Pallas kernels, on_device(): pl.pallas_call(local_kernel, grid=(steps,), in_specs=[pl.BlockSpec((speci...  16.9 us
    pallas_call x1, Pallas kernels, on_device(): pl.pallas_call(functools.partial(update_kernel, elements=elements), grid=...  14.2 us
    pallas_call x1, Pallas kernels, on_device(): pl.pallas_call(send_kernel, in_specs=[pl.BlockSpec(memory_space=pl.ANY)]...  8.43 us
    all_to_all x1, starting transfers between devices, on_device(): lax.all_to_all(send, 'sub', split_axis=0, concat_axis=0, tiled=True)  7.16 us
    pallas_call x2, Pallas kernels, scattered(): pl.pallas_call(functools.partial(scatter_kernel, other=other), grid=(grou...  5.73 us
    ppermute x1, starting transfers between devices, on_device(): from_above = lax.ppermute(down, ('z', 'core'), ring_down)  3.21 us
    unnamed x10, local copies, waits for them, and re-layouts  2.26 us
  transfers between devices with their start and end apart: 4, of which 0 were waited for; matrix products, arithmetic and copies ran while one was open for 0% of the time, Pallas kernels for 24%

profile of v3, /device:TPU:0, one launch (start us, length us, event | category | flops | bytes accessed | tf_op | source)
XLA Modules:
  0.0 83.5 jit_solution(14598857571627519357)
XLA Ops:
  0.6 8.4 %sends.1 = (bf16[6,144,2048]{2,1,0:T(8,128)(2,1)}, bf16[16,2,144,128]{3,2,1,0:T(8,128)(2,1)}, bf16[144,256]{1,0:T(8,128)(2,1)}, bf16[144,256]{1,0:T(8,128)(2,1)}) custom-call(f32[4,256,2048]{2,1,0:T(8,128)} %adj_ref.1, bf16[2,32,40]{2,1,0:T(8,128)(2,1)} %constant.55.main_ref, bf16[2,4,16,40]{3,2,1,0:T(8,128)(2,1)} %constant.68.rest_ref, ...), custom_call_target="tpu_custom_call" | custom-call | flops 12000000000 | bytes 14000000 | tf_op jit(solution)/shard_map/sends/pallas_call | solution.py:301
  9.1 7.2 %all-to-all-start = ((bf16[16,2,144,128]{3,2,1,0:T(8,128)(2,1)}), bf16[16,2,144,128]{3,2,1,0:T(8,128)(2,1)S(1)}, u32[]{:S(2)}, u32[]{:S(2)}) async-start(bf16[16,2,144,128]{3,2,1,0:T(8,128)(2,1)} %get-tuple-element.13), calls=%async_computation | async-start | bytes 2359296 | tf_op jit(solution)/shard_map/all_to_all | solution.py:318
  16.2 0.0 collective-permute-start
  16.3 3.2 %collective-permute-start.1 = (bf16[144,256]{1,0:T(8,128)(2,1)}, bf16[144,256]{1,0:T(8,128)(2,1)S(1)}, u32[]{:S(2)}, u32[]{:S(2)}) collective-permute-start(bf16[144,256]{1,0:T(8,128)(2,1)} %get-tuple-element.15), channel_id=1, source_target_pairs={{0,112},{16,0},{32,16},{48,32},{64,48},{80,64},{96,80},{112,96},{1... | collective-permute-start | bytes 221192 | tf_op jit(solution)/shard_map/ppermute | solution.py:322
  19.5 16.9 %local.1 = (f32[4,256,2048]{2,1,0:T(8,128)}, f32[6,144,2048]{2,1,0:T(8,128)}, s32[1,2048]{1,0:T(1,128)}) custom-call(f32[4,256,2048]{2,1,0:T(8,128)} %adj_ref.1, bf16[3,256,2048]{2,1,0:T(8,128)(2,1)} %vel_ref.1, bf16[768,256]{1,0:T(8,128)(2,1)} %der_ref.1, s32[6,2048]{1,0:T(8,128)} %nbr_ref.3, bf16[6,144,2048]{2,1,0:T(8,128)(2,1)} %get-tuple-element.11.pool_hbm, ...), custom_call_target="tpu_custom_call" | custom-call | flops 16000000000 | bytes 32000000 | tf_op jit(solution)/shard_map/local/pallas_call | solution.py:324
  36.4 0.0 collective-permute-done.below_ref
  36.4 0.0 copy-start.3
  36.4 0.0 collective-permute-done.1.above_ref
  36.4 0.0 copy-start.4
  36.4 0.0 all-to-all-done.recv_ref
  36.4 0.0 copy-start.2
  36.4 0.6 copy-done.3
  37.0 0.1 copy-done.4
  37.1 0.4 copy-done.2
  37.5 0.0 copy-start.1
  37.5 14.2 %update.1 = (f32[4,256,2048]{2,1,0:T(8,128)}, bf16[2048,256]{1,0:T(8,128)(2,1)}) custom-call(s32[6,2048]{1,0:T(8,128)} %nbr_ref.3, f32[6,144,2048]{2,1,0:T(8,128)} %get-tuple-element.12.gap_ref, bf16[16,2,144,128]{3,2,1,0:T(8,128)(2,1)} %copy-done.2, bf16[144,256]{1,0:T(8,128)(2,1)} %copy-done.3, bf16[144,256]{1,0:T(8,128)(2,1)} %copy-done.4, ...), custom_call_target="tpu_custom_call" | custom-call | flops 8000000000 | bytes 28000000 | tf_op jit(solution)/shard_map/update/pallas_call | solution.py:355
  51.7 0.0 copy-done.1
  51.7 0.0 copy-start
  51.7 1.2 %copy-done = bf16[2048,256]{1,0:T(8,128)(2,1)S(1)} copy-done((bf16[2048,256]{1,0:T(8,128)(2,1)S(1)}, bf16[2048,256]{1,0:T(8,128)(2,1)}, u32[]{:S(2)}) %copy-start) | copy-done | bytes 1048600
  53.0 2.9 %scatter_other.1 = f32[2048,128]{1,0:T(8,128)S(1)} custom-call(s32[1,2048]{1,0:T(1,128)S(1)} %copy-done.1, bf16[2048,256]{1,0:T(8,128)(2,1)S(1)} %copy-done), custom_call_target="tpu_custom_call" | custom-call | flops 2100000000 | bytes 2000000 | tf_op jit(solution)/shard_map/scatter_other/pallas_call | solution.py:387
  55.8 0.1 collective-permute-start.2
  55.9 2.9 %scatter_own.1 = f32[2048,128]{1,0:T(8,128)S(1)} custom-call(s32[1,2048]{1,0:T(1,128)S(1)} %copy-done.1, bf16[2048,256]{1,0:T(8,128)(2,1)S(1)} %copy-done), custom_call_target="tpu_custom_call" | custom-call | flops 2100000000 | bytes 2000000 | tf_op jit(solution)/shard_map/scatter_own/pallas_call | solution.py:387
  58.8 0.0 collective-permute-done.2
  58.8 0.1 add_convert_fusion
  58.9 23.9 %all_to_all.10 = bf16[64,32,128]{2,1,0:T(8,128)(2,1)S(1)} all-to-all(bf16[64,32,128]{2,1,0:T(8,128)(2,1)S(1)} %bitcast.5), channel_id=1, replica_groups=mesh['z'=4,'core'=2,'sub'=16] {'z','sub'}, dimensions={0} | all-to-all | bytes 1048576 | tf_op jit(solution)/shard_map/all_to_all | solution.py:401
  82.8 0.7 convert_reduce_fusion
Async XLA Ops:
  9.1 27.3 %all-to-all-start = ((bf16[16,2,144,128]{3,2,1,0:T(8,128)(2,1)}), bf16[16,2,144,128]{3,2,1,0:T(8,128)(2,1)S(1)}, u32[]{:S(2)}, u32[]{:S(2)}) async-start(bf16[16,2,144,128]{3,2,1,0:T(8,128)(2,1)} %get-tuple-element.13), calls=%async_computation | async-start | bytes 2359296 | tf_op jit(solution)/shard_map/all_to_all | solution.py:318
  16.2 20.1 %collective-permute-start = (bf16[144,256]{1,0:T(8,128)(2,1)}, bf16[144,256]{1,0:T(8,128)(2,1)S(1)}, u32[]{:S(2)}, u32[]{:S(2)}) collective-permute-start(bf16[144,256]{1,0:T(8,128)(2,1)} %get-tuple-element.14), channel_id=1, source_target_pairs={{0,16},{16,32},{32,48},{48,64},{64,80},{80,96},{96,112},{112,0},{1... | collective-permute-start | bytes 221192 | tf_op jit(solution)/shard_map/ppermute | solution.py:321
  16.3 20.1 %collective-permute-start.1 = (bf16[144,256]{1,0:T(8,128)(2,1)}, bf16[144,256]{1,0:T(8,128)(2,1)S(1)}, u32[]{:S(2)}, u32[]{:S(2)}) collective-permute-start(bf16[144,256]{1,0:T(8,128)(2,1)} %get-tuple-element.15), channel_id=1, source_target_pairs={{0,112},{16,0},{32,16},{48,32},{64,48},{80,64},{96,80},{112,96},{1... | collective-permute-start | bytes 221192 | tf_op jit(solution)/shard_map/ppermute | solution.py:322
  36.4 0.6 copy-start.3
  36.4 0.6 copy-start.4
  36.4 1.0 %copy-start.2 = (bf16[16,2,144,128]{3,2,1,0:T(8,128)(2,1)}, bf16[16,2,144,128]{3,2,1,0:T(8,128)(2,1)S(1)}, u32[]{:S(2)}) copy-start(bf16[16,2,144,128]{3,2,1,0:T(8,128)(2,1)S(1)} %all-to-all-done.recv_ref) | copy-start | bytes 3538948
  37.5 14.2 %copy-start.1 = (s32[1,2048]{1,0:T(1,128)S(1)}, s32[1,2048]{1,0:T(1,128)}, u32[]{:S(2)}) copy-start(s32[1,2048]{1,0:T(1,128)} %get-tuple-element.18.row_ref) | copy-start | bytes 24580
  51.7 1.2 %copy-start = (bf16[2048,256]{1,0:T(8,128)(2,1)S(1)}, bf16[2048,256]{1,0:T(8,128)(2,1)}, u32[]{:S(2)}) copy-start(bf16[2048,256]{1,0:T(8,128)(2,1)} %get-tuple-element.19.contrib_ref) | copy-start | bytes 3145732
  55.8 3.0 %collective-permute-start.2 = (f32[2048,128]{1,0:T(8,128)S(1)}, f32[2048,128]{1,0:T(8,128)S(1)}, u32[]{:S(2)}, u32[]{:S(2)}) collective-permute-start(f32[2048,128]{1,0:T(8,128)S(1)} %scatter_other.1), channel_id=1, source_target_pairs={{0,16},{16,0},{1,17},{17,1},{2,18},{18,2},{3,19},{19,3},{4,20},{20... | collective-permute-start | bytes 3145736 | tf_op jit(solution)/shard_map/ppermute | solution.py:398

commit v4 on v3

--- a/solution.py
+++ b/solution.py
@@ -11,9 +11,10 @@
 ORDER = 5
 SECTION = 0.125
 MIB = 1024 * 1024
-UPDATE_MIB = 56
+UPDATE_MIB = 46
 MAIN = 32
 REST = 4
+GROUP_ROWS = 512
 F32, BF16, I16, I32 = jnp.float32, jnp.bfloat16, jnp.int16, jnp.int32
 
 
@@ -44,15 +45,10 @@
     return jnp.asarray(out, BF16)
 
 
-def main_picker(faces, first, last):
-    table = face_table(ORDER)
-    return picker(last - first, [table[f, k] - first for f in faces for k in range(MAIN)])
-
-
-def rest_picker(species, faces, first, last):
+def trace_picker(species, faces, first, last):
     table = face_table(ORDER)
     return jnp.stack([
-        picker(last - first, [
+        picker(last - first, [table[f, k] - first for f in faces for k in range(MAIN)] + [
             table[f, MAIN + j] - first if t == s else None
             for f in faces for t in range(species) for j in range(REST)
         ])
@@ -85,7 +81,7 @@
 
 
 def send_kernel(
-    adj_hbm, main_ref, rest_ref, far_main_ref, far_rest_ref, ss_ref, gs_ref,
+    adj_hbm, near_ref, far_ref, ss_ref, gs_ref,
     pool_ref, send_ref, up_ref, down_ref, adj, sems,
 ):
     species = adj.shape[0]
@@ -108,26 +104,23 @@
             send_ref[2 * i, q] = jnp.where(low, ai, pltpu.roll(bi, half, 1)).astype(BF16)
             send_ref[2 * i + 1, q] = jnp.where(low, pltpu.roll(ai, half, 1), bi).astype(BF16)
 
+    def fill(faces, picks, first, last, chunk):
+        count = len(faces)
+        shared = species * REST
+        for c in range(0, elements, chunk):
+            found = [dot(picks[s], adj[s, first:last, c : c + chunk].astype(BF16)) for s in range(species)]
+            rest = sum(x[MAIN * count :] for x in found)
+            for i, f in enumerate(faces):
+                pieces = [x[MAIN * i : MAIN * (i + 1)] for x in found] + [rest[shared * i : shared * (i + 1)]]
+                pool_ref[f, :, c : c + chunk] = jnp.concatenate(pieces, axis=0).astype(BF16)
+
     copies[0].wait()
     copies[1].wait()
-    chunk = 1024
-    for f, (first, last) in enumerate((LOW, HIGH)):
-        for c in range(0, elements, chunk):
-            parts = [adj[s, first:last, c : c + chunk].astype(BF16) for s in range(species)]
-            rest = sum(dot(rest_ref[f, s], parts[s]) for s in range(species))
-            mains = [dot(main_ref[f], parts[s]) for s in range(species)]
-            pool_ref[f, :, c : c + chunk] = jnp.concatenate(mains + [rest], axis=0).astype(BF16)
+    fill((0,), near_ref[0], *LOW, 1024)
+    fill((1,), near_ref[1], *HIGH, 1024)
     exchange(0)
     copies[2].wait()
-    chunk = 512
-    for c in range(0, elements, chunk):
-        parts = [adj[s, :, c : c + chunk].astype(BF16) for s in range(species)]
-        rest = sum(dot(far_rest_ref[s], parts[s]) for s in range(species))
-        mains = [dot(far_main_ref[...], parts[s]) for s in range(species)]
-        for i in range(4):
-            pieces = [m[MAIN * i : MAIN * (i + 1)] for m in mains]
-            pieces.append(rest[species * REST * i : species * REST * (i + 1)])
-            pool_ref[2 + i, :, c : c + chunk] = jnp.concatenate(pieces, axis=0).astype(BF16)
+    fill((2, 3, 4, 5), far_ref[...], 0, HIGH[1], 512)
     exchange(1)
     down_ref[...] = dot(pool_ref[4], one_hot(elements, gs_ref[0:1, :])).astype(BF16)
     up_ref[...] = dot(pool_ref[5], one_hot(elements, gs_ref[1:2, :])).astype(BF16)
@@ -161,18 +154,22 @@
 
     @pl.when(step == 0)
     def _():
-        high = slot_ref.shape[0]
         elements = tile_ref.shape[1]
+        high, lanes = slot_ref.shape
+        fine = lanes // 2
         slot = jnp.transpose(slot_ref[...].astype(F32))
         upper = jnp.floor(slot * (1.0 / 64.0))
-        digits = jnp.concatenate([upper, slot - 64.0 * upper], axis=0).astype(BF16)
-        lanes = slot_ref.shape[1]
+        digits = jnp.concatenate([
+            jnp.concatenate([x[:fine], x[fine:]], axis=1) for x in (upper, slot - 64.0 * upper)
+        ], axis=0).astype(BF16)
+        bits = fine.bit_length() - 1
         for c in range(0, elements, block):
             tile = tile_ref[:, c : c + block]
-            shift = lanes.bit_length() - 1
-            found = dot(digits, one_hot(high, jnp.right_shift(tile, shift)))
-            rows = 64.0 * found[:lanes] + found[lanes:]
-            within = lax.broadcasted_iota(I32, rows.shape, 0) == jnp.bitwise_and(tile, lanes - 1)
+            coarse = jnp.right_shift(tile, bits)
+            place = jnp.bitwise_and(coarse, 1) * high + jnp.right_shift(coarse, 1)
+            found = dot(digits, one_hot(2 * high, place))
+            rows = 64.0 * found[:fine] + found[fine:]
+            within = lax.broadcasted_iota(I32, rows.shape, 0) == jnp.bitwise_and(tile, fine - 1)
             row_ref[:, c : c + block] = jnp.sum(jnp.where(within, rows, 0.0), axis=0, keepdims=True).astype(I32)
         for copy in copies:
             copy.wait()
@@ -184,13 +181,21 @@
 
 
 def update_kernel(
-    nbr_ref, gap_ref, recv_ref, below_ref, above_ref, fs_ref, speed_ref, order_ref, lift_ref, prof_ref, base_ref,
-    next_ref, contrib_ref, rpool, lift_sorted, flux, low_next, *, elements,
+    nbr_ref, gap_hbm, recv_ref, below_ref, above_ref, fs_ref, speed_ref, order_ref, lift_ref, prof_ref, base_hbm, row_ref,
+    next_ref, contrib_ref, other_ref, rpool, lift_sorted, flux, low_next, gap_all, base_all, sems, *, elements,
 ):
     step = pl.program_id(0)
     peers, _, rows, width = recv_ref.shape
     half = width // 2
-    species, nodes, block = base_ref.shape
+    species, nodes, block = next_ref.shape
+    steps = gap_all.shape[0]
+
+    def loads(index):
+        cols = pl.ds(pl.multiple_of(index * block, block), block)
+        return (
+            pltpu.make_async_copy(gap_hbm.at[:, :, cols], gap_all.at[index], sems.at[0, index]),
+            pltpu.make_async_copy(base_hbm.at[:, :, cols], base_all.at[index], sems.at[1, index]),
+        )
 
     def contribute(index):
         terms = [dot(prof_ref[...], low_next[s]) for s in range(species)]
@@ -202,6 +207,9 @@
 
     @pl.when(step == 0)
     def _():
+        for index in range(steps):
+            for copy in loads(index):
+                copy.start()
         low = lax.broadcasted_iota(I32, (rows, width), 1) < half
         for q in range(2):
             for i in range(peers // 2):
@@ -213,6 +221,9 @@
         lift_sorted[...] = (SECTION * jnp.transpose(dot(order_ref[...], lift_ref[...]))).astype(BF16)
         low_next[...] = jnp.zeros_like(low_next)
 
+    for copy in loads(step):
+        copy.wait()
+    gap_ref, base_ref = gap_all.at[step], base_all.at[step]
     contribute(jnp.maximum(step - 1, 0))
     upwind = dot(speed_ref[...], jnp.maximum(fs_ref[...], jnp.zeros((), BF16)))
     slots = peers * half
@@ -248,19 +259,24 @@
         next_ref[s] = value
         low_next[s] = value.astype(BF16)
 
-    @pl.when(step == pl.num_programs(0) - 1)
+    @pl.when(step == steps - 1)
     def _():
         contribute(step)
-
-
-def scatter_kernel(row_ref, contrib_ref, out_ref, *, other):
-    block, width = out_ref.shape
+        scatter(row_ref, contrib_ref, other_ref, True)
+
+
+def scatter(row_ref, contrib_ref, out_ref, other):
+    width = out_ref.shape[1]
     core = lax.axis_index("core")
-    half = 1 - core if other else core
-    first = (2 * pl.program_id(0) + half) * block
-    hot = one_hot(block, row_ref[...] - first)
-    both = dot(hot, contrib_ref[...])
-    out_ref[...] = both[:, :width] + both[:, width:]
+    side = 1 - core if other else core
+    for i in range(out_ref.shape[0] // GROUP_ROWS):
+        hot = one_hot(GROUP_ROWS, row_ref[...] - (2 * i + side) * GROUP_ROWS)
+        both = dot(hot, contrib_ref[...])
+        out_ref[i * GROUP_ROWS : (i + 1) * GROUP_ROWS, :] = both[:, :width] + both[:, width:]
+
+
+def own_kernel(row_ref, contrib_ref, out_ref):
+    scatter(row_ref, contrib_ref, out_ref, False)
 
 
 def whole(*shape):
@@ -293,14 +309,12 @@
     block = 512
     steps = elements // block
 
-    near = [((f,),) + span for f, span in enumerate((LOW, HIGH))]
-    near_main = jnp.stack([main_picker(*where) for where in near])
-    near_rest = jnp.stack([rest_picker(species, *where) for where in near])
-    far_faces = ((2, 3, 4, 5), 0, HIGH[1])
+    near = jnp.stack([trace_picker(species, (f,), *span) for f, span in enumerate((LOW, HIGH))])
+    far = trace_picker(species, (2, 3, 4, 5), 0, HIGH[1])
     vmem = pl.BlockSpec(memory_space=pltpu.VMEM)
     pool, send, up, down = pl.pallas_call(
         send_kernel,
-        in_specs=[pl.BlockSpec(memory_space=pl.ANY)] + [vmem] * 6,
+        in_specs=[pl.BlockSpec(memory_space=pl.ANY)] + [vmem] * 4,
         out_specs=[vmem] * 4,
         out_shape=[
             sds((6, rows, elements), BF16), sds((peers, 2, rows, 2 * half), BF16),
@@ -311,8 +325,7 @@
         cost_estimate=cost(12_000_000_000, 14_000_000),
         name="sends",
     )(
-        adjoint, near_main, near_rest, main_picker(*far_faces), rest_picker(species, *far_faces),
-        sub_sends, group_sends,
+        adjoint, near, far, sub_sends, group_sends,
     )
 
     received = lax.all_to_all(send, "sub", split_axis=0, concat_axis=0, tiled=True)
@@ -352,51 +365,50 @@
     )
 
     face_nodes = face_rows // 6
-    adjoint_next, contrib = pl.pallas_call(
+    width = species * heights
+    hbm = pl.BlockSpec(memory_space=pltpu.HBM)
+    adjoint_next, contrib, for_other = pl.pallas_call(
         functools.partial(update_kernel, elements=elements),
         grid=(steps,),
         in_specs=[
             pl.BlockSpec((6, block), lambda i: (0, i)),
-            pl.BlockSpec((6, rows, block), lambda i: (0, 0, i)),
-            whole(peers, 2, rows, 2 * half), whole(rows, vcap), whole(rows, vcap),
+            hbm, whole(peers, 2, rows, 2 * half), whole(rows, vcap), whole(rows, vcap),
             pl.BlockSpec((face_rows, block), lambda i: (0, i)),
             whole(2 * rows, face_rows), whole(face_rows, face_rows), whole(face_rows, nodes), whole(heights, nodes),
-            pl.BlockSpec((species, nodes, block), lambda i: (0, 0, i)),
+            hbm, whole(1, elements),
         ],
         out_specs=[
             pl.BlockSpec((species, nodes, block), lambda i: (0, 0, i)),
-            whole(elements, 2 * species * heights),
-        ],
-        out_shape=[sds((species, nodes, elements), F32), sds((elements, 2 * species * heights), BF16)],
+            whole(elements, 2 * width), whole(tiles // 2, width),
+        ],
+        out_shape=[
+            sds((species, nodes, elements), F32), sds((elements, 2 * width), BF16), sds((tiles // 2, width), F32),
+        ],
         scratch_shapes=[
             pltpu.VMEM((4, rows, slots), BF16), pltpu.VMEM((nodes, face_rows), BF16),
             pltpu.VMEM((species, face_rows, block), BF16), pltpu.VMEM((species, nodes, block), BF16),
+            pltpu.VMEM((steps, 6, rows, block), F32), pltpu.VMEM((steps, species, nodes, block), F32),
+            pltpu.SemaphoreType.DMA((2, steps)),
         ],
         compiler_params=params(UPDATE_MIB),
         cost_estimate=cost(8_000_000_000, 28_000_000),
         name="update",
     )(
         neighbours, gap, received, from_below, from_above, face_speed, speed_picker(species, face_nodes),
-        lift_picker(face_nodes), lift_operator.T, emission_profile.T, base,
-    )
-
-    width = species * heights
-    row_block = tiles // groups
-
-    def scattered(other):
-        return pl.pallas_call(
-            functools.partial(scatter_kernel, other=other),
-            grid=(groups // 2,),
-            in_specs=[whole(1, elements), whole(elements, 2 * width)],
-            out_specs=pl.BlockSpec((row_block, width), lambda i: (i, 0)),
-            out_shape=sds((tiles // 2, width), F32),
-            compiler_params=params(16),
-            cost_estimate=cost(2_100_000_000, 2_000_000),
-            name="scatter_other" if other else "scatter_own",
-        )(tile_rows, contrib)
-
-    theirs = lax.ppermute(scattered(True), "core", [(0, 1), (1, 0)])
-    partial = (scattered(False) + theirs).astype(BF16)
+        lift_picker(face_nodes), lift_operator.T, emission_profile.T, base, tile_rows,
+    )
+
+    theirs = lax.ppermute(for_other, "core", [(0, 1), (1, 0)])
+    own = pl.pallas_call(
+        own_kernel,
+        in_specs=[vmem] * 2,
+        out_specs=vmem,
+        out_shape=sds((tiles // 2, width), F32),
+        compiler_params=params(16),
+        cost_estimate=cost(2_100_000_000, 2_000_000),
+        name="scatter_own",
+    )(tile_rows, contrib)
+    partial = (own + theirs).astype(BF16)
     chips = groups * peers // 2
     pieces = lax.all_to_all(
         partial.reshape(chips, tiles // 2 // chips, width), ("z", "sub"), split_axis=0, concat_axis=0

time: 83.8 us -> 77.4 us (0.924)
  Pallas kernels: 45.3 us -> 40.4 us
  local copies, waits for them, and re-layouts: 2.26 us -> 0.72 us
    pallas_call x2 -> x1, Pallas kernels: 5.73 us -> 2.32 us  [on_device(): pl.pallas_call(own_kernel, in_specs=[vmem] * 2, out_specs=vmem, out_shape...]
    unnamed x10 -> x14, local copies, waits for them, and re-layouts: 2.26 us -> 0.72 us
    pallas_call x1, Pallas kernels: 14.2 us -> 13 us  [on_device(): pl.pallas_call(functools.partial(update_kernel, elements=elements), grid=...]
  transfers between devices with their start and end apart: 4 -> 4, of which waited for: 0 -> 1; matrix products, arithmetic and copies ran while one was open for 0% -> 0% of each run, Pallas kernels for 24% -> 25%
where the time goes in v4:
time: 77.4 us; the launch traced here: 77.1 us
  Pallas kernels  40.4 us (52%)
  blocking collectives  23.6 us (30%)
  starting transfers between devices  10.5 us (14%)
  other arithmetic  0.81 us (1%)
  between operations  0.79 us (1%)
    all_to_all x1, blocking collectives, on_device(): lax.all_to_all(partial.reshape(chips, tiles // 2 // chips, width), ('z',...  23.6 us
    pallas_call x1, Pallas kernels, on_device(): pl.pallas_call(local_kernel, grid=(steps,), in_specs=[pl.BlockSpec((speci...  17.1 us
    pallas_call x1, Pallas kernels, on_device(): pl.pallas_call(functools.partial(update_kernel, elements=elements), grid=...  13 us
    pallas_call x1, Pallas kernels, on_device(): pl.pallas_call(send_kernel, in_specs=[pl.BlockSpec(memory_space=pl.ANY)]...  8 us
    all_to_all x1, starting transfers between devices, on_device(): lax.all_to_all(send, 'sub', split_axis=0, concat_axis=0, tiled=True)  7.15 us
    ppermute x1, starting transfers between devices, on_device(): from_above = lax.ppermute(down, ('z', 'core'), ring_down)  3.21 us
    pallas_call x1, Pallas kernels, on_device(): pl.pallas_call(own_kernel, in_specs=[vmem] * 2, out_specs=vmem, out_shape...  2.32 us
  transfers between devices with their start and end apart: 4, of which 1 were waited for; matrix products, arithmetic and copies ran while one was open for 0% of the time, Pallas kernels for 25%

profile of v4, /device:TPU:0, one launch (start us, length us, event | category | flops | bytes accessed | tf_op | source)
XLA Modules:
  0.0 77.1 jit_solution(7009491703441494178)
XLA Ops:
  0.6 8.0 %sends.1 = (bf16[6,144,2048]{2,1,0:T(8,128)(2,1)}, bf16[16,2,144,128]{3,2,1,0:T(8,128)(2,1)}, bf16[144,256]{1,0:T(8,128)(2,1)}, bf16[144,256]{1,0:T(8,128)(2,1)}) custom-call(f32[4,256,2048]{2,1,0:T(8,128)} %adj_ref.1, bf16[2,4,48,40]{3,2,1,0:T(8,128)(2,1)} %constant.56.near_ref, bf16[4,192,216]{2,1,0:T(8,128)(2,1)} %constant.61.far_ref, s32[4,1024]{1,0:T(4,128)} %ss_ref.1, ...), custom_call_target="tpu_custom_call" | custom-call | flops 12000000000 | bytes 14000000 | tf_op jit(solution)/shard_map/sends/pallas_call | solution.py:315
  8.6 7.2 %all-to-all-start = ((bf16[16,2,144,128]{3,2,1,0:T(8,128)(2,1)}), bf16[16,2,144,128]{3,2,1,0:T(8,128)(2,1)S(1)}, u32[]{:S(2)}, u32[]{:S(2)}) async-start(bf16[16,2,144,128]{3,2,1,0:T(8,128)(2,1)} %get-tuple-element.14), calls=%async_computation | async-start | bytes 2359296 | tf_op jit(solution)/shard_map/all_to_all | solution.py:331
  15.8 0.0 collective-permute-start
  15.8 3.2 %collective-permute-start.1 = (bf16[144,256]{1,0:T(8,128)(2,1)}, bf16[144,256]{1,0:T(8,128)(2,1)S(1)}, u32[]{:S(2)}, u32[]{:S(2)}) collective-permute-start(bf16[144,256]{1,0:T(8,128)(2,1)} %get-tuple-element.16), channel_id=1, source_target_pairs={{0,112},{16,0},{32,16},{48,32},{64,48},{80,64},{96,80},{112,96},{1... | collective-permute-start | bytes 221192 | tf_op jit(solution)/shard_map/ppermute | solution.py:335
  19.0 0.0 copy-start
  19.0 0.0 copy-start.1
  19.0 0.0 copy-start.2
  19.0 0.0 copy-start.3
  19.0 0.0 copy-start.4
  19.1 0.0 copy-start.5
  19.1 17.1 %local.1 = (f32[4,256,2048]{2,1,0:T(8,128)}, f32[6,144,2048]{2,1,0:T(8,128)}, s32[1,2048]{1,0:T(1,128)}) custom-call(f32[4,256,2048]{2,1,0:T(8,128)} %adj_ref.1, bf16[3,256,2048]{2,1,0:T(8,128)(2,1)} %vel_ref.1, bf16[768,256]{1,0:T(8,128)(2,1)} %der_ref.1, s32[6,2048]{1,0:T(8,128)} %nbr_ref.3, bf16[6,144,2048]{2,1,0:T(8,128)(2,1)} %get-tuple-element.12.pool_hbm, ...), custom_call_target="tpu_custom_call" | custom-call | flops 16000000000 | bytes 32000000 | tf_op jit(solution)/shard_map/local/pallas_call | solution.py:337
  36.1 0.0 collective-permute-done.below_ref
  36.1 0.0 collective-permute-done.1.above_ref
  36.2 0.0 all-to-all-done.recv_ref
  36.2 0.0 copy-done
  36.2 0.0 copy-done.1
  36.2 0.0 copy-done.2
  36.2 0.0 copy-done.3
  36.2 0.0 copy-done.4
  36.2 0.0 copy-done.5
  36.2 0.0 copy-start.6
  36.2 0.7 copy-done.6
  36.9 13.0 %update.1 = (f32[4,256,2048]{2,1,0:T(8,128)}, bf16[2048,256]{1,0:T(8,128)(2,1)S(1)}, f32[2048,128]{1,0:T(8,128)S(1)}) custom-call(s32[6,2048]{1,0:T(8,128)S(1)} %copy-done.2, f32[6,144,2048]{2,1,0:T(8,128)} %get-tuple-element.13.gap_hbm, bf16[16,2,144,128]{3,2,1,0:T(8,128)(2,1)S(1)} %all-to-all-done.recv_ref, ...), custom_call_target="tpu_custom_call" | custom-call | flops 8000000000 | bytes 28000000 | tf_op jit(solution)/shard_map/update/pallas_call | solution.py:370
  49.9 0.1 collective-permute-start.2
  50.0 2.3 %scatter_own.1 = f32[2048,128]{1,0:T(8,128)S(1)} custom-call(s32[1,2048]{1,0:T(1,128)S(1)} %copy-done.6, bf16[2048,256]{1,0:T(8,128)(2,1)S(1)} %get-tuple-element.20.contrib_ref), custom_call_target="tpu_custom_call" | custom-call | flops 2100000000 | bytes 2000000 | tf_op jit(solution)/shard_map/scatter_own/pallas_call | solution.py:402
  52.4 0.3 collective-permute-done.2
  52.7 0.1 add_convert_fusion
  52.8 23.6 %all_to_all.10 = bf16[64,32,128]{2,1,0:T(8,128)(2,1)S(1)} all-to-all(bf16[64,32,128]{2,1,0:T(8,128)(2,1)S(1)} %bitcast.7), channel_id=1, replica_groups=mesh['z'=4,'core'=2,'sub'=16] {'z','sub'}, dimensions={0} | all-to-all | bytes 1048576 | tf_op jit(solution)/shard_map/all_to_all | solution.py:413
  76.4 0.7 convert_reduce_fusion
Async XLA Ops:
  8.6 27.5 %all-to-all-start = ((bf16[16,2,144,128]{3,2,1,0:T(8,128)(2,1)}), bf16[16,2,144,128]{3,2,1,0:T(8,128)(2,1)S(1)}, u32[]{:S(2)}, u32[]{:S(2)}) async-start(bf16[16,2,144,128]{3,2,1,0:T(8,128)(2,1)} %get-tuple-element.14), calls=%async_computation | async-start | bytes 2359296 | tf_op jit(solution)/shard_map/all_to_all | solution.py:331
  15.8 20.3 %collective-permute-start = (bf16[144,256]{1,0:T(8,128)(2,1)}, bf16[144,256]{1,0:T(8,128)(2,1)S(1)}, u32[]{:S(2)}, u32[]{:S(2)}) collective-permute-start(bf16[144,256]{1,0:T(8,128)(2,1)} %get-tuple-element.15), channel_id=1, source_target_pairs={{0,16},{16,32},{32,48},{48,64},{64,80},{80,96},{96,112},{112,0},{1... | collective-permute-start | bytes 221192 | tf_op jit(solution)/shard_map/ppermute | solution.py:334
  15.8 20.3 %collective-permute-start.1 = (bf16[144,256]{1,0:T(8,128)(2,1)}, bf16[144,256]{1,0:T(8,128)(2,1)S(1)}, u32[]{:S(2)}, u32[]{:S(2)}) collective-permute-start(bf16[144,256]{1,0:T(8,128)(2,1)} %get-tuple-element.16), channel_id=1, source_target_pairs={{0,112},{16,0},{32,16},{48,32},{64,48},{80,64},{96,80},{112,96},{1... | collective-permute-start | bytes 221192 | tf_op jit(solution)/shard_map/ppermute | solution.py:335
  19.0 17.1 %copy-start = (bf16[216,2048]{1,0:T(8,128)(2,1)S(1)}, bf16[216,2048]{1,0:T(8,128)(2,1)}, u32[]{:S(2)}) copy-start(bf16[216,2048]{1,0:T(8,128)(2,1)} %fs_ref.1) | copy-start | bytes 2654212
  19.0 17.1 %copy-start.1 = (bf16[256,216]{0,1:T(8,128)(2,1)S(1)}, bf16[256,216]{0,1:T(8,128)(2,1)}, u32[]{:S(2)}) copy-start(bf16[256,216]{0,1:T(8,128)(2,1)} %param.29) | copy-start | bytes 331780
  19.0 17.1 %copy-start.2 = (s32[6,2048]{1,0:T(8,128)S(1)}, s32[6,2048]{1,0:T(8,128)}, u32[]{:S(2)}) copy-start(s32[6,2048]{1,0:T(8,128)} %nbr_ref.3) | copy-start | bytes 147460
  19.0 17.2 %copy-start.3 = (bf16[256,32]{0,1:T(8,128)(2,1)S(1)}, bf16[256,32]{0,1:T(8,128)(2,1)}, u32[]{:S(2)}) copy-start(bf16[256,32]{0,1:T(8,128)(2,1)} %param.30) | copy-start | bytes 49156
  19.0 17.2 %copy-start.4 = (bf16[288,216]{1,0:T(8,128)(2,1)S(1)}, bf16[288,216]{1,0:T(8,128)(2,1)}, u32[]{:S(2)}) copy-start(bf16[288,216]{1,0:T(8,128)(2,1)} %constant.42.clone.speed_ref) | copy-start | bytes 373252
  19.1 17.2 %copy-start.5 = (bf16[216,216]{1,0:T(8,128)(2,1)S(1)}, bf16[216,216]{1,0:T(8,128)(2,1)}, u32[]{:S(2)}) copy-start(bf16[216,216]{1,0:T(8,128)(2,1)} %constant.43.clone.order_ref) | copy-start | bytes 279940
  36.2 0.7 copy-start.6
  49.9 2.7 %collective-permute-start.2 = (f32[2048,128]{1,0:T(8,128)S(1)}, f32[2048,128]{1,0:T(8,128)S(1)}, u32[]{:S(2)}, u32[]{:S(2)}) collective-permute-start(f32[2048,128]{1,0:T(8,128)S(1)} %get-tuple-element.21), channel_id=1, source_target_pairs={{0,16},{16,0},{1,17},{17,1},{2,18},{18,2},{3,19},{19,3},{4,20},{20... | collective-permute-start | bytes 3145736 | tf_op jit(solution)/shard_map/ppermute | solution.py:401

commit v5 on v4

--- a/solution.py
+++ b/solution.py
@@ -81,18 +81,24 @@
 
 
 def send_kernel(
-    adj_hbm, near_ref, far_ref, ss_ref, gs_ref,
-    pool_ref, send_ref, up_ref, down_ref, adj, sems,
+    adj_hbm, near_hbm, far_hbm, ss_hbm, gs_hbm, pool_hbm, send_hbm, up_hbm, down_hbm,
+    adj, near_ref, far_ref, ss_ref, gs_ref, pool_ref, send_ref, up_ref, down_ref, in_sems, pool_sems, out_sems,
 ):
     species = adj.shape[0]
     rows, elements = pool_ref.shape[1:]
     half = send_ref.shape[3] // 2
-    copies = [
-        pltpu.make_async_copy(adj_hbm.at[:, a:b, :], adj.at[:, a:b, :], sems.at[i])
-        for i, (a, b) in enumerate((LOW, HIGH, MID))
-    ]
+    pairs = [(near_hbm, near_ref), (ss_hbm, ss_ref)]
+    pairs += [(adj_hbm.at[:, a:b, :], adj.at[:, a:b, :]) for a, b in (LOW, HIGH, MID)]
+    pairs += [(far_hbm, far_ref), (gs_hbm, gs_ref)]
+    copies = [pltpu.make_async_copy(x, y, in_sems.at[i]) for i, (x, y) in enumerate(pairs)]
     for copy in copies:
         copy.start()
+    leaving = []
+
+    def leave(source, target, sem):
+        leaving.append(pltpu.make_async_copy(source, target, sem))
+        leaving[-1].start()
+
     low = lax.broadcasted_iota(I32, (rows, 2 * half), 1) < half
 
     def exchange(q):
@@ -114,88 +120,140 @@
                 pieces = [x[MAIN * i : MAIN * (i + 1)] for x in found] + [rest[shared * i : shared * (i + 1)]]
                 pool_ref[f, :, c : c + chunk] = jnp.concatenate(pieces, axis=0).astype(BF16)
 
-    copies[0].wait()
-    copies[1].wait()
+    for copy in copies[:4]:
+        copy.wait()
     fill((0,), near_ref[0], *LOW, 1024)
     fill((1,), near_ref[1], *HIGH, 1024)
     exchange(0)
-    copies[2].wait()
+    leave(send_ref.at[:, 0], send_hbm.at[:, 0], out_sems.at[0])
+    for f in (0, 1):
+        leave(pool_ref.at[f], pool_hbm.at[f], pool_sems.at[f])
+    for copy in copies[4:]:
+        copy.wait()
     fill((2, 3, 4, 5), far_ref[...], 0, HIGH[1], 512)
-    exchange(1)
+    for f in (2, 3, 4, 5):
+        leave(pool_ref.at[f], pool_hbm.at[f], pool_sems.at[f])
     down_ref[...] = dot(pool_ref[4], one_hot(elements, gs_ref[0:1, :])).astype(BF16)
     up_ref[...] = dot(pool_ref[5], one_hot(elements, gs_ref[1:2, :])).astype(BF16)
+    exchange(1)
+    leave(down_ref, down_hbm, out_sems.at[1])
+    leave(up_ref, up_hbm, out_sems.at[2])
+    leave(send_ref.at[:, 1], send_hbm.at[:, 1], out_sems.at[3])
+    for copy in leaving:
+        copy.wait()
 
 
 def local_kernel(
-    adj_ref, vel_ref, der_ref, nbr_ref, pool_hbm, tile_ref, slot_ref, base_ref, gap_ref, row_ref, pool, mixed, sems,
+    adj_hbm, vel_hbm, der_hbm, pool_hbm, nbr_ref, tile_ref, slot_ref, base_hbm, gap_hbm, row_ref,
+    adj_all, vel_all, der, pool, mixed, gap_all, adj_sems, vel_sems, pool_sems, der_sem, base_sems, gap_sems,
 ):
     step = pl.program_id(0)
-    species, nodes, block = adj_ref.shape
+    steps, species, nodes, block = adj_all.shape
     group = 16
-    copies = [pltpu.make_async_copy(pool_hbm.at[f], pool.at[f], sems.at[f]) for f in range(6)]
+
+    def entering(index):
+        cols = pl.ds(pl.multiple_of(index * block, block), block)
+        return (
+            pltpu.make_async_copy(adj_hbm.at[:, :, cols], adj_all.at[index], adj_sems.at[index]),
+            pltpu.make_async_copy(vel_hbm.at[:, :, cols], vel_all.at[index], vel_sems.at[index]),
+        )
+
+    def base_leaving(index):
+        return pltpu.make_async_copy(adj_all.at[index], base_hbm.at[index], base_sems.at[index])
+
+    def gap_leaving(index, f):
+        return pltpu.make_async_copy(gap_all.at[index, f], gap_hbm.at[index, f], gap_sems.at[index, f])
+
+    matrix = pltpu.make_async_copy(der_hbm, der, der_sem.at[0])
+    pools = [pltpu.make_async_copy(pool_hbm.at[f], pool.at[f], pool_sems.at[f]) for f in range(6)]
 
     @pl.when(step == 0)
     def _():
-        for copy in copies:
+        matrix.start()
+        for copy in (*entering(0), *pools):
             copy.start()
+        for index in range(1, steps):
+            for copy in entering(index):
+                copy.start()
+        tile_rows(tile_ref, slot_ref, row_ref, block)
+        matrix.wait()
         for d in range(3):
             for b in range(nodes // group):
-                rows = der_ref[d * nodes + b * group : d * nodes + (b + 1) * group, :]
+                rows = der[d * nodes + b * group : d * nodes + (b + 1) * group, :]
                 mixed[(3 * b + d) * group : (3 * b + d + 1) * group, :] = rows * jnp.asarray(SECTION, BF16)
 
+    for copy in entering(step):
+        copy.wait()
     for s in range(species):
-        g = dot(mixed[...], adj_ref[s].astype(BF16))
+        g = dot(mixed[...], adj_all[step, s].astype(BF16))
         for b in range(nodes // group):
             rows = slice(b * group, (b + 1) * group)
-            total = adj_ref[s, rows]
+            total = adj_all[step, s, rows]
             for d in range(3):
-                total += vel_ref[d, rows].astype(F32) * g[(3 * b + d) * group : (3 * b + d + 1) * group]
-            base_ref[s, rows] = total
+                total += vel_all[step, d, rows].astype(F32) * g[(3 * b + d) * group : (3 * b + d + 1) * group]
+            adj_all[step, s, rows] = total
+    base_leaving(step).start()
 
     @pl.when(step == 0)
     def _():
-        elements = tile_ref.shape[1]
-        high, lanes = slot_ref.shape
-        fine = lanes // 2
-        slot = jnp.transpose(slot_ref[...].astype(F32))
-        upper = jnp.floor(slot * (1.0 / 64.0))
-        digits = jnp.concatenate([
-            jnp.concatenate([x[:fine], x[fine:]], axis=1) for x in (upper, slot - 64.0 * upper)
-        ], axis=0).astype(BF16)
-        bits = fine.bit_length() - 1
-        for c in range(0, elements, block):
-            tile = tile_ref[:, c : c + block]
-            coarse = jnp.right_shift(tile, bits)
-            place = jnp.bitwise_and(coarse, 1) * high + jnp.right_shift(coarse, 1)
-            found = dot(digits, one_hot(2 * high, place))
-            rows = 64.0 * found[:fine] + found[fine:]
-            within = lax.broadcasted_iota(I32, rows.shape, 0) == jnp.bitwise_and(tile, fine - 1)
-            row_ref[:, c : c + block] = jnp.sum(jnp.where(within, rows, 0.0), axis=0, keepdims=True).astype(I32)
-        for copy in copies:
+        for copy in pools:
             copy.wait()
 
     cols = pl.ds(pl.multiple_of(step * block, block), block)
     for f in range(6):
-        hot = one_hot(pool.shape[2], nbr_ref[f : f + 1, :])
-        gap_ref[f] = dot(pool[f ^ 1], hot) - pool[f, :, cols].astype(F32)
+        hot = one_hot(pool.shape[2], nbr_ref[f : f + 1, cols])
+        gap_all[step, f] = dot(pool[f ^ 1], hot) - pool[f, :, cols].astype(F32)
+        gap_leaving(step, f).start()
+
+    @pl.when(step == steps - 1)
+    def _():
+        for index in range(steps):
+            base_leaving(index).wait()
+            for f in range(6):
+                gap_leaving(index, f).wait()
+
+
+def tile_rows(tile_ref, slot_ref, row_ref, block):
+    elements = tile_ref.shape[1]
+    high, lanes = slot_ref.shape
+    fine = lanes // 2
+    slot = jnp.transpose(slot_ref[...].astype(F32))
+    upper = jnp.floor(slot * (1.0 / 64.0))
+    digits = jnp.concatenate([
+        jnp.concatenate([x[:fine], x[fine:]], axis=1) for x in (upper, slot - 64.0 * upper)
+    ], axis=0).astype(BF16)
+    bits = fine.bit_length() - 1
+    for c in range(0, elements, block):
+        tile = tile_ref[:, c : c + block]
+        coarse = jnp.right_shift(tile, bits)
+        place = jnp.bitwise_and(coarse, 1) * high + jnp.right_shift(coarse, 1)
+        found = dot(digits, one_hot(2 * high, place))
+        rows = 64.0 * found[:fine] + found[fine:]
+        within = lax.broadcasted_iota(I32, rows.shape, 0) == jnp.bitwise_and(tile, fine - 1)
+        row_ref[:, c : c + block] = jnp.sum(jnp.where(within, rows, 0.0), axis=0, keepdims=True).astype(I32)
 
 
 def update_kernel(
-    nbr_ref, gap_hbm, recv_ref, below_ref, above_ref, fs_ref, speed_ref, order_ref, lift_ref, prof_ref, base_hbm, row_ref,
-    next_ref, contrib_ref, other_ref, rpool, lift_sorted, flux, low_next, gap_all, base_all, sems, *, elements,
+    nbr_ref, gap_hbm, recv_ref, below_ref, above_ref, fs_ref, speed_ref, order_ref, lift_ref, prof_ref, base_hbm, row_hbm,
+    next_hbm, contrib_ref, other_ref, seen_ref, rpool, lift_sorted, flux, low_next, gap_all, base_all, row_ref,
+    sems, next_sems, row_sem, *, elements,
 ):
     step = pl.program_id(0)
     peers, _, rows, width = recv_ref.shape
     half = width // 2
-    species, nodes, block = next_ref.shape
-    steps = gap_all.shape[0]
+    steps, species, nodes, block = base_all.shape
 
     def loads(index):
+        return (
+            pltpu.make_async_copy(gap_hbm.at[index], gap_all.at[index], sems.at[0, index]),
+            pltpu.make_async_copy(base_hbm.at[index], base_all.at[index], sems.at[1, index]),
+        )
+
+    def leaving(index):
         cols = pl.ds(pl.multiple_of(index * block, block), block)
-        return (
-            pltpu.make_async_copy(gap_hbm.at[:, :, cols], gap_all.at[index], sems.at[0, index]),
-            pltpu.make_async_copy(base_hbm.at[:, :, cols], base_all.at[index], sems.at[1, index]),
-        )
+        return pltpu.make_async_copy(base_all.at[index], next_hbm.at[:, :, cols], next_sems.at[index])
+
+    lines = pltpu.make_async_copy(row_hbm, row_ref, row_sem.at[0])
 
     def contribute(index):
         terms = [dot(prof_ref[...], low_next[s]) for s in range(species)]
@@ -210,6 +268,7 @@
         for index in range(steps):
             for copy in loads(index):
                 copy.start()
+        lines.start()
         low = lax.broadcasted_iota(I32, (rows, width), 1) < half
         for q in range(2):
             for i in range(peers // 2):
@@ -256,13 +315,18 @@
         flux[s, 6 * MAIN :, :] = jnp.concatenate(tails[s], axis=0).astype(BF16)
     for s in range(species):
         value = base_ref[s] + dot(lift_sorted[...], flux[s])
-        next_ref[s] = value
+        base_ref[s] = value
         low_next[s] = value.astype(BF16)
+    leaving(step).start()
 
     @pl.when(step == steps - 1)
     def _():
         contribute(step)
+        lines.wait()
+        seen_ref[...] = row_ref[...]
         scatter(row_ref, contrib_ref, other_ref, True)
+        for index in range(steps):
+            leaving(index).wait()
 
 
 def scatter(row_ref, contrib_ref, out_ref, other):
@@ -312,15 +376,20 @@
     near = jnp.stack([trace_picker(species, (f,), *span) for f, span in enumerate((LOW, HIGH))])
     far = trace_picker(species, (2, 3, 4, 5), 0, HIGH[1])
     vmem = pl.BlockSpec(memory_space=pltpu.VMEM)
+    hbm = pl.BlockSpec(memory_space=pltpu.HBM)
+    made = [
+        sds((6, rows, elements), BF16), sds((peers, 2, rows, 2 * half), BF16), sds((rows, vcap), BF16), sds((rows, vcap), BF16),
+    ]
     pool, send, up, down = pl.pallas_call(
         send_kernel,
-        in_specs=[pl.BlockSpec(memory_space=pl.ANY)] + [vmem] * 4,
-        out_specs=[vmem] * 4,
-        out_shape=[
-            sds((6, rows, elements), BF16), sds((peers, 2, rows, 2 * half), BF16),
-            sds((rows, vcap), BF16), sds((rows, vcap), BF16),
-        ],
-        scratch_shapes=[pltpu.VMEM((species, HIGH[1], elements), F32), pltpu.SemaphoreType.DMA((3,))],
+        in_specs=[hbm] * 5,
+        out_specs=[hbm] * 4,
+        out_shape=made,
+        scratch_shapes=[
+            pltpu.VMEM((species, HIGH[1], elements), F32),
+            *(pltpu.VMEM(x.shape, x.dtype) for x in (near, far, sub_sends, group_sends, *made)),
+            pltpu.SemaphoreType.DMA((7,)), pltpu.SemaphoreType.DMA((6,)), pltpu.SemaphoreType.DMA((4,)),
+        ],
         compiler_params=params(60),
         cost_estimate=cost(12_000_000_000, 14_000_000),
         name="sends",
@@ -334,40 +403,31 @@
     from_below = lax.ppermute(up, ("z", "core"), ring_up)
     from_above = lax.ppermute(down, ("z", "core"), ring_down)
 
-    base, gap, tile_rows = pl.pallas_call(
+    base, gap, tile_row = pl.pallas_call(
         local_kernel,
         grid=(steps,),
-        in_specs=[
-            pl.BlockSpec((species, nodes, block), lambda i: (0, 0, i)),
-            pl.BlockSpec((3, nodes, block), lambda i: (0, 0, i)),
-            whole(3 * nodes, nodes),
-            pl.BlockSpec((6, block), lambda i: (0, i)),
-            pl.BlockSpec(memory_space=pl.ANY),
-            whole(1, elements), whole(tiles // 128, 128),
-        ],
-        out_specs=[
-            pl.BlockSpec((species, nodes, block), lambda i: (0, 0, i)),
-            pl.BlockSpec((6, rows, block), lambda i: (0, 0, i)),
-            whole(1, elements),
-        ],
+        in_specs=[hbm] * 4 + [whole(6, elements), whole(1, elements), whole(tiles // 128, 128)],
+        out_specs=[hbm, hbm, whole(1, elements)],
         out_shape=[
-            sds((species, nodes, elements), F32), sds((6, rows, elements), F32), sds((1, elements), I32),
+            sds((steps, species, nodes, block), F32), sds((steps, 6, rows, block), F32), sds((1, elements), I32),
         ],
         scratch_shapes=[
-            pltpu.VMEM((6, rows, elements), BF16), pltpu.VMEM((3 * nodes, nodes), BF16), pltpu.SemaphoreType.DMA((6,)),
+            pltpu.VMEM((steps, species, nodes, block), F32), pltpu.VMEM((steps, 3, nodes, block), BF16),
+            pltpu.VMEM((3 * nodes, nodes), BF16), pltpu.VMEM((6, rows, elements), BF16),
+            pltpu.VMEM((3 * nodes, nodes), BF16), pltpu.VMEM((steps, 6, rows, block), F32),
+            *(pltpu.SemaphoreType.DMA(shape) for shape in ((steps,), (steps,), (6,), (1,), (steps,), (steps, 6))),
         ],
         compiler_params=params(60),
         cost_estimate=cost(16_000_000_000, 32_000_000),
         name="local",
     )(
-        adjoint, velocity, derivatives, neighbours, pool, element_tile.reshape(1, elements),
+        adjoint, velocity, derivatives, pool, neighbours, element_tile.reshape(1, elements),
         tile_slot.reshape(tiles // 128, 128),
     )
 
     face_nodes = face_rows // 6
     width = species * heights
-    hbm = pl.BlockSpec(memory_space=pltpu.HBM)
-    adjoint_next, contrib, for_other = pl.pallas_call(
+    adjoint_next, contrib, for_other, seen_row = pl.pallas_call(
         functools.partial(update_kernel, elements=elements),
         grid=(steps,),
         in_specs=[
@@ -375,27 +435,28 @@
             hbm, whole(peers, 2, rows, 2 * half), whole(rows, vcap), whole(rows, vcap),
             pl.BlockSpec((face_rows, block), lambda i: (0, i)),
             whole(2 * rows, face_rows), whole(face_rows, face_rows), whole(face_rows, nodes), whole(heights, nodes),
-            hbm, whole(1, elements),
+            hbm, hbm,
         ],
         out_specs=[
-            pl.BlockSpec((species, nodes, block), lambda i: (0, 0, i)),
-            whole(elements, 2 * width), whole(tiles // 2, width),
+            hbm, whole(elements, 2 * width), whole(tiles // 2, width), whole(1, elements),
         ],
         out_shape=[
             sds((species, nodes, elements), F32), sds((elements, 2 * width), BF16), sds((tiles // 2, width), F32),
+            sds((1, elements), I32),
         ],
         scratch_shapes=[
             pltpu.VMEM((4, rows, slots), BF16), pltpu.VMEM((nodes, face_rows), BF16),
             pltpu.VMEM((species, face_rows, block), BF16), pltpu.VMEM((species, nodes, block), BF16),
             pltpu.VMEM((steps, 6, rows, block), F32), pltpu.VMEM((steps, species, nodes, block), F32),
-            pltpu.SemaphoreType.DMA((2, steps)),
+            pltpu.VMEM((1, elements), I32),
+            pltpu.SemaphoreType.DMA((2, steps)), pltpu.SemaphoreType.DMA((steps,)), pltpu.SemaphoreType.DMA((1,)),
         ],
         compiler_params=params(UPDATE_MIB),
         cost_estimate=cost(8_000_000_000, 28_000_000),
         name="update",
     )(
         neighbours, gap, received, from_below, from_above, face_speed, speed_picker(species, face_nodes),
-        lift_picker(face_nodes), lift_operator.T, emission_profile.T, base, tile_rows,
+        lift_picker(face_nodes), lift_operator.T, emission_profile.T, base, tile_row,
     )
 
     theirs = lax.ppermute(for_other, "core", [(0, 1), (1, 0)])
@@ -407,7 +468,7 @@
         compiler_params=params(16),
         cost_estimate=cost(2_100_000_000, 2_000_000),
         name="scatter_own",
-    )(tile_rows, contrib)
+    )(seen_row, contrib)
     partial = (own + theirs).astype(BF16)
     chips = groups * peers // 2
     pieces = lax.all_to_all(

time: 77.4 us -> 77.3 us (level)
    pallas_call x1, Pallas kernels: 13 us -> 11.2 us  [on_device(): pl.pallas_call(functools.partial(update_kernel, elements=elements), grid=...]
    pallas_call x2, Pallas kernels: 25.1 us -> 26.7 us  [the longest x1 19.4 us: on_device(): pl.pallas_call(local_kernel, grid=(steps,), in_specs=[hbm] * 4 + [whole(6...]
  transfers between devices with their start and end apart: 4 -> 4, of which waited for: 1 -> 1; matrix products, arithmetic and copies ran while one was open for 0% -> 0% of each run, Pallas kernels for 25% -> 28%
where the time goes in v5:
time: 77.3 us; the launch traced here: 77 us
  Pallas kernels  40.2 us (52%)
  blocking collectives  23.6 us (31%)
  starting transfers between devices  10.5 us (14%)
  other arithmetic  0.81 us (1%)
  between operations  0.79 us (1%)
    all_to_all x1, blocking collectives, on_device(): lax.all_to_all(partial.reshape(chips, tiles // 2 // chips, width), ('z',...  23.6 us
    pallas_call x1, Pallas kernels, on_device(): pl.pallas_call(local_kernel, grid=(steps,), in_specs=[hbm] * 4 + [whole(6...  19.4 us
    pallas_call x1, Pallas kernels, on_device(): pl.pallas_call(functools.partial(update_kernel, elements=elements), grid=...  11.2 us
    pallas_call x1, Pallas kernels, on_device(): pl.pallas_call(send_kernel, in_specs=[hbm] * 5, out_specs=[hbm] * 4, out_...  7.28 us
    all_to_all x1, starting transfers between devices, on_device(): lax.all_to_all(send, 'sub', split_axis=0, concat_axis=0, tiled=True)  7.16 us
    ppermute x1, starting transfers between devices, on_device(): from_above = lax.ppermute(down, ('z', 'core'), ring_down)  3.21 us
    pallas_call x1, Pallas kernels, on_device(): pl.pallas_call(own_kernel, in_specs=[vmem] * 2, out_specs=vmem, out_shape...  2.32 us
  transfers between devices with their start and end apart: 4, of which 1 were waited for; matrix products, arithmetic and copies ran while one was open for 0% of the time, Pallas kernels for 28%

profile of v5, /device:TPU:0, one launch (start us, length us, event | category | flops | bytes accessed | tf_op | source)
XLA Modules:
  0.0 77.0 jit_solution(16159331011930405257)
XLA Ops:
  0.6 7.3 %sends.1 = (bf16[6,144,2048]{2,1,0:T(8,128)(2,1)}, bf16[16,2,144,128]{3,2,1,0:T(8,128)(2,1)}, bf16[144,256]{1,0:T(8,128)(2,1)}, bf16[144,256]{1,0:T(8,128)(2,1)}) custom-call(f32[4,256,2048]{2,1,0:T(8,128)} %adj_hbm.3, bf16[2,4,48,40]{3,2,1,0:T(8,128)(2,1)} %constant.56.near_hbm, bf16[4,192,216]{2,1,0:T(8,128)(2,1)} %constant.61.far_hbm, s32[4,1024]{1,0:T(4,128)} %ss_hbm.1, ...), custom_call_target="tpu_custom_call" | custom-call | flops 12000000000 | bytes 14000000 | tf_op jit(solution)/shard_map/sends/pallas_call | solution.py:383
  7.9 7.2 %all-to-all-start = ((bf16[16,2,144,128]{3,2,1,0:T(8,128)(2,1)}), bf16[16,2,144,128]{3,2,1,0:T(8,128)(2,1)S(1)}, u32[]{:S(2)}, u32[]{:S(2)}) async-start(bf16[16,2,144,128]{3,2,1,0:T(8,128)(2,1)} %get-tuple-element.15), calls=%async_computation | async-start | bytes 2359296 | tf_op jit(solution)/shard_map/all_to_all | solution.py:400
  15.1 0.0 collective-permute-start
  15.1 3.2 %collective-permute-start.1 = (bf16[144,256]{1,0:T(8,128)(2,1)}, bf16[144,256]{1,0:T(8,128)(2,1)S(1)}, u32[]{:S(2)}, u32[]{:S(2)}) collective-permute-start(bf16[144,256]{1,0:T(8,128)(2,1)} %get-tuple-element.17), channel_id=1, source_target_pairs={{0,112},{16,0},{32,16},{48,32},{64,48},{80,64},{96,80},{112,96},{1... | collective-permute-start | bytes 221192 | tf_op jit(solution)/shard_map/ppermute | solution.py:404
  18.3 0.0 copy-start
  18.3 0.0 copy-start.1
  18.3 0.0 copy-start.2
  18.3 0.0 copy-start.3
  18.3 0.0 copy-start.4
  18.3 0.0 copy-start.5
  18.4 19.4 %local.1 = (f32[4,4,256,512]{3,2,1,0:T(8,128)}, f32[4,6,144,512]{3,2,1,0:T(8,128)}, s32[1,2048]{1,0:T(1,128)}) custom-call(f32[4,256,2048]{2,1,0:T(8,128)} %adj_hbm.3, bf16[3,256,2048]{2,1,0:T(8,128)(2,1)} %vel_hbm.1, bf16[768,256]{1,0:T(8,128)(2,1)} %der_hbm.1, bf16[6,144,2048]{2,1,0:T(8,128)(2,1)} %get-tuple-element.13.pool_hbm, s32[6,2048]{1,0:T(8,128)} %nbr_ref.3, ...), custom_call_target="tpu_custom_call" | custom-call | flops 16000000000 | bytes 32000000 | tf_op jit(solution)/shard_map/local/pallas_call | solution.py:406
  37.8 0.0 collective-permute-done.below_ref
  37.8 0.0 collective-permute-done.1.above_ref
  37.8 0.0 all-to-all-done.recv_ref
  37.8 0.0 copy-done
  37.8 0.0 copy-done.1
  37.8 0.0 copy-done.2
  37.8 0.0 copy-done.3
  37.8 0.0 copy-done.4
  37.8 0.0 copy-done.5
  37.8 0.0 copy-start.6
  37.9 0.7 copy-done.6
  38.5 11.2 %update.1 = (f32[4,256,2048]{2,1,0:T(8,128)}, bf16[2048,256]{1,0:T(8,128)(2,1)S(1)}, f32[2048,128]{1,0:T(8,128)S(1)}, s32[1,2048]{1,0:T(1,128)S(1)}) custom-call(s32[6,2048]{1,0:T(8,128)S(1)} %copy-done.2, f32[4,6,144,512]{3,2,1,0:T(8,128)} %get-tuple-element.14.gap_hbm, bf16[16,2,144,128]{3,2,1,0:T(8,128)(2,1)S(1)} %all-to-all-done.recv_ref, ...), custom_call_target="tpu_custom_call" | custom-call | flops 8000000000 | bytes 28000000 | tf_op jit(solution)/shard_map/update/pallas_call | solution.py:430
  49.8 0.1 collective-permute-start.2
  49.9 2.3 %scatter_own.1 = f32[2048,128]{1,0:T(8,128)S(1)} custom-call(s32[1,2048]{1,0:T(1,128)S(1)} %get-tuple-element.21.row_ref, bf16[2048,256]{1,0:T(8,128)(2,1)S(1)} %get-tuple-element.22.contrib_ref), custom_call_target="tpu_custom_call" | custom-call | flops 2100000000 | bytes 2000000 | tf_op jit(solution)/shard_map/scatter_own/pallas_call | solution.py:463
  52.2 0.3 collective-permute-done.2
  52.5 0.1 add_convert_fusion
  52.6 23.6 %all_to_all.10 = bf16[64,32,128]{2,1,0:T(8,128)(2,1)S(1)} all-to-all(bf16[64,32,128]{2,1,0:T(8,128)(2,1)S(1)} %bitcast.7), channel_id=1, replica_groups=mesh['z'=4,'core'=2,'sub'=16] {'z','sub'}, dimensions={0} | all-to-all | bytes 1048576 | tf_op jit(solution)/shard_map/all_to_all | solution.py:474
  76.3 0.7 convert_reduce_fusion
Async XLA Ops:
  7.9 29.9 %all-to-all-start = ((bf16[16,2,144,128]{3,2,1,0:T(8,128)(2,1)}), bf16[16,2,144,128]{3,2,1,0:T(8,128)(2,1)S(1)}, u32[]{:S(2)}, u32[]{:S(2)}) async-start(bf16[16,2,144,128]{3,2,1,0:T(8,128)(2,1)} %get-tuple-element.15), calls=%async_computation | async-start | bytes 2359296 | tf_op jit(solution)/shard_map/all_to_all | solution.py:400
  15.1 22.7 %collective-permute-start = (bf16[144,256]{1,0:T(8,128)(2,1)}, bf16[144,256]{1,0:T(8,128)(2,1)S(1)}, u32[]{:S(2)}, u32[]{:S(2)}) collective-permute-start(bf16[144,256]{1,0:T(8,128)(2,1)} %get-tuple-element.16), channel_id=1, source_target_pairs={{0,16},{16,32},{32,48},{48,64},{64,80},{80,96},{96,112},{112,0},{1... | collective-permute-start | bytes 221192 | tf_op jit(solution)/shard_map/ppermute | solution.py:403
  15.1 22.7 %collective-permute-start.1 = (bf16[144,256]{1,0:T(8,128)(2,1)}, bf16[144,256]{1,0:T(8,128)(2,1)S(1)}, u32[]{:S(2)}, u32[]{:S(2)}) collective-permute-start(bf16[144,256]{1,0:T(8,128)(2,1)} %get-tuple-element.17), channel_id=1, source_target_pairs={{0,112},{16,0},{32,16},{48,32},{64,48},{80,64},{96,80},{112,96},{1... | collective-permute-start | bytes 221192 | tf_op jit(solution)/shard_map/ppermute | solution.py:404
  18.3 19.5 %copy-start = (bf16[216,2048]{1,0:T(8,128)(2,1)S(1)}, bf16[216,2048]{1,0:T(8,128)(2,1)}, u32[]{:S(2)}) copy-start(bf16[216,2048]{1,0:T(8,128)(2,1)} %fs_ref.1) | copy-start | bytes 2654212
  18.3 19.5 %copy-start.1 = (bf16[256,216]{0,1:T(8,128)(2,1)S(1)}, bf16[256,216]{0,1:T(8,128)(2,1)}, u32[]{:S(2)}) copy-start(bf16[256,216]{0,1:T(8,128)(2,1)} %param.29) | copy-start | bytes 331780
  18.3 19.5 %copy-start.2 = (s32[6,2048]{1,0:T(8,128)S(1)}, s32[6,2048]{1,0:T(8,128)}, u32[]{:S(2)}) copy-start(s32[6,2048]{1,0:T(8,128)} %nbr_ref.3) | copy-start | bytes 147460
  18.3 19.5 %copy-start.3 = (bf16[256,32]{0,1:T(8,128)(2,1)S(1)}, bf16[256,32]{0,1:T(8,128)(2,1)}, u32[]{:S(2)}) copy-start(bf16[256,32]{0,1:T(8,128)(2,1)} %param.30) | copy-start | bytes 49156
  18.3 19.5 %copy-start.4 = (bf16[288,216]{1,0:T(8,128)(2,1)S(1)}, bf16[288,216]{1,0:T(8,128)(2,1)}, u32[]{:S(2)}) copy-start(bf16[288,216]{1,0:T(8,128)(2,1)} %constant.42.clone.speed_ref) | copy-start | bytes 373252
  18.3 19.5 %copy-start.5 = (bf16[216,216]{1,0:T(8,128)(2,1)S(1)}, bf16[216,216]{1,0:T(8,128)(2,1)}, u32[]{:S(2)}) copy-start(bf16[216,216]{1,0:T(8,128)(2,1)} %constant.43.clone.order_ref) | copy-start | bytes 279940
  37.8 0.7 copy-start.6
  49.8 2.7 %collective-permute-start.2 = (f32[2048,128]{1,0:T(8,128)S(1)}, f32[2048,128]{1,0:T(8,128)S(1)}, u32[]{:S(2)}, u32[]{:S(2)}) collective-permute-start(f32[2048,128]{1,0:T(8,128)S(1)} %get-tuple-element.23), channel_id=1, source_target_pairs={{0,16},{16,0},{1,17},{17,1},{2,18},{18,2},{3,19},{19,3},{4,20},{20... | collective-permute-start | bytes 3145736 | tf_op jit(solution)/shard_map/ppermute | solution.py:462

commit v6 on v5

--- a/solution.py
+++ b/solution.py
@@ -144,99 +144,68 @@
 
 
 def local_kernel(
-    adj_hbm, vel_hbm, der_hbm, pool_hbm, nbr_ref, tile_ref, slot_ref, base_hbm, gap_hbm, row_ref,
-    adj_all, vel_all, der, pool, mixed, gap_all, adj_sems, vel_sems, pool_sems, der_sem, base_sems, gap_sems,
+    adj_ref, vel_ref, der_ref, nbr_ref, pool_hbm, tile_ref, slot_ref, base_ref, gap_ref, pool, mixed, digits, sems,
 ):
     step = pl.program_id(0)
-    steps, species, nodes, block = adj_all.shape
+    species, nodes, block = adj_ref.shape
+    rows = pool.shape[1]
     group = 16
-
-    def entering(index):
-        cols = pl.ds(pl.multiple_of(index * block, block), block)
-        return (
-            pltpu.make_async_copy(adj_hbm.at[:, :, cols], adj_all.at[index], adj_sems.at[index]),
-            pltpu.make_async_copy(vel_hbm.at[:, :, cols], vel_all.at[index], vel_sems.at[index]),
-        )
-
-    def base_leaving(index):
-        return pltpu.make_async_copy(adj_all.at[index], base_hbm.at[index], base_sems.at[index])
-
-    def gap_leaving(index, f):
-        return pltpu.make_async_copy(gap_all.at[index, f], gap_hbm.at[index, f], gap_sems.at[index, f])
-
-    matrix = pltpu.make_async_copy(der_hbm, der, der_sem.at[0])
-    pools = [pltpu.make_async_copy(pool_hbm.at[f], pool.at[f], pool_sems.at[f]) for f in range(6)]
+    copies = [pltpu.make_async_copy(pool_hbm.at[f], pool.at[f], sems.at[f]) for f in range(6)]
 
     @pl.when(step == 0)
     def _():
-        matrix.start()
-        for copy in (*entering(0), *pools):
+        for copy in copies:
             copy.start()
-        for index in range(1, steps):
-            for copy in entering(index):
-                copy.start()
-        tile_rows(tile_ref, slot_ref, row_ref, block)
-        matrix.wait()
         for d in range(3):
             for b in range(nodes // group):
-                rows = der[d * nodes + b * group : d * nodes + (b + 1) * group, :]
-                mixed[(3 * b + d) * group : (3 * b + d + 1) * group, :] = rows * jnp.asarray(SECTION, BF16)
-
-    for copy in entering(step):
-        copy.wait()
+                lines = der_ref[d * nodes + b * group : d * nodes + (b + 1) * group, :]
+                mixed[(3 * b + d) * group : (3 * b + d + 1) * group, :] = lines * jnp.asarray(SECTION, BF16)
+        digits[...] = slot_digits(slot_ref)
+
     for s in range(species):
-        g = dot(mixed[...], adj_all[step, s].astype(BF16))
+        g = dot(mixed[...], adj_ref[s].astype(BF16))
         for b in range(nodes // group):
-            rows = slice(b * group, (b + 1) * group)
-            total = adj_all[step, s, rows]
+            lines = slice(b * group, (b + 1) * group)
+            total = adj_ref[s, lines]
             for d in range(3):
-                total += vel_all[step, d, rows].astype(F32) * g[(3 * b + d) * group : (3 * b + d + 1) * group]
-            adj_all[step, s, rows] = total
-    base_leaving(step).start()
+                total += vel_ref[d, lines].astype(F32) * g[(3 * b + d) * group : (3 * b + d + 1) * group]
+            base_ref[0, s, lines] = total
+    gap_ref[0, 6 * rows :] = tile_rows(tile_ref[...], digits[...])
 
     @pl.when(step == 0)
     def _():
-        for copy in pools:
+        for copy in copies:
             copy.wait()
 
     cols = pl.ds(pl.multiple_of(step * block, block), block)
     for f in range(6):
-        hot = one_hot(pool.shape[2], nbr_ref[f : f + 1, cols])
-        gap_all[step, f] = dot(pool[f ^ 1], hot) - pool[f, :, cols].astype(F32)
-        gap_leaving(step, f).start()
-
-    @pl.when(step == steps - 1)
-    def _():
-        for index in range(steps):
-            base_leaving(index).wait()
-            for f in range(6):
-                gap_leaving(index, f).wait()
-
-
-def tile_rows(tile_ref, slot_ref, row_ref, block):
-    elements = tile_ref.shape[1]
-    high, lanes = slot_ref.shape
-    fine = lanes // 2
+        hot = one_hot(pool.shape[2], nbr_ref[f : f + 1, :])
+        gap_ref[0, rows * f : rows * (f + 1)] = dot(pool[f ^ 1], hot) - pool[f, :, cols].astype(F32)
+
+
+def slot_digits(slot_ref):
+    fine = slot_ref.shape[1] // 2
     slot = jnp.transpose(slot_ref[...].astype(F32))
     upper = jnp.floor(slot * (1.0 / 64.0))
-    digits = jnp.concatenate([
+    return jnp.concatenate([
         jnp.concatenate([x[:fine], x[fine:]], axis=1) for x in (upper, slot - 64.0 * upper)
     ], axis=0).astype(BF16)
-    bits = fine.bit_length() - 1
-    for c in range(0, elements, block):
-        tile = tile_ref[:, c : c + block]
-        coarse = jnp.right_shift(tile, bits)
-        place = jnp.bitwise_and(coarse, 1) * high + jnp.right_shift(coarse, 1)
-        found = dot(digits, one_hot(2 * high, place))
-        rows = 64.0 * found[:fine] + found[fine:]
-        within = lax.broadcasted_iota(I32, rows.shape, 0) == jnp.bitwise_and(tile, fine - 1)
-        row_ref[:, c : c + block] = jnp.sum(jnp.where(within, rows, 0.0), axis=0, keepdims=True).astype(I32)
+
+
+def tile_rows(tile, digits):
+    fine, high = digits.shape[0] // 2, digits.shape[1] // 2
+    coarse = jnp.right_shift(tile, fine.bit_length() - 1)
+    place = jnp.bitwise_and(coarse, 1) * high + jnp.right_shift(coarse, 1)
+    found = dot(digits, one_hot(2 * high, place))
+    rows = 64.0 * found[:fine] + found[fine:]
+    within = lax.broadcasted_iota(I32, rows.shape, 0) == jnp.bitwise_and(tile, fine - 1)
+    return jnp.broadcast_to(jnp.sum(jnp.where(within, rows, 0.0), axis=0, keepdims=True), (8, tile.shape[1]))
 
 
 def update_kernel(
-    nbr_ref, gap_hbm, recv_ref, below_ref, above_ref, fs_ref, speed_ref, order_ref, lift_ref, prof_ref, base_hbm, row_hbm,
+    nbr_ref, gap_hbm, recv_ref, below_ref, above_ref, fs_ref, speed_ref, order_ref, lift_ref, prof_ref, base_hbm,
     next_hbm, contrib_ref, other_ref, seen_ref, rpool, lift_sorted, flux, low_next, gap_all, base_all, row_ref,
-    sems, next_sems, row_sem, *, elements,
+    sems, next_sems, *, elements,
 ):
     step = pl.program_id(0)
     peers, _, rows, width = recv_ref.shape
@@ -252,8 +221,6 @@
     def leaving(index):
         cols = pl.ds(pl.multiple_of(index * block, block), block)
         return pltpu.make_async_copy(base_all.at[index], next_hbm.at[:, :, cols], next_sems.at[index])
-
-    lines = pltpu.make_async_copy(row_hbm, row_ref, row_sem.at[0])
 
     def contribute(index):
         terms = [dot(prof_ref[...], low_next[s]) for s in range(species)]
@@ -268,7 +235,6 @@
         for index in range(steps):
             for copy in loads(index):
                 copy.start()
-        lines.start()
         low = lax.broadcasted_iota(I32, (rows, width), 1) < half
         for q in range(2):
             for i in range(peers // 2):
@@ -283,6 +249,7 @@
     for copy in loads(step):
         copy.wait()
     gap_ref, base_ref = gap_all.at[step], base_all.at[step]
+    row_ref[:, pl.ds(pl.multiple_of(step * block, block), block)] = gap_ref[6 * rows : 6 * rows + 1].astype(I32)
     contribute(jnp.maximum(step - 1, 0))
     upwind = dot(speed_ref[...], jnp.maximum(fs_ref[...], jnp.zeros((), BF16)))
     slots = peers * half
@@ -298,7 +265,7 @@
                 source = below_ref if t == 5 else above_ref
                 hot = one_hot(source.shape[1], nbr_ref[f : f + 1, :] - (elements + slots))
                 far = dot(source[...], hot)
-            gap = gap_ref[f] + far
+            gap = gap_ref[rows * f : rows * (f + 1)] + far
             speed = upwind[MAIN * f : MAIN * (f + 1)]
             mains.append([speed * gap[MAIN * s : MAIN * (s + 1)] for s in range(species)])
             line = 6 * MAIN + species * REST * f
@@ -322,7 +289,6 @@
     @pl.when(step == steps - 1)
     def _():
         contribute(step)
-        lines.wait()
         seen_ref[...] = row_ref[...]
         scatter(row_ref, contrib_ref, other_ref, True)
         for index in range(steps):
@@ -403,25 +369,31 @@
     from_below = lax.ppermute(up, ("z", "core"), ring_up)
     from_above = lax.ppermute(down, ("z", "core"), ring_down)
 
-    base, gap, tile_row = pl.pallas_call(
+    base, gap = pl.pallas_call(
         local_kernel,
         grid=(steps,),
-        in_specs=[hbm] * 4 + [whole(6, elements), whole(1, elements), whole(tiles // 128, 128)],
-        out_specs=[hbm, hbm, whole(1, elements)],
-        out_shape=[
-            sds((steps, species, nodes, block), F32), sds((steps, 6, rows, block), F32), sds((1, elements), I32),
-        ],
+        in_specs=[
+            pl.BlockSpec((species, nodes, block), lambda i: (0, 0, i)),
+            pl.BlockSpec((3, nodes, block), lambda i: (0, 0, i)),
+            whole(3 * nodes, nodes),
+            pl.BlockSpec((6, block), lambda i: (0, i)),
+            hbm,
+            pl.BlockSpec((1, block), lambda i: (0, i)), whole(tiles // 128, 128),
+        ],
+        out_specs=[
+            pl.BlockSpec((1, species, nodes, block), lambda i: (i, 0, 0, 0)),
+            pl.BlockSpec((1, 6 * rows + 8, block), lambda i: (i, 0, 0)),
+        ],
+        out_shape=[sds((steps, species, nodes, block), F32), sds((steps, 6 * rows + 8, block), F32)],
         scratch_shapes=[
-            pltpu.VMEM((steps, species, nodes, block), F32), pltpu.VMEM((steps, 3, nodes, block), BF16),
-            pltpu.VMEM((3 * nodes, nodes), BF16), pltpu.VMEM((6, rows, elements), BF16),
-            pltpu.VMEM((3 * nodes, nodes), BF16), pltpu.VMEM((steps, 6, rows, block), F32),
-            *(pltpu.SemaphoreType.DMA(shape) for shape in ((steps,), (steps,), (6,), (1,), (steps,), (steps, 6))),
+            pltpu.VMEM((6, rows, elements), BF16), pltpu.VMEM((3 * nodes, nodes), BF16),
+            pltpu.VMEM((128, 2 * tiles // 128), BF16), pltpu.SemaphoreType.DMA((6,)),
         ],
         compiler_params=params(60),
         cost_estimate=cost(16_000_000_000, 32_000_000),
         name="local",
     )(
-        adjoint, velocity, derivatives, pool, neighbours, element_tile.reshape(1, elements),
+        adjoint, velocity, derivatives, neighbours, pool, element_tile.reshape(1, elements),
         tile_slot.reshape(tiles // 128, 128),
     )
 
@@ -435,7 +407,7 @@
             hbm, whole(peers, 2, rows, 2 * half), whole(rows, vcap), whole(rows, vcap),
             pl.BlockSpec((face_rows, block), lambda i: (0, i)),
             whole(2 * rows, face_rows), whole(face_rows, face_rows), whole(face_rows, nodes), whole(heights, nodes),
-            hbm, hbm,
+            hbm,
         ],
         out_specs=[
             hbm, whole(elements, 2 * width), whole(tiles // 2, width), whole(1, elements),
@@ -447,16 +419,16 @@
         scratch_shapes=[
             pltpu.VMEM((4, rows, slots), BF16), pltpu.VMEM((nodes, face_rows), BF16),
             pltpu.VMEM((species, face_rows, block), BF16), pltpu.VMEM((species, nodes, block), BF16),
-            pltpu.VMEM((steps, 6, rows, block), F32), pltpu.VMEM((steps, species, nodes, block), F32),
+            pltpu.VMEM((steps, 6 * rows + 8, block), F32), pltpu.VMEM((steps, species, nodes, block), F32),
             pltpu.VMEM((1, elements), I32),
-            pltpu.SemaphoreType.DMA((2, steps)), pltpu.SemaphoreType.DMA((steps,)), pltpu.SemaphoreType.DMA((1,)),
+            pltpu.SemaphoreType.DMA((2, steps)), pltpu.SemaphoreType.DMA((steps,)),
         ],
         compiler_params=params(UPDATE_MIB),
         cost_estimate=cost(8_000_000_000, 28_000_000),
         name="update",
     )(
         neighbours, gap, received, from_below, from_above, face_speed, speed_picker(species, face_nodes),
-        lift_picker(face_nodes), lift_operator.T, emission_profile.T, base, tile_row,
+        lift_picker(face_nodes), lift_operator.T, emission_profile.T, base,
     )
 
     theirs = lax.ppermute(for_other, "core", [(0, 1), (1, 0)])

time: 77.3 us -> 74.8 us (0.968)
  Pallas kernels: 40.2 us -> 38.4 us
    pallas_call x1, Pallas kernels: 19.4 us -> 17.1 us  [on_device(): pl.pallas_call(local_kernel, grid=(steps,), in_specs=[pl.BlockSpec((speci...]
  transfers between devices with their start and end apart: 4 -> 4, of which waited for: 1 -> 1; matrix products, arithmetic and copies ran while one was open for 0% -> 0% of each run, Pallas kernels for 28% -> 26%
where the time goes in v6:
time: 74.8 us; the launch traced here: 74.5 us
  Pallas kernels  38.4 us (51%)
  blocking collectives  23.6 us (32%)
  starting transfers between devices  10.5 us (14%)
  other arithmetic  0.81 us (1%)
  between operations  0.78 us (1%)
    all_to_all x1, blocking collectives, on_device(): lax.all_to_all(partial.reshape(chips, tiles // 2 // chips, width), ('z',...  23.6 us
    pallas_call x1, Pallas kernels, on_device(): pl.pallas_call(local_kernel, grid=(steps,), in_specs=[pl.BlockSpec((speci...  17.1 us
    pallas_call x1, Pallas kernels, on_device(): pl.pallas_call(functools.partial(update_kernel, elements=elements), grid=...  11.7 us
    pallas_call x1, Pallas kernels, on_device(): pl.pallas_call(send_kernel, in_specs=[hbm] * 5, out_specs=[hbm] * 4, out_...  7.33 us
    all_to_all x1, starting transfers between devices, on_device(): lax.all_to_all(send, 'sub', split_axis=0, concat_axis=0, tiled=True)  7.16 us
    ppermute x1, starting transfers between devices, on_device(): from_above = lax.ppermute(down, ('z', 'core'), ring_down)  3.21 us
    pallas_call x1, Pallas kernels, on_device(): pl.pallas_call(own_kernel, in_specs=[vmem] * 2, out_specs=vmem, out_shape...  2.32 us
  transfers between devices with their start and end apart: 4, of which 1 were waited for; matrix products, arithmetic and copies ran while one was open for 0% of the time, Pallas kernels for 26%

profile of v6, /device:TPU:0, one launch (start us, length us, event | category | flops | bytes accessed | tf_op | source)
XLA Modules:
  0.0 74.5 jit_solution(12105214889258733673)
XLA Ops:
  0.6 7.3 %sends.1 = (bf16[6,144,2048]{2,1,0:T(8,128)(2,1)}, bf16[16,2,144,128]{3,2,1,0:T(8,128)(2,1)}, bf16[144,256]{1,0:T(8,128)(2,1)}, bf16[144,256]{1,0:T(8,128)(2,1)}) custom-call(f32[4,256,2048]{2,1,0:T(8,128)} %adj_ref.1, bf16[2,4,48,40]{3,2,1,0:T(8,128)(2,1)} %constant.56.near_hbm, bf16[4,192,216]{2,1,0:T(8,128)(2,1)} %constant.61.far_hbm, s32[4,1024]{1,0:T(4,128)} %ss_hbm.1, ...), custom_call_target="tpu_custom_call" | custom-call | flops 12000000000 | bytes 14000000 | tf_op jit(solution)/shard_map/sends/pallas_call | solution.py:349
  8.0 7.2 %all-to-all-start = ((bf16[16,2,144,128]{3,2,1,0:T(8,128)(2,1)}), bf16[16,2,144,128]{3,2,1,0:T(8,128)(2,1)S(1)}, u32[]{:S(2)}, u32[]{:S(2)}) async-start(bf16[16,2,144,128]{3,2,1,0:T(8,128)(2,1)} %get-tuple-element.14), calls=%async_computation | async-start | bytes 2359296 | tf_op jit(solution)/shard_map/all_to_all | solution.py:366
  15.1 0.0 collective-permute-start
  15.2 3.2 %collective-permute-start.1 = (bf16[144,256]{1,0:T(8,128)(2,1)}, bf16[144,256]{1,0:T(8,128)(2,1)S(1)}, u32[]{:S(2)}, u32[]{:S(2)}) collective-permute-start(bf16[144,256]{1,0:T(8,128)(2,1)} %get-tuple-element.16), channel_id=1, source_target_pairs={{0,112},{16,0},{32,16},{48,32},{64,48},{80,64},{96,80},{112,96},{1... | collective-permute-start | bytes 221192 | tf_op jit(solution)/shard_map/ppermute | solution.py:370
  18.4 0.0 copy-start
  18.4 0.0 copy-start.1
  18.4 0.0 copy-start.2
  18.4 0.0 copy-start.3
  18.4 0.0 copy-start.4
  18.4 0.0 copy-start.5
  18.4 17.1 %local.1 = (f32[4,4,256,512]{3,2,1,0:T(8,128)}, f32[4,872,512]{2,1,0:T(8,128)}) custom-call(f32[4,256,2048]{2,1,0:T(8,128)} %adj_ref.1, bf16[3,256,2048]{2,1,0:T(8,128)(2,1)} %vel_ref.1, bf16[768,256]{1,0:T(8,128)(2,1)} %der_ref.1, s32[6,2048]{1,0:T(8,128)} %nbr_ref.3, bf16[6,144,2048]{2,1,0:T(8,128)(2,1)} %get-tuple-element.12.pool_hbm, s32[1,2048]{1,0:T(1,128)} %bitcast.9, ...), custom_call_target="tpu_custom_call" | custom-call | flops 16000000000 | bytes 32000000 | tf_op jit(solution)/shard_map/local/pallas_call | solution.py:372
  35.5 0.0 collective-permute-done.below_ref
  35.5 0.0 collective-permute-done.1.above_ref
  35.5 0.0 all-to-all-done.recv_ref
  35.5 0.0 copy-done
  35.5 0.0 copy-done.1
  35.5 0.0 copy-done.2
  35.5 0.0 copy-done.3
  35.6 0.0 copy-done.4
  35.6 0.0 copy-done.5
  35.6 11.7 %update.1 = (f32[4,256,2048]{2,1,0:T(8,128)}, bf16[2048,256]{1,0:T(8,128)(2,1)S(1)}, f32[2048,128]{1,0:T(8,128)S(1)}, s32[1,2048]{1,0:T(1,128)S(1)}) custom-call(s32[6,2048]{1,0:T(8,128)S(1)} %copy-done.2, f32[4,872,512]{2,1,0:T(8,128)} %get-tuple-element.13.gap_hbm, bf16[16,2,144,128]{3,2,1,0:T(8,128)(2,1)S(1)} %all-to-all-done.recv_ref, ...), custom_call_target="tpu_custom_call" | custom-call | flops 8000000000 | bytes 28000000 | tf_op jit(solution)/shard_map/update/pallas_call | solution.py:402
  47.3 0.1 collective-permute-start.2
  47.4 2.3 %scatter_own.1 = f32[2048,128]{1,0:T(8,128)S(1)} custom-call(s32[1,2048]{1,0:T(1,128)S(1)} %get-tuple-element.19.row_ref, bf16[2048,256]{1,0:T(8,128)(2,1)S(1)} %get-tuple-element.20.contrib_ref), custom_call_target="tpu_custom_call" | custom-call | flops 2100000000 | bytes 2000000 | tf_op jit(solution)/shard_map/scatter_own/pallas_call | solution.py:435
  49.7 0.3 collective-permute-done.2
  50.0 0.1 add_convert_fusion
  50.1 23.6 %all_to_all.10 = bf16[64,32,128]{2,1,0:T(8,128)(2,1)S(1)} all-to-all(bf16[64,32,128]{2,1,0:T(8,128)(2,1)S(1)} %bitcast.7), channel_id=1, replica_groups=mesh['z'=4,'core'=2,'sub'=16] {'z','sub'}, dimensions={0} | all-to-all | bytes 1048576 | tf_op jit(solution)/shard_map/all_to_all | solution.py:446
  73.8 0.7 convert_reduce_fusion
Async XLA Ops:
  8.0 27.5 %all-to-all-start = ((bf16[16,2,144,128]{3,2,1,0:T(8,128)(2,1)}), bf16[16,2,144,128]{3,2,1,0:T(8,128)(2,1)S(1)}, u32[]{:S(2)}, u32[]{:S(2)}) async-start(bf16[16,2,144,128]{3,2,1,0:T(8,128)(2,1)} %get-tuple-element.14), calls=%async_computation | async-start | bytes 2359296 | tf_op jit(solution)/shard_map/all_to_all | solution.py:366
  15.1 20.4 %collective-permute-start = (bf16[144,256]{1,0:T(8,128)(2,1)}, bf16[144,256]{1,0:T(8,128)(2,1)S(1)}, u32[]{:S(2)}, u32[]{:S(2)}) collective-permute-start(bf16[144,256]{1,0:T(8,128)(2,1)} %get-tuple-element.15), channel_id=1, source_target_pairs={{0,16},{16,32},{32,48},{48,64},{64,80},{80,96},{96,112},{112,0},{1... | collective-permute-start | bytes 221192 | tf_op jit(solution)/shard_map/ppermute | solution.py:369
  15.2 20.3 %collective-permute-start.1 = (bf16[144,256]{1,0:T(8,128)(2,1)}, bf16[144,256]{1,0:T(8,128)(2,1)S(1)}, u32[]{:S(2)}, u32[]{:S(2)}) collective-permute-start(bf16[144,256]{1,0:T(8,128)(2,1)} %get-tuple-element.16), channel_id=1, source_target_pairs={{0,112},{16,0},{32,16},{48,32},{64,48},{80,64},{96,80},{112,96},{1... | collective-permute-start | bytes 221192 | tf_op jit(solution)/shard_map/ppermute | solution.py:370
  18.4 17.2 %copy-start = (bf16[216,2048]{1,0:T(8,128)(2,1)S(1)}, bf16[216,2048]{1,0:T(8,128)(2,1)}, u32[]{:S(2)}) copy-start(bf16[216,2048]{1,0:T(8,128)(2,1)} %fs_ref.1) | copy-start | bytes 2654212
  18.4 17.2 %copy-start.1 = (bf16[256,216]{0,1:T(8,128)(2,1)S(1)}, bf16[256,216]{0,1:T(8,128)(2,1)}, u32[]{:S(2)}) copy-start(bf16[256,216]{0,1:T(8,128)(2,1)} %param.29) | copy-start | bytes 331780
  18.4 17.2 %copy-start.2 = (s32[6,2048]{1,0:T(8,128)S(1)}, s32[6,2048]{1,0:T(8,128)}, u32[]{:S(2)}) copy-start(s32[6,2048]{1,0:T(8,128)} %nbr_ref.3) | copy-start | bytes 147460
  18.4 17.2 %copy-start.3 = (bf16[256,32]{0,1:T(8,128)(2,1)S(1)}, bf16[256,32]{0,1:T(8,128)(2,1)}, u32[]{:S(2)}) copy-start(bf16[256,32]{0,1:T(8,128)(2,1)} %param.30) | copy-start | bytes 49156
  18.4 17.2 %copy-start.4 = (bf16[288,216]{1,0:T(8,128)(2,1)S(1)}, bf16[288,216]{1,0:T(8,128)(2,1)}, u32[]{:S(2)}) copy-start(bf16[288,216]{1,0:T(8,128)(2,1)} %constant.42.clone.speed_ref) | copy-start | bytes 373252
  18.4 17.2 %copy-start.5 = (bf16[216,216]{1,0:T(8,128)(2,1)S(1)}, bf16[216,216]{1,0:T(8,128)(2,1)}, u32[]{:S(2)}) copy-start(bf16[216,216]{1,0:T(8,128)(2,1)} %constant.43.clone.order_ref) | copy-start | bytes 279940
  47.3 2.7 %collective-permute-start.2 = (f32[2048,128]{1,0:T(8,128)S(1)}, f32[2048,128]{1,0:T(8,128)S(1)}, u32[]{:S(2)}, u32[]{:S(2)}) collective-permute-start(f32[2048,128]{1,0:T(8,128)S(1)} %get-tuple-element.21), channel_id=1, source_target_pairs={{0,16},{16,0},{1,17},{17,1},{2,18},{18,2},{3,19},{19,3},{4,20},{20... | collective-permute-start | bytes 3145736 | tf_op jit(solution)/shard_map/ppermute | solution.py:434

commit v7 on v6

--- a/solution.py
+++ b/solution.py
@@ -226,7 +226,7 @@
         terms = [dot(prof_ref[...], low_next[s]) for s in range(species)]
         contrib = jnp.transpose(jnp.concatenate(terms, axis=0))
         high = contrib.astype(BF16)
-        lines = pl.ds(pl.multiple_of(index * block, block), block)
+        lines = pl.ds(index * block if isinstance(index, int) else pl.multiple_of(index * block, block), block)
         contrib_ref[lines, : contrib.shape[1]] = high
         contrib_ref[lines, contrib.shape[1] :] = (contrib - high.astype(F32)).astype(BF16)
 
@@ -235,14 +235,12 @@
         for index in range(steps):
             for copy in loads(index):
                 copy.start()
-        low = lax.broadcasted_iota(I32, (rows, width), 1) < half
         for q in range(2):
             for i in range(peers // 2):
                 lanes = slice(width * i, width * (i + 1))
-                x = recv_ref[2 * i, q].astype(F32)
-                y = recv_ref[2 * i + 1, q].astype(F32)
-                rpool[2 * q, :, lanes] = jnp.where(low, x, pltpu.roll(y, half, 1)).astype(BF16)
-                rpool[2 * q + 1, :, lanes] = jnp.where(low, pltpu.roll(x, half, 1), y).astype(BF16)
+                x, y = recv_ref[2 * i, q], recv_ref[2 * i + 1, q]
+                rpool[2 * q, :, lanes] = jnp.concatenate([x[:, :half], y[:, :half]], axis=1)
+                rpool[2 * q + 1, :, lanes] = jnp.concatenate([x[:, half:], y[:, half:]], axis=1)
         lift_sorted[...] = (SECTION * jnp.transpose(dot(order_ref[...], lift_ref[...]))).astype(BF16)
         low_next[...] = jnp.zeros_like(low_next)
 
@@ -288,20 +286,22 @@
 
     @pl.when(step == steps - 1)
     def _():
-        contribute(step)
+        contribute(steps - 1)
         seen_ref[...] = row_ref[...]
-        scatter(row_ref, contrib_ref, other_ref, True)
+        scatter(row_ref, contrib_ref, other_ref, True, elements - block)
         for index in range(steps):
             leaving(index).wait()
 
 
-def scatter(row_ref, contrib_ref, out_ref, other):
+def scatter(row_ref, contrib_ref, out_ref, other, cut=0):
     width = out_ref.shape[1]
     core = lax.axis_index("core")
     side = 1 - core if other else core
     for i in range(out_ref.shape[0] // GROUP_ROWS):
-        hot = one_hot(GROUP_ROWS, row_ref[...] - (2 * i + side) * GROUP_ROWS)
-        both = dot(hot, contrib_ref[...])
+        lines = row_ref[...] - (2 * i + side) * GROUP_ROWS
+        both = dot(one_hot(GROUP_ROWS, lines[:, cut:]), contrib_ref[cut:])
+        if cut:
+            both = dot(one_hot(GROUP_ROWS, lines[:, :cut]), contrib_ref[:cut]) + both
         out_ref[i * GROUP_ROWS : (i + 1) * GROUP_ROWS, :] = both[:, :width] + both[:, width:]
 
 

time: 74.8 us -> 74.3 us (level)
  no operation moved by 1% of the time
where the time goes in v7:
time: 74.3 us; the launch traced here: 74 us
  Pallas kernels  38 us (51%)
  blocking collectives  23.6 us (32%)
  starting transfers between devices  10.5 us (14%)
  other arithmetic  0.81 us (1%)
  between operations  0.78 us (1%)
    all_to_all x1, blocking collectives, on_device(): lax.all_to_all(partial.reshape(chips, tiles // 2 // chips, width), ('z',...  23.6 us
    pallas_call x1, Pallas kernels, on_device(): pl.pallas_call(local_kernel, grid=(steps,), in_specs=[pl.BlockSpec((speci...  17.1 us
    pallas_call x1, Pallas kernels, on_device(): pl.pallas_call(functools.partial(update_kernel, elements=elements), grid=...  11.2 us
    pallas_call x1, Pallas kernels, on_device(): pl.pallas_call(send_kernel, in_specs=[hbm] * 5, out_specs=[hbm] * 4, out_...  7.33 us
    all_to_all x1, starting transfers between devices, on_device(): lax.all_to_all(send, 'sub', split_axis=0, concat_axis=0, tiled=True)  7.16 us
    ppermute x1, starting transfers between devices, on_device(): from_above = lax.ppermute(down, ('z', 'core'), ring_down)  3.21 us
    pallas_call x1, Pallas kernels, on_device(): pl.pallas_call(own_kernel, in_specs=[vmem] * 2, out_specs=vmem, out_shape...  2.32 us
  transfers between devices with their start and end apart: 4, of which 1 were waited for; matrix products, arithmetic and copies ran while one was open for 0% of the time, Pallas kernels for 26%

profile of v7, /device:TPU:0, one launch (start us, length us, event | category | flops | bytes accessed | tf_op | source)
XLA Modules:
  0.0 74.0 jit_solution(16067324189624246729)
XLA Ops:
  0.6 7.3 %sends.1 = (bf16[6,144,2048]{2,1,0:T(8,128)(2,1)}, bf16[16,2,144,128]{3,2,1,0:T(8,128)(2,1)}, bf16[144,256]{1,0:T(8,128)(2,1)}, bf16[144,256]{1,0:T(8,128)(2,1)}) custom-call(f32[4,256,2048]{2,1,0:T(8,128)} %adj_ref.1, bf16[2,4,48,40]{3,2,1,0:T(8,128)(2,1)} %constant.56.near_hbm, bf16[4,192,216]{2,1,0:T(8,128)(2,1)} %constant.61.far_hbm, s32[4,1024]{1,0:T(4,128)} %ss_hbm.1, ...), custom_call_target="tpu_custom_call" | custom-call | flops 12000000000 | bytes 14000000 | tf_op jit(solution)/shard_map/sends/pallas_call | solution.py:349
  8.0 7.2 %all-to-all-start = ((bf16[16,2,144,128]{3,2,1,0:T(8,128)(2,1)}), bf16[16,2,144,128]{3,2,1,0:T(8,128)(2,1)S(1)}, u32[]{:S(2)}, u32[]{:S(2)}) async-start(bf16[16,2,144,128]{3,2,1,0:T(8,128)(2,1)} %get-tuple-element.14), calls=%async_computation | async-start | bytes 2359296 | tf_op jit(solution)/shard_map/all_to_all | solution.py:366
  15.1 0.0 collective-permute-start
  15.2 3.2 %collective-permute-start.1 = (bf16[144,256]{1,0:T(8,128)(2,1)}, bf16[144,256]{1,0:T(8,128)(2,1)S(1)}, u32[]{:S(2)}, u32[]{:S(2)}) collective-permute-start(bf16[144,256]{1,0:T(8,128)(2,1)} %get-tuple-element.16), channel_id=1, source_target_pairs={{0,112},{16,0},{32,16},{48,32},{64,48},{80,64},{96,80},{112,96},{1... | collective-permute-start | bytes 221192 | tf_op jit(solution)/shard_map/ppermute | solution.py:370
  18.4 0.0 copy-start
  18.4 0.0 copy-start.1
  18.4 0.0 copy-start.2
  18.4 0.0 copy-start.3
  18.4 0.0 copy-start.4
  18.4 0.0 copy-start.5
  18.4 17.1 %local.1 = (f32[4,4,256,512]{3,2,1,0:T(8,128)}, f32[4,872,512]{2,1,0:T(8,128)}) custom-call(f32[4,256,2048]{2,1,0:T(8,128)} %adj_ref.1, bf16[3,256,2048]{2,1,0:T(8,128)(2,1)} %vel_ref.1, bf16[768,256]{1,0:T(8,128)(2,1)} %der_ref.1, s32[6,2048]{1,0:T(8,128)} %nbr_ref.3, bf16[6,144,2048]{2,1,0:T(8,128)(2,1)} %get-tuple-element.12.pool_hbm, s32[1,2048]{1,0:T(1,128)} %bitcast.9, ...), custom_call_target="tpu_custom_call" | custom-call | flops 16000000000 | bytes 32000000 | tf_op jit(solution)/shard_map/local/pallas_call | solution.py:372
  35.5 0.0 collective-permute-done.below_ref
  35.5 0.0 collective-permute-done.1.above_ref
  35.5 0.0 all-to-all-done.recv_ref
  35.5 0.0 copy-done
  35.5 0.0 copy-done.1
  35.5 0.0 copy-done.2
  35.5 0.0 copy-done.3
  35.6 0.0 copy-done.4
  35.6 0.0 copy-done.5
  35.6 11.2 %update.1 = (f32[4,256,2048]{2,1,0:T(8,128)}, bf16[2048,256]{1,0:T(8,128)(2,1)S(1)}, f32[2048,128]{1,0:T(8,128)S(1)}, s32[1,2048]{1,0:T(1,128)S(1)}) custom-call(s32[6,2048]{1,0:T(8,128)S(1)} %copy-done.2, f32[4,872,512]{2,1,0:T(8,128)} %get-tuple-element.13.gap_hbm, bf16[16,2,144,128]{3,2,1,0:T(8,128)(2,1)S(1)} %all-to-all-done.recv_ref, ...), custom_call_target="tpu_custom_call" | custom-call | flops 8000000000 | bytes 28000000 | tf_op jit(solution)/shard_map/update/pallas_call | solution.py:402
  46.8 0.1 collective-permute-start.2
  46.9 2.3 %scatter_own.1 = f32[2048,128]{1,0:T(8,128)S(1)} custom-call(s32[1,2048]{1,0:T(1,128)S(1)} %get-tuple-element.19.row_ref, bf16[2048,256]{1,0:T(8,128)(2,1)S(1)} %get-tuple-element.20.contrib_ref), custom_call_target="tpu_custom_call" | custom-call | flops 2100000000 | bytes 2000000 | tf_op jit(solution)/shard_map/scatter_own/pallas_call | solution.py:435
  49.2 0.3 collective-permute-done.2
  49.6 0.1 add_convert_fusion
  49.7 23.6 %all_to_all.10 = bf16[64,32,128]{2,1,0:T(8,128)(2,1)S(1)} all-to-all(bf16[64,32,128]{2,1,0:T(8,128)(2,1)S(1)} %bitcast.7), channel_id=1, replica_groups=mesh['z'=4,'core'=2,'sub'=16] {'z','sub'}, dimensions={0} | all-to-all | bytes 1048576 | tf_op jit(solution)/shard_map/all_to_all | solution.py:446
  73.3 0.7 convert_reduce_fusion
Async XLA Ops:
  8.0 27.5 %all-to-all-start = ((bf16[16,2,144,128]{3,2,1,0:T(8,128)(2,1)}), bf16[16,2,144,128]{3,2,1,0:T(8,128)(2,1)S(1)}, u32[]{:S(2)}, u32[]{:S(2)}) async-start(bf16[16,2,144,128]{3,2,1,0:T(8,128)(2,1)} %get-tuple-element.14), calls=%async_computation | async-start | bytes 2359296 | tf_op jit(solution)/shard_map/all_to_all | solution.py:366
  15.1 20.4 %collective-permute-start = (bf16[144,256]{1,0:T(8,128)(2,1)}, bf16[144,256]{1,0:T(8,128)(2,1)S(1)}, u32[]{:S(2)}, u32[]{:S(2)}) collective-permute-start(bf16[144,256]{1,0:T(8,128)(2,1)} %get-tuple-element.15), channel_id=1, source_target_pairs={{0,16},{16,32},{32,48},{48,64},{64,80},{80,96},{96,112},{112,0},{1... | collective-permute-start | bytes 221192 | tf_op jit(solution)/shard_map/ppermute | solution.py:369
  15.2 20.3 %collective-permute-start.1 = (bf16[144,256]{1,0:T(8,128)(2,1)}, bf16[144,256]{1,0:T(8,128)(2,1)S(1)}, u32[]{:S(2)}, u32[]{:S(2)}) collective-permute-start(bf16[144,256]{1,0:T(8,128)(2,1)} %get-tuple-element.16), channel_id=1, source_target_pairs={{0,112},{16,0},{32,16},{48,32},{64,48},{80,64},{96,80},{112,96},{1... | collective-permute-start | bytes 221192 | tf_op jit(solution)/shard_map/ppermute | solution.py:370
  18.4 17.2 %copy-start = (bf16[216,2048]{1,0:T(8,128)(2,1)S(1)}, bf16[216,2048]{1,0:T(8,128)(2,1)}, u32[]{:S(2)}) copy-start(bf16[216,2048]{1,0:T(8,128)(2,1)} %fs_ref.1) | copy-start | bytes 2654212
  18.4 17.2 %copy-start.1 = (bf16[256,216]{0,1:T(8,128)(2,1)S(1)}, bf16[256,216]{0,1:T(8,128)(2,1)}, u32[]{:S(2)}) copy-start(bf16[256,216]{0,1:T(8,128)(2,1)} %param.29) | copy-start | bytes 331780
  18.4 17.2 %copy-start.2 = (s32[6,2048]{1,0:T(8,128)S(1)}, s32[6,2048]{1,0:T(8,128)}, u32[]{:S(2)}) copy-start(s32[6,2048]{1,0:T(8,128)} %nbr_ref.3) | copy-start | bytes 147460
  18.4 17.2 %copy-start.3 = (bf16[256,32]{0,1:T(8,128)(2,1)S(1)}, bf16[256,32]{0,1:T(8,128)(2,1)}, u32[]{:S(2)}) copy-start(bf16[256,32]{0,1:T(8,128)(2,1)} %param.30) | copy-start | bytes 49156
  18.4 17.2 %copy-start.4 = (bf16[288,216]{1,0:T(8,128)(2,1)S(1)}, bf16[288,216]{1,0:T(8,128)(2,1)}, u32[]{:S(2)}) copy-start(bf16[288,216]{1,0:T(8,128)(2,1)} %constant.42.clone.speed_ref) | copy-start | bytes 373252
  18.4 17.2 %copy-start.5 = (bf16[216,216]{1,0:T(8,128)(2,1)S(1)}, bf16[216,216]{1,0:T(8,128)(2,1)}, u32[]{:S(2)}) copy-start(bf16[216,216]{1,0:T(8,128)(2,1)} %constant.43.clone.order_ref) | copy-start | bytes 279940
  46.8 2.7 %collective-permute-start.2 = (f32[2048,128]{1,0:T(8,128)S(1)}, f32[2048,128]{1,0:T(8,128)S(1)}, u32[]{:S(2)}, u32[]{:S(2)}) collective-permute-start(f32[2048,128]{1,0:T(8,128)S(1)} %get-tuple-element.21), channel_id=1, source_target_pairs={{0,16},{16,0},{1,17},{17,1},{2,18},{18,2},{3,19},{19,3},{4,20},{20... | collective-permute-start | bytes 3145736 | tf_op jit(solution)/shard_map/ppermute | solution.py:434

commit v8 on v7

--- a/solution.py
+++ b/solution.py
@@ -81,8 +81,8 @@
 
 
 def send_kernel(
-    adj_hbm, near_hbm, far_hbm, ss_hbm, gs_hbm, pool_hbm, send_hbm, up_hbm, down_hbm,
-    adj, near_ref, far_ref, ss_ref, gs_ref, pool_ref, send_ref, up_ref, down_ref, in_sems, pool_sems, out_sems,
+    adj_hbm, near_hbm, far_hbm, ss_hbm, gs_hbm, pool_hbm, send_hbm, mate_hbm, next_hbm,
+    adj, near_ref, far_ref, ss_ref, gs_ref, pool_ref, send_ref, mate_ref, next_ref, in_sems, pool_sems, out_sems,
 ):
     species = adj.shape[0]
     rows, elements = pool_ref.shape[1:]
@@ -133,11 +133,12 @@
     fill((2, 3, 4, 5), far_ref[...], 0, HIGH[1], 512)
     for f in (2, 3, 4, 5):
         leave(pool_ref.at[f], pool_hbm.at[f], pool_sems.at[f])
-    down_ref[...] = dot(pool_ref[4], one_hot(elements, gs_ref[0:1, :])).astype(BF16)
-    up_ref[...] = dot(pool_ref[5], one_hot(elements, gs_ref[1:2, :])).astype(BF16)
+    core = lax.axis_index("core")
+    for target, upper in ((mate_ref, 1 - core), (next_ref, core)):
+        target[...] = dot(pool_ref[4 + upper], one_hot(elements, gs_ref[pl.ds(upper, 1), :])).astype(BF16)
     exchange(1)
-    leave(down_ref, down_hbm, out_sems.at[1])
-    leave(up_ref, up_hbm, out_sems.at[2])
+    leave(mate_ref, mate_hbm, out_sems.at[1])
+    leave(next_ref, next_hbm, out_sems.at[2])
     leave(send_ref.at[:, 1], send_hbm.at[:, 1], out_sems.at[3])
     for copy in leaving:
         copy.wait()
@@ -203,7 +204,7 @@
 
 
 def update_kernel(
-    nbr_ref, gap_hbm, recv_ref, below_ref, above_ref, fs_ref, speed_ref, order_ref, lift_ref, prof_ref, base_hbm,
+    nbr_ref, gap_hbm, recv_ref, mate_ref, near_ref, fs_ref, speed_ref, order_ref, lift_ref, prof_ref, base_hbm,
     next_hbm, contrib_ref, other_ref, seen_ref, rpool, lift_sorted, flux, low_next, gap_all, base_all, row_ref,
     sems, next_sems, *, elements,
 ):
@@ -251,6 +252,7 @@
     contribute(jnp.maximum(step - 1, 0))
     upwind = dot(speed_ref[...], jnp.maximum(fs_ref[...], jnp.zeros((), BF16)))
     slots = peers * half
+    core = lax.axis_index("core")
     first = lax.broadcasted_iota(I32, (2 * REST, block), 0) < REST
     tails = [[] for _ in range(species)]
     for q in range(3):
@@ -260,9 +262,10 @@
             if t < 4:
                 far = dot(rpool[t], one_hot(slots, nbr_ref[f : f + 1, :] - elements))
             else:
-                source = below_ref if t == 5 else above_ref
+                mine = core == (1 if t == 5 else 0)
+                source = jnp.where(mine, mate_ref[...].astype(F32), near_ref[...].astype(F32)).astype(BF16)
                 hot = one_hot(source.shape[1], nbr_ref[f : f + 1, :] - (elements + slots))
-                far = dot(source[...], hot)
+                far = dot(source, hot)
             gap = gap_ref[rows * f : rows * (f + 1)] + far
             speed = upwind[MAIN * f : MAIN * (f + 1)]
             mains.append([speed * gap[MAIN * s : MAIN * (s + 1)] for s in range(species)])
@@ -346,7 +349,7 @@
     made = [
         sds((6, rows, elements), BF16), sds((peers, 2, rows, 2 * half), BF16), sds((rows, vcap), BF16), sds((rows, vcap), BF16),
     ]
-    pool, send, up, down = pl.pallas_call(
+    pool, send, for_mate, for_next = pl.pallas_call(
         send_kernel,
         in_specs=[hbm] * 5,
         out_specs=[hbm] * 4,
@@ -364,10 +367,9 @@
     )
 
     received = lax.all_to_all(send, "sub", split_axis=0, concat_axis=0, tiled=True)
-    ring_up = [(g, (g + 1) % groups) for g in range(groups)]
-    ring_down = [(g, (g - 1) % groups) for g in range(groups)]
-    from_below = lax.ppermute(up, ("z", "core"), ring_up)
-    from_above = lax.ppermute(down, ("z", "core"), ring_down)
+    across = [(g, (g + 1 if g % 2 else g - 1) % groups) for g in range(groups)]
+    from_mate = lax.ppermute(for_mate, "core", [(0, 1), (1, 0)])
+    from_next = lax.ppermute(for_next, ("z", "core"), across)
 
     base, gap = pl.pallas_call(
         local_kernel,
@@ -427,7 +429,7 @@
         cost_estimate=cost(8_000_000_000, 28_000_000),
         name="update",
     )(
-        neighbours, gap, received, from_below, from_above, face_speed, speed_picker(species, face_nodes),
+        neighbours, gap, received, from_mate, from_next, face_speed, speed_picker(species, face_nodes),
         lift_picker(face_nodes), lift_operator.T, emission_profile.T, base,
     )
 

time: 74.3 us -> 74.1 us (level)
  blocking collectives: 23.6 us -> 22.4 us
  starting transfers between devices: 10.5 us -> 11.5 us
    all_to_all x1, blocking collectives: 23.6 us -> 22.4 us  [on_device(): lax.all_to_all(partial.reshape(chips, tiles // 2 // chips, width), ('z',...]
    ppermute x2, starting transfers between devices: 3.23 us -> 4.23 us  [the longest x1 4.14 us: on_device(): from_next = lax.ppermute(for_next, ('z', 'core'), across)]
where the time goes in v8:
time: 74.1 us; the launch traced here: 73.8 us
  Pallas kernels  38 us (51%)
  blocking collectives  22.4 us (30%)
  starting transfers between devices  11.5 us (16%)
  other arithmetic  0.81 us (1%)
  between operations  0.78 us (1%)
    all_to_all x1, blocking collectives, on_device(): lax.all_to_all(partial.reshape(chips, tiles // 2 // chips, width), ('z',...  22.4 us
    pallas_call x1, Pallas kernels, on_device(): pl.pallas_call(local_kernel, grid=(steps,), in_specs=[pl.BlockSpec((speci...  17.1 us
    pallas_call x1, Pallas kernels, on_device(): pl.pallas_call(functools.partial(update_kernel, elements=elements), grid=...  11.2 us
    pallas_call x1, Pallas kernels, on_device(): pl.pallas_call(send_kernel, in_specs=[hbm] * 5, out_specs=[hbm] * 4, out_...  7.37 us
    all_to_all x1, starting transfers between devices, on_device(): lax.all_to_all(send, 'sub', split_axis=0, concat_axis=0, tiled=True)  7.15 us
    ppermute x1, starting transfers between devices, on_device(): from_next = lax.ppermute(for_next, ('z', 'core'), across)  4.14 us
    pallas_call x1, Pallas kernels, on_device(): pl.pallas_call(own_kernel, in_specs=[vmem] * 2, out_specs=vmem, out_shape...  2.32 us
  transfers between devices with their start and end apart: 4, of which 1 were waited for; matrix products, arithmetic and copies ran while one was open for 0% of the time, Pallas kernels for 26%

profile of v8, /device:TPU:0, one launch (start us, length us, event | category | flops | bytes accessed | tf_op | source)
XLA Modules:
  0.0 73.8 jit_solution(15282012244057171174)
XLA Ops:
  0.6 7.4 %sends.1 = (bf16[6,144,2048]{2,1,0:T(8,128)(2,1)}, bf16[16,2,144,128]{3,2,1,0:T(8,128)(2,1)}, bf16[144,256]{1,0:T(8,128)(2,1)}, bf16[144,256]{1,0:T(8,128)(2,1)}) custom-call(f32[4,256,2048]{2,1,0:T(8,128)} %adj_ref.1, bf16[2,4,48,40]{3,2,1,0:T(8,128)(2,1)} %constant.56.near_hbm, bf16[4,192,216]{2,1,0:T(8,128)(2,1)} %constant.61.far_hbm, s32[4,1024]{1,0:T(4,128)} %ss_hbm.1, ...), custom_call_target="tpu_custom_call" | custom-call | flops 12000000000 | bytes 14000000 | tf_op jit(solution)/shard_map/sends/pallas_call | solution.py:352
  8.0 7.2 %all-to-all-start = ((bf16[16,2,144,128]{3,2,1,0:T(8,128)(2,1)}), bf16[16,2,144,128]{3,2,1,0:T(8,128)(2,1)S(1)}, u32[]{:S(2)}, u32[]{:S(2)}) async-start(bf16[16,2,144,128]{3,2,1,0:T(8,128)(2,1)} %get-tuple-element.14), calls=%async_computation | async-start | bytes 2359296 | tf_op jit(solution)/shard_map/all_to_all | solution.py:369
  15.2 0.1 collective-permute-start
  15.3 4.1 %collective-permute-start.1 = (bf16[144,256]{1,0:T(8,128)(2,1)}, bf16[144,256]{1,0:T(8,128)(2,1)S(1)}, u32[]{:S(2)}, u32[]{:S(2)}) collective-permute-start(bf16[144,256]{1,0:T(8,128)(2,1)} %get-tuple-element.16), channel_id=1, source_target_pairs={{0,112},{16,32},{32,16},{48,64},{64,48},{80,96},{96,80},{112,0},{1... | collective-permute-start | bytes 221192 | tf_op jit(solution)/shard_map/ppermute | solution.py:372
  19.4 0.0 copy-start
  19.4 0.0 copy-start.1
  19.4 0.0 copy-start.2
  19.4 0.0 copy-start.3
  19.4 0.0 copy-start.4
  19.4 0.0 copy-start.5
  19.4 17.1 %local.1 = (f32[4,4,256,512]{3,2,1,0:T(8,128)}, f32[4,872,512]{2,1,0:T(8,128)}) custom-call(f32[4,256,2048]{2,1,0:T(8,128)} %adj_ref.1, bf16[3,256,2048]{2,1,0:T(8,128)(2,1)} %vel_ref.1, bf16[768,256]{1,0:T(8,128)(2,1)} %der_ref.1, s32[6,2048]{1,0:T(8,128)} %nbr_ref.3, bf16[6,144,2048]{2,1,0:T(8,128)(2,1)} %get-tuple-element.12.pool_hbm, s32[1,2048]{1,0:T(1,128)} %bitcast.9, ...), custom_call_target="tpu_custom_call" | custom-call | flops 16000000000 | bytes 32000000 | tf_op jit(solution)/shard_map/local/pallas_call | solution.py:374
  36.5 0.0 collective-permute-done.mate_ref
  36.5 0.0 collective-permute-done.1.near_ref
  36.6 0.0 all-to-all-done.recv_ref
  36.6 0.0 copy-done
  36.6 0.0 copy-done.1
  36.6 0.0 copy-done.2
  36.6 0.0 copy-done.3
  36.6 0.0 copy-done.4
  36.6 0.0 copy-done.5
  36.6 11.2 %update.1 = (f32[4,256,2048]{2,1,0:T(8,128)}, bf16[2048,256]{1,0:T(8,128)(2,1)S(1)}, f32[2048,128]{1,0:T(8,128)S(1)}, s32[1,2048]{1,0:T(1,128)S(1)}) custom-call(s32[6,2048]{1,0:T(8,128)S(1)} %copy-done.2, f32[4,872,512]{2,1,0:T(8,128)} %get-tuple-element.13.gap_hbm, bf16[16,2,144,128]{3,2,1,0:T(8,128)(2,1)S(1)} %all-to-all-done.recv_ref, ...), custom_call_target="tpu_custom_call" | custom-call | flops 8000000000 | bytes 28000000 | tf_op jit(solution)/shard_map/update/pallas_call | solution.py:404
  47.9 0.1 collective-permute-start.2
  48.0 2.3 %scatter_own.1 = f32[2048,128]{1,0:T(8,128)S(1)} custom-call(s32[1,2048]{1,0:T(1,128)S(1)} %get-tuple-element.19.row_ref, bf16[2048,256]{1,0:T(8,128)(2,1)S(1)} %get-tuple-element.20.contrib_ref), custom_call_target="tpu_custom_call" | custom-call | flops 2100000000 | bytes 2000000 | tf_op jit(solution)/shard_map/scatter_own/pallas_call | solution.py:437
  50.3 0.3 collective-permute-done.2
  50.6 0.1 add_convert_fusion
  50.7 22.4 %all_to_all.10 = bf16[64,32,128]{2,1,0:T(8,128)(2,1)S(1)} all-to-all(bf16[64,32,128]{2,1,0:T(8,128)(2,1)S(1)} %bitcast.7), channel_id=1, replica_groups=mesh['z'=4,'core'=2,'sub'=16] {'z','sub'}, dimensions={0} | all-to-all | bytes 1048576 | tf_op jit(solution)/shard_map/all_to_all | solution.py:448
  73.1 0.7 convert_reduce_fusion
Async XLA Ops:
  8.0 28.5 %all-to-all-start = ((bf16[16,2,144,128]{3,2,1,0:T(8,128)(2,1)}), bf16[16,2,144,128]{3,2,1,0:T(8,128)(2,1)S(1)}, u32[]{:S(2)}, u32[]{:S(2)}) async-start(bf16[16,2,144,128]{3,2,1,0:T(8,128)(2,1)} %get-tuple-element.14), calls=%async_computation | async-start | bytes 2359296 | tf_op jit(solution)/shard_map/all_to_all | solution.py:369
  15.2 21.4 %collective-permute-start = (bf16[144,256]{1,0:T(8,128)(2,1)}, bf16[144,256]{1,0:T(8,128)(2,1)S(1)}, u32[]{:S(2)}, u32[]{:S(2)}) collective-permute-start(bf16[144,256]{1,0:T(8,128)(2,1)} %get-tuple-element.15), channel_id=1, source_target_pairs={{0,16},{16,0},{1,17},{17,1},{2,18},{18,2},{3,19},{19,3},{4,20},{20... | collective-permute-start | bytes 221192 | tf_op jit(solution)/shard_map/ppermute | solution.py:371
  15.3 21.3 %collective-permute-start.1 = (bf16[144,256]{1,0:T(8,128)(2,1)}, bf16[144,256]{1,0:T(8,128)(2,1)S(1)}, u32[]{:S(2)}, u32[]{:S(2)}) collective-permute-start(bf16[144,256]{1,0:T(8,128)(2,1)} %get-tuple-element.16), channel_id=1, source_target_pairs={{0,112},{16,32},{32,16},{48,64},{64,48},{80,96},{96,80},{112,0},{1... | collective-permute-start | bytes 221192 | tf_op jit(solution)/shard_map/ppermute | solution.py:372
  19.4 17.2 %copy-start = (bf16[216,2048]{1,0:T(8,128)(2,1)S(1)}, bf16[216,2048]{1,0:T(8,128)(2,1)}, u32[]{:S(2)}) copy-start(bf16[216,2048]{1,0:T(8,128)(2,1)} %fs_ref.1) | copy-start | bytes 2654212
  19.4 17.2 %copy-start.1 = (bf16[256,216]{0,1:T(8,128)(2,1)S(1)}, bf16[256,216]{0,1:T(8,128)(2,1)}, u32[]{:S(2)}) copy-start(bf16[256,216]{0,1:T(8,128)(2,1)} %param.29) | copy-start | bytes 331780
  19.4 17.2 %copy-start.2 = (s32[6,2048]{1,0:T(8,128)S(1)}, s32[6,2048]{1,0:T(8,128)}, u32[]{:S(2)}) copy-start(s32[6,2048]{1,0:T(8,128)} %nbr_ref.3) | copy-start | bytes 147460
  19.4 17.2 %copy-start.3 = (bf16[256,32]{0,1:T(8,128)(2,1)S(1)}, bf16[256,32]{0,1:T(8,128)(2,1)}, u32[]{:S(2)}) copy-start(bf16[256,32]{0,1:T(8,128)(2,1)} %param.30) | copy-start | bytes 49156
  19.4 17.2 %copy-start.4 = (bf16[288,216]{1,0:T(8,128)(2,1)S(1)}, bf16[288,216]{1,0:T(8,128)(2,1)}, u32[]{:S(2)}) copy-start(bf16[288,216]{1,0:T(8,128)(2,1)} %constant.42.clone.speed_ref) | copy-start | bytes 373252
  19.4 17.2 %copy-start.5 = (bf16[216,216]{1,0:T(8,128)(2,1)S(1)}, bf16[216,216]{1,0:T(8,128)(2,1)}, u32[]{:S(2)}) copy-start(bf16[216,216]{1,0:T(8,128)(2,1)} %constant.43.clone.order_ref) | copy-start | bytes 279940
  47.9 2.7 %collective-permute-start.2 = (f32[2048,128]{1,0:T(8,128)S(1)}, f32[2048,128]{1,0:T(8,128)S(1)}, u32[]{:S(2)}, u32[]{:S(2)}) collective-permute-start(f32[2048,128]{1,0:T(8,128)S(1)} %get-tuple-element.21), channel_id=1, source_target_pairs={{0,16},{16,0},{1,17},{17,1},{2,18},{18,2},{3,19},{19,3},{4,20},{20... | collective-permute-start | bytes 3145736 | tf_op jit(solution)/shard_map/ppermute | solution.py:436
